TPU v7x, 1024 devices: a whole 4x8x16 slice. The times are simulated.
1024 devices in a mesh: cluster: 64 (over y, x, core), split: 16 (over z).
Axes of the slice: x: 4, y: 8, z: 16, core: 2. Of those that a mesh axis runs over, the one named last changes fastest.
Arguments:
- embeddings: bfloat16 [131072, 1024], P(('cluster', 'split'))
- assignment: int32 [131072], P(('cluster', 'split')), may hold values from 0 to 63, as said below
Outputs:
- nearest_cosine: float32 [64, 16, 256], P('cluster', 'split')
- centroid_distance: float32 [64, 16, 256], P('cluster', 'split')
Inputs may be any that keep to these rules, and one draw needn't show every extreme that they name: `assignment`: in each aligned block of 128 rows exactly 32 clusters appear, each on exactly 4 rows; every cluster appears in some block. `embeddings`: no row is all zero.
All inputs are finite; a program needn't handle non-finite values.
Results may differ from a plain program's by a relative error of at most 0.00045.
Values may be sent and summed in bfloat16 or wider, within the bound.
No kernel may reach another device: no remote copies, remote signals or barrier semaphores. Data moves between devices by JAX's collectives and lax.ppermute only.
A program may use at most 32 MiB of HBM per device.

v0:
```python
import jax
import jax.numpy as jnp
from jax import lax
from jax.sharding import PartitionSpec as P

epsilon = 1e-06


def normalize_rows(values):
    as_float = values.astype(jnp.float32)
    return (
        as_float * lax.rsqrt(jnp.sum(as_float * as_float, axis=1, keepdims=True) + epsilon)
    ).astype(jnp.bfloat16)


def scores_tile(own_block, own_first, far_block, far_alive):
    scores = lax.dot_general(
        own_block, far_block, (((1,), (1,)), ((), ())), preferred_element_type=jnp.float32
    )
    own_index = own_first + jnp.arange(own_block.shape[0], dtype=jnp.int32)
    far_index = jnp.arange(far_block.shape[0], dtype=jnp.int32)
    usable = (far_alive[None, :] > 0) & (far_index[None, :] != own_index[:, None])
    return jnp.where(usable, scores, -2.0)


def local(embeddings, assignment):
    owners = lax.axis_size("cluster")
    row_count = embeddings.shape[0]
    feature_width = embeddings.shape[1]
    per_owner = 2 * row_count // owners
    slot_count = owners * per_owner
    normed = normalize_rows(embeddings)
    onehot = (assignment[:, None] == jnp.arange(owners, dtype=jnp.int32)[None, :]).astype(
        jnp.float32
    )
    earlier = (jnp.arange(row_count)[None, :] < jnp.arange(row_count)[:, None]).astype(jnp.float32)
    before = jnp.dot(earlier, onehot, preferred_element_type=jnp.float32)
    rank_in_owner = jnp.sum(before * onehot, axis=1).astype(jnp.int32)
    target = assignment * per_owner + rank_in_owner
    placement_table = target[None, :] == jnp.arange(slot_count, dtype=jnp.int32)[:, None]
    outgoing = jnp.dot(
        placement_table.astype(jnp.bfloat16), normed, preferred_element_type=jnp.float32
    ).astype(jnp.bfloat16)
    filled = jnp.sum(placement_table.astype(jnp.float32), axis=1).astype(jnp.bfloat16)
    members, alive_mask = (
        lax.all_to_all(
            outgoing.reshape(owners, per_owner, feature_width),
            "cluster",
            split_axis=0,
            concat_axis=0,
            tiled=True,
        ),
        lax.all_to_all(
            filled.reshape(owners, per_owner), "cluster", split_axis=0, concat_axis=0, tiled=True
        ),
    )
    members = members.reshape(slot_count, feature_width)
    alive_mask = alive_mask.reshape(slot_count)
    alive_float = alive_mask.astype(jnp.float32)
    local_sum = jnp.dot(alive_mask[None, :], members, preferred_element_type=jnp.float32)[0]
    center = lax.psum(local_sum, "split")
    centre_cos = jnp.sum(members.astype(jnp.float32) * center[None, :], axis=1) * lax.rsqrt(
        jnp.sum(center * center) + epsilon
    )
    distance = jnp.where(alive_float > 0, 1.0 - centre_cos, 0.0)
    my_index = lax.axis_index("split")
    own_first = my_index * slot_count
    nearest = jnp.maximum(
        jnp.full((slot_count,), -2.0, jnp.float32),
        jnp.max(
            scores_tile(
                members,
                own_first,
                lax.all_gather(members, "split", axis=0, tiled=True),
                lax.all_gather(alive_mask, "split", axis=0, tiled=True),
            ),
            axis=1,
        ),
    )
    nearest = jnp.where(alive_float > 0, nearest, 0.0)
    return (nearest.reshape(1, 1, slot_count), distance.reshape(1, 1, slot_count))


def solution(mesh):
    in_specs = (P(("cluster", "split"), None), P(("cluster", "split")))
    out_specs = (P("cluster", "split", None), P("cluster", "split", None))
    return jax.shard_map(local, mesh=mesh, in_specs=in_specs, out_specs=out_specs, check_vma=False)
```

profile of v0, /device:TPU:1, one launch (start us, length us, event | category | flops | bytes accessed | tf_op | source)
XLA Modules:
  0.0 169.4 jit_solution(10248414316638128479)
XLA Ops:
  7.2 0.0 all-gather.3.cloned.1.call-start
  7.2 0.9 fusion.2
  8.1 0.7 convert_add_fusion
  8.8 1.1 fusion.3
  9.9 1.3 convolution_convert_fusion
  11.2 0.2 reshape.113
  11.4 35.2 %all_to_all.11 = bf16[64,4,1024]{2,1,0:T(4,128)(2,1)S(1)} all-to-all(bf16[64,4,1024]{2,1,0:T(4,128)(2,1)S(1)} %reshape.113), channel_id=1, replica_groups=mesh['cluster'=64,'split'=16] {'cluster'}, dimensions={0} | all-to-all | bytes 1048576 | tf_op jit(solution)/shard_map/all_to_all | solution.py:46
  46.6 1.0 reshape.114
  47.6 0.0 all-gather.3.cloned.1.call-update
  47.6 0.1 convert_reduce_fusion
  47.7 0.7 convert_element_type.60
  48.5 5.7 %all-to-all-start = ((bf16[64,1,4]{2,1,0:T(2,128)(2,1)}), bf16[64,1,4]{2,1,0:T(2,128)(2,1)S(1)}, u32[]{:S(2)}, u32[]{:S(2)}) async-start(bf16[64,1,4]{2,1,0:T(2,128)(2,1)} %convert_element_type.60), calls=%async_computation | async-start | bytes 65536 | tf_op jit(solution)/shard_map/all_to_all | solution.py:53
  54.2 9.4 %all-to-all-done = bf16[64,1,4]{2,1,0:T(2,128)(2,1)S(1)} async-done(((bf16[64,1,4]{2,1,0:T(2,128)(2,1)}), bf16[64,1,4]{2,1,0:T(2,128)(2,1)S(1)}, u32[]{:S(2)}, u32[]{:S(2)}) %all-to-all-start) | async-done | bytes 544 | tf_op jit(solution)/shard_map/all_to_all | solution.py:53
  63.6 0.1 reduce.2
  63.7 0.1 reshape.120
  63.8 0.1 reshape.115
  63.9 0.1 compare_reduce_fusion
  64.0 0.1 gt.26
  64.2 32.1 %all-gather = bf16[16,1,256]{2,1,0:T(2,128)(2,1)S(1)} all-gather(bf16[1,1,256]{2,1,0:T(2,128)(2,1)S(1)} %reshape.115), channel_id=1, replica_groups=mesh['cluster'=64,'split'=16] {'split'}, dimensions={0}, use_global_device_ids=true | all-gather | bytes 8704 | tf_op jit(solution)/shard_map/all_gather | solution.py:75
  96.3 0.1 compare_reduce_fusion.1
  96.4 1.2 fusion.9
  97.6 23.5 %psum.7 = f32[1024]{0:T(1024)S(1)} all-reduce(f32[1024]{0:T(1024)S(1)} %bitcast.6), channel_id=1, replica_groups=mesh['cluster'=64,'split'=16] {'split'}, use_global_device_ids=true, to_apply=%region_4.0 | all-reduce | flops 1024 | bytes 8192 | tf_op jit(solution)/shard_map/psum | solution.py:61
  121.1 0.6 multiply_reduce_fusion.1
  122.4 0.3 multiply_reduce_fusion
  122.8 0.1 sub.18
  122.9 32.7 %all-gather.3.cloned.1.call-done = bf16[4096,1024]{1,0:T(8,128)(2,1)} async-done(((bf16[256,1024]{1,0:T(8,128)(2,1)}), bf16[4096,1024]{1,0:T(8,128)(2,1)}) %all-gather.3.cloned.1.call-update) | async-done | bytes 8388624 | tf_op jit(solution)/shard_map/all_gather | solution.py:74
  155.6 6.4 %fusion.1 = f32[256]{0:T(256)S(1)} fusion(bf16[256,1024]{1,0:T(8,128)(2,1)} %reshape.114, bf16[4096,1024]{1,0:T(8,128)(2,1)} %all-gather.3.cloned.1.call-done, s32[256]{0:T(256)S(1)} %iota_add_fusion, pred[4096]{0:T(1024)(128)(4,1)S(1)} %reshape.118), kind=kOutput, calls=%fused_computation.3 | convolution fusion | flops 2151677696 | bytes 8919040 | tf_op jit(solution)/shard_map/dot_general | solution.py:17
  162.0 0.6 broadcast_select_fusion
  (5 shorter events, 0.0 us)
Async XLA Ops:
  7.2 148.4 %all-gather.3.cloned.1.call-start = ((), (), s32[]{:S(2)}) async-start(), calls=%async_computation.2 | async-start | bytes 8912896 | tf_op jit(solution)/shard_map/all_gather | solution.py:74
  48.5 15.1 %all-to-all-start = ((bf16[64,1,4]{2,1,0:T(2,128)(2,1)}), bf16[64,1,4]{2,1,0:T(2,128)(2,1)S(1)}, u32[]{:S(2)}, u32[]{:S(2)}) async-start(bf16[64,1,4]{2,1,0:T(2,128)(2,1)} %convert_element_type.60), calls=%async_computation | async-start | bytes 65536 | tf_op jit(solution)/shard_map/all_to_all | solution.py:53
Sparse Core Ops, SparseCore 0:
  47.7 107.7 all-gather.2
where the time goes:
time: 170 us; the launch traced here: 169 us
  blocking collectives  90.9 us (53%)
  waiting for transfers between devices  42.1 us (25%)
  between operations  14.8 us (9%)
  matrix products  9.83 us (6%)
  starting transfers between devices  5.76 us (3%)
  other arithmetic  3.69 us (2%)
  local copies, waits for them, and re-layouts  2.37 us (1%)
    all_to_all x1, blocking collectives, local(): lax.all_to_all(outgoing.reshape(owners, per_owner, feature_width), 'clust...  35.2 us
    all_gather x1, waiting for transfers between devices, local(): lax.all_gather(members, 'split', axis=0, tiled=True)  32.7 us
    all_gather x1, blocking collectives, local(): lax.all_gather(alive_mask, 'split', axis=0, tiled=True)  32.1 us
    psum x1, blocking collectives, local(): center = lax.psum(local_sum, 'split')  23.5 us
    all_to_all x1, waiting for transfers between devices, local(): lax.all_to_all(filled.reshape(owners, per_owner), 'cluster', split_axis=0...  9.37 us
    dot_general x1, matrix products, scores_tile(): lax.dot_general(own_block, far_block, (((1,), (1,)), ((), ())), preferred...  6.38 us
    all_to_all x1, starting transfers between devices, local(): lax.all_to_all(filled.reshape(owners, per_owner), 'cluster', split_axis=0...  5.72 us
  transfers between devices with their start and end apart: 2, of which 2 were waited for; matrix products, arithmetic and copies ran while one was open for 2% of the time, Pallas kernels for 0%

commit v1 on v0

v1 whole, which is shorter than its diff:
```python
import jax
import jax.numpy as jnp
from jax import lax
from jax.sharding import PartitionSpec as P

EPSILON = 1e-06
NEVER = -2.0
DEAD_MARK = 2.0
CHUNKS = 1


def normalize_rows(values):
    as_float = values.astype(jnp.float32)
    return (
        as_float * lax.rsqrt(jnp.sum(as_float * as_float, axis=1, keepdims=True) + EPSILON)
    ).astype(jnp.bfloat16)


def outgoing_rows(embeddings, assignment, owners, per_owner):
    row_count = embeddings.shape[0]
    slot_count = owners * per_owner
    normed = normalize_rows(embeddings)
    same = assignment[:, None] == assignment[None, :]
    earlier = jnp.arange(row_count)[None, :] < jnp.arange(row_count)[:, None]
    rank = jnp.sum((same & earlier).astype(jnp.int32), axis=1)
    target = assignment * per_owner + rank
    table = target[None, :] == jnp.arange(slot_count, dtype=jnp.int32)[:, None]
    rows = jnp.dot(table.astype(jnp.bfloat16), normed, preferred_element_type=jnp.float32)
    filled = jnp.any(table, axis=1)
    first = jnp.arange(embeddings.shape[1], dtype=jnp.int32)[None, :] == 0
    rows = jnp.where(first & ~filled[:, None], DEAD_MARK, rows)
    return rows.astype(jnp.bfloat16)


def alive_of(block):
    return block[:, 0] < jnp.bfloat16(1.5)


def dots(a, b):
    return lax.dot_general(a, b, (((1,), (1,)), ((), ())), preferred_element_type=jnp.float32)


def row_best(a, b, b_alive):
    return jnp.max(jnp.where(b_alive[None, :], dots(a, b), NEVER), axis=1)


def shift(value, by, n):
    return lax.ppermute(value, "split", [(i, (i + by) % n) for i in range(n)])


def local(embeddings, assignment):
    owners = lax.axis_size("cluster")
    n = lax.axis_size("split")
    width = embeddings.shape[1]
    per_owner = 2 * embeddings.shape[0] // owners
    slots = owners * per_owner
    send = outgoing_rows(embeddings, assignment, owners, per_owner)
    own = lax.all_to_all(
        send.reshape(owners, per_owner, width), "cluster", split_axis=0, concat_axis=0, tiled=True
    ).reshape(slots, width)

    size = slots // CHUNKS
    down = [[own[c * size : (c + 1) * size]] for c in range(CHUNKS)]
    up = [[own[c * size : (c + 1) * size]] for c in range(CHUNKS)]
    for step in range(4):
        for c in range(CHUNKS):
            down[c].append(shift(down[c][-1], 1, n))
            up[c].append(shift(up[c][-1], -1, n))
    block = {0: [own]}
    for d in range(1, 5):
        block[-d] = [down[c][d] for c in range(CHUNKS)]
        block[d] = [up[c][d] for c in range(CHUNKS)]
    alive = {d: [alive_of(x) for x in block[d]] for d in block}

    diagonal = jnp.arange(slots)[None, :] == jnp.arange(slots)[:, None]
    own_alive = alive[0][0]
    best = jnp.max(jnp.where(own_alive[None, :] & ~diagonal, dots(own, own), NEVER), axis=1)
    for d in (-1, 1, -2, 2, -3, 3, -4, 4):
        for x, live in zip(block[d], alive[d]):
            best = jnp.maximum(best, row_best(own, x, live))

    def pair_best(p, q):
        return jnp.concatenate(
            [
                jnp.max(jnp.stack([row_best(a, b, l) for b, l in zip(block[q], alive[q])]), axis=0)
                for a in block[p]
            ]
        )

    r = {}

    def add(p, value):
        r[p] = value if p not in r else jnp.maximum(r[p], value)

    for p, q in ((-3, 2), (-3, 3)):
        add(p, pair_best(p, q))
        add(q, pair_best(q, p))
    early = {p: shift(v, p, n) for p, v in r.items()}
    r = {}
    add(-3, pair_best(-3, 4))
    add(4, pair_best(4, -3))
    add(4, pair_best(4, -4))
    late = {p: shift(v, p, n) for p, v in r.items()}
    for v in list(early.values()) + list(late.values()):
        best = jnp.maximum(best, v)
    nearest = jnp.where(own_alive, best, 0.0)

    total = 0.0
    for d in (-2, -1, 0, 1):
        for x, live in zip(block[d], alive[d]):
            total = total + jnp.dot(
                live.astype(jnp.bfloat16)[None, :], x, preferred_element_type=jnp.float32
            )
    total = total + shift(total, 4, n)
    total = total + shift(total, 8, n)
    center = total[0]
    cosine = jnp.sum(own.astype(jnp.float32) * center[None, :], axis=1) * lax.rsqrt(
        jnp.sum(center * center) + EPSILON
    )
    distance = jnp.where(own_alive, 1.0 - cosine, 0.0)
    return nearest.reshape(1, 1, slots), distance.reshape(1, 1, slots)


def solution(mesh):
    in_specs = (P(("cluster", "split"), None), P(("cluster", "split")))
    out_specs = (P("cluster", "split", None), P("cluster", "split", None))
    return jax.shard_map(local, mesh=mesh, in_specs=in_specs, out_specs=out_specs, check_vma=False)
```

time: 170 us -> 150 us (0.88)
  the two profiles are of different devices: /device:TPU:1 before, /device:TPU:10 now
where the time goes in v1:
time: 150 us
  starting transfers between devices  64.1 us (43%)
  waiting for transfers between devices  38.3 us (26%)
  blocking collectives  33.1 us (22%)
  matrix products  6.78 us (5%)
  other arithmetic  4.62 us (3%)
  between operations  1.7 us (1%)
    ppermute x15, starting transfers between devices, shift(): return lax.ppermute(value, 'split', [(i, (i + by) % n) for i in range(n)])  64.1 us
    ppermute x15, waiting for transfers between devices, shift(): return lax.ppermute(value, 'split', [(i, (i + by) % n) for i in range(n)])  38.3 us
    all_to_all x1, blocking collectives, local(): lax.all_to_all(send.reshape(owners, per_owner, width), 'cluster', split_a...  33.1 us
    dot_general x16, matrix products, dots(): lax.dot_general(a, b, (((1,), (1,)), ((), ())), preferred_element_type=jn...  5.68 us
  transfers between devices with their start and end apart: 15, of which 6 were waited for; matrix products, arithmetic and copies ran while one was open for 6% of the time, Pallas kernels for 0%

profile of v1, /device:TPU:10, one launch (start us, length us, event | category | flops | bytes accessed | tf_op | source)
XLA Modules:
  0.0 149.7 jit_solution(2937907890807255378)
XLA Ops:
  0.7 1.1 fusion.14
  1.8 0.6 copy-done.1
  2.8 0.4 fusion
  3.2 0.2 reshape.164
  3.4 33.1 %all_to_all.5 = bf16[64,4,1024]{2,1,0:T(4,128)(2,1)S(1)} all-to-all(bf16[64,4,1024]{2,1,0:T(4,128)(2,1)S(1)} %reshape.164), channel_id=1, replica_groups=mesh['cluster'=64,'split'=16] {'cluster'}, dimensions={0} | all-to-all | bytes 1048576 | tf_op jit(solution)/shard_map/all_to_all | solution.py:58
  36.6 12.1 %collective-permute-start.1 = (bf16[256,1024]{1,0:T(8,128)(2,1)S(1)}, bf16[256,1024]{1,0:T(8,128)(2,1)S(1)}, u32[]{:S(2)}, u32[]{:S(2)}) collective-permute-start(bf16[256,1024]{1,0:T(8,128)(2,1)S(1)} %reshape.165), channel_id=1, source_target_pairs={{0,15},{1,0},{2,1},{3,2},{4,3},{5,4},{6,5},{7,6},{8,7},{9,8},{10,9... | collective-permute-start | bytes 1572872 | tf_op jit(solution)/shard_map/ppermute | solution.py:48
  48.8 1.9 %collective-permute-start = (bf16[256,1024]{1,0:T(8,128)(2,1)S(1)}, bf16[256,1024]{1,0:T(8,128)(2,1)S(1)}, u32[]{:S(2)}, u32[]{:S(2)}) collective-permute-start(bf16[256,1024]{1,0:T(8,128)(2,1)S(1)} %reshape.165), channel_id=1, source_target_pairs={{0,1},{1,2},{2,3},{3,4},{4,5},{5,6},{6,7},{7,8},{8,9},{9,10},{10,1... | collective-permute-start | bytes 1572872 | tf_op jit(solution)/shard_map/ppermute | solution.py:48
  50.8 0.4 fusion.1
  51.2 0.2 fusion.25
  51.4 9.2 %collective-permute-done.1 = bf16[256,1024]{1,0:T(8,128)(2,1)S(1)} collective-permute-done((bf16[256,1024]{1,0:T(8,128)(2,1)S(1)}, bf16[256,1024]{1,0:T(8,128)(2,1)S(1)}, u32[]{:S(2)}, u32[]{:S(2)}) %collective-permute-start.1) | collective-permute-done | bytes 524320 | tf_op jit(solution)/shard_map/ppermute | solution.py:48
  60.6 5.6 %collective-permute-start.3 = (bf16[256,1024]{1,0:T(8,128)(2,1)S(1)}, bf16[256,1024]{1,0:T(8,128)(2,1)S(1)}, u32[]{:S(2)}, u32[]{:S(2)}) collective-permute-start(bf16[256,1024]{1,0:T(8,128)(2,1)S(1)} %collective-permute-done.1), channel_id=1, source_target_pairs={{0,15},{1,0},{2,1},{3,2},{4,3},{5,4},{6,5},{7,6},{8,7},{9,8},{10,9... | collective-permute-start | bytes 1572872 | tf_op jit(solution)/shard_map/ppermute | solution.py:48
  66.4 1.9 %collective-permute-start.2 = (bf16[256,1024]{1,0:T(8,128)(2,1)S(1)}, bf16[256,1024]{1,0:T(8,128)(2,1)S(1)}, u32[]{:S(2)}, u32[]{:S(2)}) collective-permute-start(bf16[256,1024]{1,0:T(8,128)(2,1)S(1)} %collective-permute-done), channel_id=1, source_target_pairs={{0,1},{1,2},{2,3},{3,4},{4,5},{5,6},{6,7},{7,8},{8,9},{9,10},{10,1... | collective-permute-start | bytes 1572872 | tf_op jit(solution)/shard_map/ppermute | solution.py:48
  68.3 0.4 select_reduce_fusion.1
  68.7 0.4 select_reduce_fusion.2
  69.1 0.2 fusion.26
  69.4 13.3 %collective-permute-done.2 = bf16[256,1024]{1,0:T(8,128)(2,1)S(1)} collective-permute-done((bf16[256,1024]{1,0:T(8,128)(2,1)S(1)}, bf16[256,1024]{1,0:T(8,128)(2,1)S(1)}, u32[]{:S(2)}, u32[]{:S(2)}) %collective-permute-start.2) | collective-permute-done | bytes 524320 | tf_op jit(solution)/shard_map/ppermute | solution.py:48
  83.1 1.9 %collective-permute-start.13 = (f32[1,1024]{1,0:T(1,128)S(1)}, f32[1,1024]{1,0:T(1,128)S(1)}, u32[]{:S(2)}, u32[]{:S(2)}) collective-permute-start(f32[1,1024]{1,0:T(1,128)S(1)} %bitcast.53), channel_id=1, source_target_pairs={{0,4},{1,5},{2,6},{3,7},{4,8},{5,9},{6,10},{7,11},{8,12},{9,13},{1... | collective-permute-start | bytes 12296 | tf_op jit(solution)/shard_map/ppermute | solution.py:48
  85.1 1.9 %collective-permute-start.5 = (bf16[256,1024]{1,0:T(8,128)(2,1)S(1)}, bf16[256,1024]{1,0:T(8,128)(2,1)S(1)}, u32[]{:S(2)}, u32[]{:S(2)}) collective-permute-start(bf16[256,1024]{1,0:T(8,128)(2,1)S(1)} %collective-permute-done.3), channel_id=1, source_target_pairs={{0,15},{1,0},{2,1},{3,2},{4,3},{5,4},{6,5},{7,6},{8,7},{9,8},{10,9... | collective-permute-start | bytes 1572872 | tf_op jit(solution)/shard_map/ppermute | solution.py:48
  87.0 0.4 select_reduce_fusion
  87.4 3.9 %collective-permute-start.4 = (bf16[256,1024]{1,0:T(8,128)(2,1)S(1)}, bf16[256,1024]{1,0:T(8,128)(2,1)S(1)}, u32[]{:S(2)}, u32[]{:S(2)}) collective-permute-start(bf16[256,1024]{1,0:T(8,128)(2,1)S(1)} %collective-permute-done.2), channel_id=1, source_target_pairs={{0,1},{1,2},{2,3},{3,4},{4,5},{5,6},{6,7},{7,8},{8,9},{9,10},{10,1... | collective-permute-start | bytes 1572872 | tf_op jit(solution)/shard_map/ppermute | solution.py:48
  91.3 1.2 collective-permute-done.13
  92.6 7.8 %collective-permute-start.14 = (f32[1,1024]{1,0:T(1,128)S(1)}, f32[1,1024]{1,0:T(1,128)S(1)}, u32[]{:S(2)}, u32[]{:S(2)}) collective-permute-start(f32[1,1024]{1,0:T(1,128)S(1)} %add.44), channel_id=1, source_target_pairs={{0,8},{1,9},{2,10},{3,11},{4,12},{5,13},{6,14},{7,15},{8,0},{9,1},... | collective-permute-start | bytes 12296 | tf_op jit(solution)/shard_map/ppermute | solution.py:48
  100.4 0.4 fusion.2
  100.7 7.7 %collective-permute-done.14 = f32[1,1024]{1,0:T(1,128)S(1)} collective-permute-done((f32[1,1024]{1,0:T(1,128)S(1)}, f32[1,1024]{1,0:T(1,128)S(1)}, u32[]{:S(2)}, u32[]{:S(2)}) %collective-permute-start.14) | collective-permute-done | bytes 4128 | tf_op jit(solution)/shard_map/ppermute | solution.py:48
  108.4 0.3 multiply_reduce_fusion
  108.7 0.6 multiply_reduce_fusion.1
  110.1 0.6 reshape_select_fusion
  110.8 0.4 fusion.7
  111.2 0.4 fusion.8
  111.6 3.6 %collective-permute-start.8 = (f32[256]{0:T(256)S(1)}, f32[256]{0:T(256)S(1)}, u32[]{:S(2)}, u32[]{:S(2)}) collective-permute-start(f32[256]{0:T(256)S(1)} %max.53), channel_id=1, source_target_pairs={{0,13},{1,14},{2,15},{3,0},{4,1},{5,2},{6,3},{7,4},{8,5},{9,6},{10... | collective-permute-start | bytes 3080 | tf_op jit(solution)/shard_map/ppermute | solution.py:48
  115.1 3.9 %collective-permute-start.7 = (bf16[256,1024]{1,0:T(8,128)(2,1)S(1)}, bf16[256,1024]{1,0:T(8,128)(2,1)S(1)}, u32[]{:S(2)}, u32[]{:S(2)}) collective-permute-start(bf16[256,1024]{1,0:T(8,128)(2,1)S(1)} %collective-permute-done.5), channel_id=1, source_target_pairs={{0,15},{1,0},{2,1},{3,2},{4,3},{5,4},{6,5},{7,6},{8,7},{9,8},{10,9... | collective-permute-start | bytes 1572872 | tf_op jit(solution)/shard_map/ppermute | solution.py:48
  119.2 0.4 fusion.9
  119.6 1.9 %collective-permute-start.9 = (f32[256]{0:T(256)S(1)}, f32[256]{0:T(256)S(1)}, u32[]{:S(2)}, u32[]{:S(2)}) collective-permute-start(f32[256]{0:T(256)S(1)} %fusion.9), channel_id=1, source_target_pairs={{0,2},{1,3},{2,4},{3,5},{4,6},{5,7},{6,8},{7,9},{8,10},{9,11},{10,... | collective-permute-start | bytes 3080 | tf_op jit(solution)/shard_map/ppermute | solution.py:48
  121.5 0.4 fusion.10
  121.8 4.5 %collective-permute-start.10 = (f32[256]{0:T(256)S(1)}, f32[256]{0:T(256)S(1)}, u32[]{:S(2)}, u32[]{:S(2)}) collective-permute-start(f32[256]{0:T(256)S(1)} %fusion.10), channel_id=1, source_target_pairs={{0,3},{1,4},{2,5},{3,6},{4,7},{5,8},{6,9},{7,10},{8,11},{9,12},{10... | collective-permute-start | bytes 3080 | tf_op jit(solution)/shard_map/ppermute | solution.py:48
  126.3 2.7 %collective-permute-start.6 = (bf16[256,1024]{1,0:T(8,128)(2,1)S(1)}, bf16[256,1024]{1,0:T(8,128)(2,1)S(1)}, u32[]{:S(2)}, u32[]{:S(2)}) collective-permute-start(bf16[256,1024]{1,0:T(8,128)(2,1)S(1)} %collective-permute-done.4), channel_id=1, source_target_pairs={{0,1},{1,2},{2,3},{3,4},{4,5},{5,6},{6,7},{7,8},{8,9},{9,10},{10,1... | collective-permute-start | bytes 1572872 | tf_op jit(solution)/shard_map/ppermute | solution.py:48
  129.1 0.4 fusion.4
  129.4 0.4 fusion.3
  129.9 0.4 fusion.11
  130.3 4.3 %collective-permute-start.11 = (f32[256]{0:T(256)S(1)}, f32[256]{0:T(256)S(1)}, u32[]{:S(2)}, u32[]{:S(2)}) collective-permute-start(f32[256]{0:T(256)S(1)} %fusion.11), channel_id=1, source_target_pairs={{0,13},{1,14},{2,15},{3,0},{4,1},{5,2},{6,3},{7,4},{8,5},{9,6},{10... | collective-permute-start | bytes 3080 | tf_op jit(solution)/shard_map/ppermute | solution.py:48
  134.6 0.4 fusion.12
  134.9 4.4 %collective-permute-done.6 = bf16[256,1024]{1,0:T(8,128)(2,1)S(1)} collective-permute-done((bf16[256,1024]{1,0:T(8,128)(2,1)S(1)}, bf16[256,1024]{1,0:T(8,128)(2,1)S(1)}, u32[]{:S(2)}, u32[]{:S(2)}) %collective-permute-start.6) | collective-permute-done | bytes 524320 | tf_op jit(solution)/shard_map/ppermute | solution.py:48
  139.4 0.4 fusion.13
  139.8 6.1 %collective-permute-start.12 = (f32[256]{0:T(256)S(1)}, f32[256]{0:T(256)S(1)}, u32[]{:S(2)}, u32[]{:S(2)}) collective-permute-start(f32[256]{0:T(256)S(1)} %max.58), channel_id=1, source_target_pairs={{0,4},{1,5},{2,6},{3,7},{4,8},{5,9},{6,10},{7,11},{8,12},{9,13},{1... | collective-permute-start | bytes 3080 | tf_op jit(solution)/shard_map/ppermute | solution.py:48
  145.9 0.4 fusion.6
  146.2 0.4 fusion.5
  146.6 2.5 %collective-permute-done.12 = f32[256]{0:T(256)S(1)} collective-permute-done((f32[256]{0:T(256)S(1)}, f32[256]{0:T(256)S(1)}, u32[]{:S(2)}, u32[]{:S(2)}) %collective-permute-start.12) | collective-permute-done | bytes 1056 | tf_op jit(solution)/shard_map/ppermute | solution.py:48
  149.2 0.6 maximum_select_fusion
  (41 shorter events, 2.0 us)
Async XLA Ops:
  0.6 2.1 %copy-start = (bf16[128,1024]{1,0:T(8,128)(2,1)S(1)}, bf16[128,1024]{1,0:T(8,128)(2,1)}, u32[]{:S(2)}) copy-start(bf16[128,1024]{1,0:T(8,128)(2,1)} %param.2) | copy-start | bytes 786436
  1.8 0.7 copy-start.1
  36.6 23.9 %collective-permute-start.1 = (bf16[256,1024]{1,0:T(8,128)(2,1)S(1)}, bf16[256,1024]{1,0:T(8,128)(2,1)S(1)}, u32[]{:S(2)}, u32[]{:S(2)}) collective-permute-start(bf16[256,1024]{1,0:T(8,128)(2,1)S(1)} %reshape.165), channel_id=1, source_target_pairs={{0,15},{1,0},{2,1},{3,2},{4,3},{5,4},{6,5},{7,6},{8,7},{9,8},{10,9... | collective-permute-start | bytes 1572872 | tf_op jit(solution)/shard_map/ppermute | solution.py:48
  48.8 17.5 %collective-permute-start = (bf16[256,1024]{1,0:T(8,128)(2,1)S(1)}, bf16[256,1024]{1,0:T(8,128)(2,1)S(1)}, u32[]{:S(2)}, u32[]{:S(2)}) collective-permute-start(bf16[256,1024]{1,0:T(8,128)(2,1)S(1)} %reshape.165), channel_id=1, source_target_pairs={{0,1},{1,2},{2,3},{3,4},{4,5},{5,6},{6,7},{7,8},{8,9},{9,10},{10,1... | collective-permute-start | bytes 1572872 | tf_op jit(solution)/shard_map/ppermute | solution.py:48
  60.6 24.4 %collective-permute-start.3 = (bf16[256,1024]{1,0:T(8,128)(2,1)S(1)}, bf16[256,1024]{1,0:T(8,128)(2,1)S(1)}, u32[]{:S(2)}, u32[]{:S(2)}) collective-permute-start(bf16[256,1024]{1,0:T(8,128)(2,1)S(1)} %collective-permute-done.1), channel_id=1, source_target_pairs={{0,15},{1,0},{2,1},{3,2},{4,3},{5,4},{6,5},{7,6},{8,7},{9,8},{10,9... | collective-permute-start | bytes 1572872 | tf_op jit(solution)/shard_map/ppermute | solution.py:48
  66.4 16.3 %collective-permute-start.2 = (bf16[256,1024]{1,0:T(8,128)(2,1)S(1)}, bf16[256,1024]{1,0:T(8,128)(2,1)S(1)}, u32[]{:S(2)}, u32[]{:S(2)}) collective-permute-start(bf16[256,1024]{1,0:T(8,128)(2,1)S(1)} %collective-permute-done), channel_id=1, source_target_pairs={{0,1},{1,2},{2,3},{3,4},{4,5},{5,6},{6,7},{7,8},{8,9},{9,10},{10,1... | collective-permute-start | bytes 1572872 | tf_op jit(solution)/shard_map/ppermute | solution.py:48
  83.1 9.5 %collective-permute-start.13 = (f32[1,1024]{1,0:T(1,128)S(1)}, f32[1,1024]{1,0:T(1,128)S(1)}, u32[]{:S(2)}, u32[]{:S(2)}) collective-permute-start(f32[1,1024]{1,0:T(1,128)S(1)} %bitcast.53), channel_id=1, source_target_pairs={{0,4},{1,5},{2,6},{3,7},{4,8},{5,9},{6,10},{7,11},{8,12},{9,13},{1... | collective-permute-start | bytes 12296 | tf_op jit(solution)/shard_map/ppermute | solution.py:48
  85.1 25.6 %collective-permute-start.5 = (bf16[256,1024]{1,0:T(8,128)(2,1)S(1)}, bf16[256,1024]{1,0:T(8,128)(2,1)S(1)}, u32[]{:S(2)}, u32[]{:S(2)}) collective-permute-start(bf16[256,1024]{1,0:T(8,128)(2,1)S(1)} %collective-permute-done.3), channel_id=1, source_target_pairs={{0,15},{1,0},{2,1},{3,2},{4,3},{5,4},{6,5},{7,6},{8,7},{9,8},{10,9... | collective-permute-start | bytes 1572872 | tf_op jit(solution)/shard_map/ppermute | solution.py:48
  87.4 23.4 %collective-permute-start.4 = (bf16[256,1024]{1,0:T(8,128)(2,1)S(1)}, bf16[256,1024]{1,0:T(8,128)(2,1)S(1)}, u32[]{:S(2)}, u32[]{:S(2)}) collective-permute-start(bf16[256,1024]{1,0:T(8,128)(2,1)S(1)} %collective-permute-done.2), channel_id=1, source_target_pairs={{0,1},{1,2},{2,3},{3,4},{4,5},{5,6},{6,7},{7,8},{8,9},{9,10},{10,1... | collective-permute-start | bytes 1572872 | tf_op jit(solution)/shard_map/ppermute | solution.py:48
  92.6 15.8 %collective-permute-start.14 = (f32[1,1024]{1,0:T(1,128)S(1)}, f32[1,1024]{1,0:T(1,128)S(1)}, u32[]{:S(2)}, u32[]{:S(2)}) collective-permute-start(f32[1,1024]{1,0:T(1,128)S(1)} %add.44), channel_id=1, source_target_pairs={{0,8},{1,9},{2,10},{3,11},{4,12},{5,13},{6,14},{7,15},{8,0},{9,1},... | collective-permute-start | bytes 12296 | tf_op jit(solution)/shard_map/ppermute | solution.py:48
  111.6 35.0 %collective-permute-start.8 = (f32[256]{0:T(256)S(1)}, f32[256]{0:T(256)S(1)}, u32[]{:S(2)}, u32[]{:S(2)}) collective-permute-start(f32[256]{0:T(256)S(1)} %max.53), channel_id=1, source_target_pairs={{0,13},{1,14},{2,15},{3,0},{4,1},{5,2},{6,3},{7,4},{8,5},{9,6},{10... | collective-permute-start | bytes 3080 | tf_op jit(solution)/shard_map/ppermute | solution.py:48
  115.1 14.6 %collective-permute-start.7 = (bf16[256,1024]{1,0:T(8,128)(2,1)S(1)}, bf16[256,1024]{1,0:T(8,128)(2,1)S(1)}, u32[]{:S(2)}, u32[]{:S(2)}) collective-permute-start(bf16[256,1024]{1,0:T(8,128)(2,1)S(1)} %collective-permute-done.5), channel_id=1, source_target_pairs={{0,15},{1,0},{2,1},{3,2},{4,3},{5,4},{6,5},{7,6},{8,7},{9,8},{10,9... | collective-permute-start | bytes 1572872 | tf_op jit(solution)/shard_map/ppermute | solution.py:48
  119.6 27.0 %collective-permute-start.9 = (f32[256]{0:T(256)S(1)}, f32[256]{0:T(256)S(1)}, u32[]{:S(2)}, u32[]{:S(2)}) collective-permute-start(f32[256]{0:T(256)S(1)} %fusion.9), channel_id=1, source_target_pairs={{0,2},{1,3},{2,4},{3,5},{4,6},{5,7},{6,8},{7,9},{8,10},{9,11},{10,... | collective-permute-start | bytes 3080 | tf_op jit(solution)/shard_map/ppermute | solution.py:48
  121.8 24.8 %collective-permute-start.10 = (f32[256]{0:T(256)S(1)}, f32[256]{0:T(256)S(1)}, u32[]{:S(2)}, u32[]{:S(2)}) collective-permute-start(f32[256]{0:T(256)S(1)} %fusion.10), channel_id=1, source_target_pairs={{0,3},{1,4},{2,5},{3,6},{4,7},{5,8},{6,9},{7,10},{8,11},{9,12},{10... | collective-permute-start | bytes 3080 | tf_op jit(solution)/shard_map/ppermute | solution.py:48
  126.3 12.9 %collective-permute-start.6 = (bf16[256,1024]{1,0:T(8,128)(2,1)S(1)}, bf16[256,1024]{1,0:T(8,128)(2,1)S(1)}, u32[]{:S(2)}, u32[]{:S(2)}) collective-permute-start(bf16[256,1024]{1,0:T(8,128)(2,1)S(1)} %collective-permute-done.4), channel_id=1, source_target_pairs={{0,1},{1,2},{2,3},{3,4},{4,5},{5,6},{6,7},{7,8},{8,9},{9,10},{10,1... | collective-permute-start | bytes 1572872 | tf_op jit(solution)/shard_map/ppermute | solution.py:48
  130.3 16.4 %collective-permute-start.11 = (f32[256]{0:T(256)S(1)}, f32[256]{0:T(256)S(1)}, u32[]{:S(2)}, u32[]{:S(2)}) collective-permute-start(f32[256]{0:T(256)S(1)} %fusion.11), channel_id=1, source_target_pairs={{0,13},{1,14},{2,15},{3,0},{4,1},{5,2},{6,3},{7,4},{8,5},{9,6},{10... | collective-permute-start | bytes 3080 | tf_op jit(solution)/shard_map/ppermute | solution.py:48
  139.8 9.4 %collective-permute-start.12 = (f32[256]{0:T(256)S(1)}, f32[256]{0:T(256)S(1)}, u32[]{:S(2)}, u32[]{:S(2)}) collective-permute-start(f32[256]{0:T(256)S(1)} %max.58), channel_id=1, source_target_pairs={{0,4},{1,5},{2,6},{3,7},{4,8},{5,9},{6,10},{7,11},{8,12},{9,13},{1... | collective-permute-start | bytes 3080 | tf_op jit(solution)/shard_map/ppermute | solution.py:48

commit v2 on v1

v2 whole, which is shorter than its diff:
```python
import jax
import jax.numpy as jnp
from jax import lax
from jax.sharding import PartitionSpec as P

EPSILON = 1e-06
NEVER = -2.0
DEAD_MARK = 2.0
CHUNKS = 2


def normalize_rows(values):
    as_float = values.astype(jnp.float32)
    return (
        as_float * lax.rsqrt(jnp.sum(as_float * as_float, axis=1, keepdims=True) + EPSILON)
    ).astype(jnp.bfloat16)


def outgoing_rows(embeddings, assignment, owners, per_owner):
    row_count = embeddings.shape[0]
    slot_count = owners * per_owner
    normed = normalize_rows(embeddings)
    same = assignment[:, None] == assignment[None, :]
    earlier = jnp.arange(row_count)[None, :] < jnp.arange(row_count)[:, None]
    rank = jnp.sum((same & earlier).astype(jnp.int32), axis=1)
    target = assignment * per_owner + rank
    table = target[None, :] == jnp.arange(slot_count, dtype=jnp.int32)[:, None]
    rows = jnp.dot(table.astype(jnp.bfloat16), normed, preferred_element_type=jnp.float32)
    filled = jnp.any(table, axis=1)
    first = jnp.arange(embeddings.shape[1], dtype=jnp.int32)[None, :] == 0
    rows = jnp.where(first & ~filled[:, None], DEAD_MARK, rows)
    return rows.astype(jnp.bfloat16)


def dots(a, b):
    return sum(
        lax.dot_general(x, y, (((1,), (1,)), ((), ())), preferred_element_type=jnp.float32)
        for x, y in zip(a, b)
    )


def best_over(far, rows):
    alive = far[0][:, 0:1] < 1.5
    return jnp.max(jnp.where(alive, dots(far, rows), NEVER), axis=0)


def shift(value, by, n):
    return lax.ppermute(value, "split", [(i, (i + by) % n) for i in range(n)])


def local(embeddings, assignment):
    owners = lax.axis_size("cluster")
    n = lax.axis_size("split")
    width = embeddings.shape[1]
    per_owner = 2 * embeddings.shape[0] // owners
    slots = owners * per_owner
    send = outgoing_rows(embeddings, assignment, owners, per_owner)
    part = width // CHUNKS
    own = [
        lax.all_to_all(
            send[:, c * part : (c + 1) * part].reshape(owners, per_owner, part),
            "cluster",
            split_axis=0,
            concat_axis=0,
            tiled=True,
        ).reshape(slots, part)
        for c in range(CHUNKS)
    ]

    block = {0: own}
    for step in range(1, 5):
        block[-step] = [shift(x, 1, n) for x in block[1 - step]]
        block[step] = [shift(x, -1, n) for x in block[step - 1]]

    alive = own[0][:, 0] < 1.5
    index = jnp.arange(slots)
    usable = alive[:, None] & (index[None, :] != index[:, None])
    best = jnp.max(jnp.where(usable, dots(own, own), NEVER), axis=0)
    for d in (-1, 1, -2, 2, -3, 3, -4, 4):
        best = jnp.maximum(best, best_over(block[d], own))

    message = {
        -4: best_over(block[2], block[-4]),
        -3: jnp.maximum(best_over(block[2], block[-3]), best_over(block[4], block[-3])),
        2: jnp.maximum(best_over(block[-3], block[2]), best_over(block[-4], block[2])),
        4: jnp.maximum(best_over(block[-3], block[4]), best_over(block[-4], block[4])),
    }

    sums = []
    for c in range(CHUNKS):
        total = 0.0
        for d in range(-4, 4):
            weight = (block[d][0][:, 0:1] < 1.5).astype(jnp.bfloat16)
            total = total + lax.dot_general(
                weight, block[d][c], (((0,), (0,)), ((), ())), preferred_element_type=jnp.float32
            )
        sums.append(total[0])
    for d in (-4, 4):
        message[d] = jnp.concatenate([message[d]] + sums)
    arrived = {d: shift(v, d, n) for d, v in message.items()}
    for v in arrived.values():
        best = jnp.maximum(best, v[:slots])
    nearest = jnp.where(alive, best, 0.0)

    center = arrived[-4][slots:] + arrived[4][slots:]
    cosine = sum(
        jnp.sum(x.astype(jnp.float32) * center[None, c * part : (c + 1) * part], axis=1)
        for c, x in enumerate(own)
    ) * lax.rsqrt(jnp.sum(center * center) + EPSILON)
    distance = jnp.where(alive, 1.0 - cosine, 0.0)
    return nearest.reshape(1, 1, slots), distance.reshape(1, 1, slots)


def solution(mesh):
    in_specs = (P(("cluster", "split"), None), P(("cluster", "split")))
    out_specs = (P("cluster", "split", None), P("cluster", "split", None))
    return jax.shard_map(local, mesh=mesh, in_specs=in_specs, out_specs=out_specs, check_vma=False)
```

time: 150 us -> 145 us (0.967)
  the two profiles are of different devices: /device:TPU:10 before, /device:TPU:2 now
where the time goes in v2:
time: 145 us; the launch traced here: 144 us
  starting transfers between devices  106 us (73%)
  waiting for transfers between devices  17.4 us (12%)
  matrix products  11.4 us (8%)
  other arithmetic  4.65 us (3%)
  local copies, waits for them, and re-layouts  2.5 us (2%)
  between operations  1.96 us (1%)
    ppermute x20, starting transfers between devices, shift(): return lax.ppermute(value, 'split', [(i, (i + by) % n) for i in range(n)])  82.9 us
    all_to_all x2, starting transfers between devices, local(): lax.all_to_all(send[:, c * part:(c + 1) * part].reshape(owners, per_owner...  22.9 us
    all_to_all x2, waiting for transfers between devices, local(): lax.all_to_all(send[:, c * part:(c + 1) * part].reshape(owners, per_owner...  11.5 us
    dot_general x32, matrix products, dots(): lax.dot_general(x, y, (((1,), (1,)), ((), ())), preferred_element_type=jn...  8.72 us
    ppermute x20, waiting for transfers between devices, shift(): return lax.ppermute(value, 'split', [(i, (i + by) % n) for i in range(n)])  5.9 us
  transfers between devices with their start and end apart: 22, of which 3 were waited for; matrix products, arithmetic and copies ran while one was open for 10% of the time, Pallas kernels for 0%

profile of v2, /device:TPU:2, one launch (start us, length us, event | category | flops | bytes accessed | tf_op | source)
XLA Modules:
  0.0 143.7 jit_solution(16959380614893660323)
XLA Ops:
  0.7 1.1 fusion.25
  1.8 0.6 copy-done.1
  2.8 0.4 fusion
  3.2 0.8 reshape.147
  4.0 17.2 %all-to-all-start = ((bf16[64,4,512]{2,1,0:T(4,128)(2,1)}), bf16[64,4,512]{2,1,0:T(4,128)(2,1)S(1)}, u32[]{:S(2)}, u32[]{:S(2)}) async-start(bf16[64,4,512]{2,1,0:T(4,128)(2,1)} %reshape.147), calls=%async_computation | async-start | bytes 524288 | tf_op jit(solution)/shard_map/all_to_all | solution.py:60
  21.2 0.8 reshape.149
  22.0 11.5 %all-to-all-done = bf16[64,4,512]{2,1,0:T(4,128)(2,1)S(1)} async-done(((bf16[64,4,512]{2,1,0:T(4,128)(2,1)}), bf16[64,4,512]{2,1,0:T(4,128)(2,1)S(1)}, u32[]{:S(2)}, u32[]{:S(2)}) %all-to-all-start) | async-done | bytes 262176 | tf_op jit(solution)/shard_map/all_to_all | solution.py:60
  33.5 5.7 %all-to-all-start.1 = ((bf16[64,4,512]{2,1,0:T(4,128)(2,1)}), bf16[64,4,512]{2,1,0:T(4,128)(2,1)S(1)}, u32[]{:S(2)}, u32[]{:S(2)}) async-start(bf16[64,4,512]{2,1,0:T(4,128)(2,1)} %reshape.149), calls=%async_computation.1 | async-start | bytes 524288 | tf_op jit(solution)/shard_map/all_to_all | solution.py:60
  39.4 11.5 %collective-permute-start.2 = (bf16[256,512]{1,0:T(8,128)(2,1)S(1)}, bf16[256,512]{1,0:T(8,128)(2,1)S(1)}, u32[]{:S(2)}, u32[]{:S(2)}) collective-permute-start(bf16[256,512]{1,0:T(8,128)(2,1)S(1)} %reshape.148), channel_id=1, source_target_pairs={{0,15},{1,0},{2,1},{3,2},{4,3},{5,4},{6,5},{7,6},{8,7},{9,8},{10,9... | collective-permute-start | bytes 786440 | tf_op jit(solution)/shard_map/ppermute | solution.py:48
  50.9 1.9 %collective-permute-start = (bf16[256,512]{1,0:T(8,128)(2,1)S(1)}, bf16[256,512]{1,0:T(8,128)(2,1)S(1)}, u32[]{:S(2)}, u32[]{:S(2)}) collective-permute-start(bf16[256,512]{1,0:T(8,128)(2,1)S(1)} %reshape.148), channel_id=1, source_target_pairs={{0,1},{1,2},{2,3},{3,4},{4,5},{5,6},{6,7},{7,8},{8,9},{9,10},{10,1... | collective-permute-start | bytes 786440 | tf_op jit(solution)/shard_map/ppermute | solution.py:48
  53.5 9.7 %collective-permute-start.3 = (bf16[256,512]{1,0:T(8,128)(2,1)S(1)}, bf16[256,512]{1,0:T(8,128)(2,1)S(1)}, u32[]{:S(2)}, u32[]{:S(2)}) collective-permute-start(bf16[256,512]{1,0:T(8,128)(2,1)S(1)} %reshape.150), channel_id=1, source_target_pairs={{0,15},{1,0},{2,1},{3,2},{4,3},{5,4},{6,5},{7,6},{8,7},{9,8},{10,9... | collective-permute-start | bytes 786440 | tf_op jit(solution)/shard_map/ppermute | solution.py:48
  63.2 1.9 %collective-permute-start.1 = (bf16[256,512]{1,0:T(8,128)(2,1)S(1)}, bf16[256,512]{1,0:T(8,128)(2,1)S(1)}, u32[]{:S(2)}, u32[]{:S(2)}) collective-permute-start(bf16[256,512]{1,0:T(8,128)(2,1)S(1)} %reshape.150), channel_id=1, source_target_pairs={{0,1},{1,2},{2,3},{3,4},{4,5},{5,6},{6,7},{7,8},{8,9},{9,10},{10,1... | collective-permute-start | bytes 786440 | tf_op jit(solution)/shard_map/ppermute | solution.py:48
  65.1 0.3 fusion.13
  65.7 5.1 %collective-permute-start.6 = (bf16[256,512]{1,0:T(8,128)(2,1)S(1)}, bf16[256,512]{1,0:T(8,128)(2,1)S(1)}, u32[]{:S(2)}, u32[]{:S(2)}) collective-permute-start(bf16[256,512]{1,0:T(8,128)(2,1)S(1)} %collective-permute-done.2), channel_id=1, source_target_pairs={{0,15},{1,0},{2,1},{3,2},{4,3},{5,4},{6,5},{7,6},{8,7},{9,8},{10,9... | collective-permute-start | bytes 786440 | tf_op jit(solution)/shard_map/ppermute | solution.py:48
  70.8 1.9 %collective-permute-start.4 = (bf16[256,512]{1,0:T(8,128)(2,1)S(1)}, bf16[256,512]{1,0:T(8,128)(2,1)S(1)}, u32[]{:S(2)}, u32[]{:S(2)}) collective-permute-start(bf16[256,512]{1,0:T(8,128)(2,1)S(1)} %collective-permute-done), channel_id=1, source_target_pairs={{0,1},{1,2},{2,3},{3,4},{4,5},{5,6},{6,7},{7,8},{8,9},{9,10},{10,1... | collective-permute-start | bytes 786440 | tf_op jit(solution)/shard_map/ppermute | solution.py:48
  73.0 5.1 %collective-permute-start.7 = (bf16[256,512]{1,0:T(8,128)(2,1)S(1)}, bf16[256,512]{1,0:T(8,128)(2,1)S(1)}, u32[]{:S(2)}, u32[]{:S(2)}) collective-permute-start(bf16[256,512]{1,0:T(8,128)(2,1)S(1)} %collective-permute-done.3), channel_id=1, source_target_pairs={{0,15},{1,0},{2,1},{3,2},{4,3},{5,4},{6,5},{7,6},{8,7},{9,8},{10,9... | collective-permute-start | bytes 786440 | tf_op jit(solution)/shard_map/ppermute | solution.py:48
  79.0 1.9 %collective-permute-start.5 = (bf16[256,512]{1,0:T(8,128)(2,1)S(1)}, bf16[256,512]{1,0:T(8,128)(2,1)S(1)}, u32[]{:S(2)}, u32[]{:S(2)}) collective-permute-start(bf16[256,512]{1,0:T(8,128)(2,1)S(1)} %collective-permute-done.1), channel_id=1, source_target_pairs={{0,1},{1,2},{2,3},{3,4},{4,5},{5,6},{6,7},{7,8},{8,9},{9,10},{10,1... | collective-permute-start | bytes 786440 | tf_op jit(solution)/shard_map/ppermute | solution.py:48
  80.9 0.3 select_reduce_fusion.2
  81.8 5.1 %collective-permute-start.10 = (bf16[256,512]{1,0:T(8,128)(2,1)S(1)}, bf16[256,512]{1,0:T(8,128)(2,1)S(1)}, u32[]{:S(2)}, u32[]{:S(2)}) collective-permute-start(bf16[256,512]{1,0:T(8,128)(2,1)S(1)} %collective-permute-done.6), channel_id=1, source_target_pairs={{0,15},{1,0},{2,1},{3,2},{4,3},{5,4},{6,5},{7,6},{8,7},{9,8},{10,9... | collective-permute-start | bytes 786440 | tf_op jit(solution)/shard_map/ppermute | solution.py:48
  86.9 1.9 %collective-permute-start.8 = (bf16[256,512]{1,0:T(8,128)(2,1)S(1)}, bf16[256,512]{1,0:T(8,128)(2,1)S(1)}, u32[]{:S(2)}, u32[]{:S(2)}) collective-permute-start(bf16[256,512]{1,0:T(8,128)(2,1)S(1)} %collective-permute-done.4), channel_id=1, source_target_pairs={{0,1},{1,2},{2,3},{3,4},{4,5},{5,6},{6,7},{7,8},{8,9},{9,10},{10,1... | collective-permute-start | bytes 786440 | tf_op jit(solution)/shard_map/ppermute | solution.py:48
  89.1 5.1 %collective-permute-start.11 = (bf16[256,512]{1,0:T(8,128)(2,1)S(1)}, bf16[256,512]{1,0:T(8,128)(2,1)S(1)}, u32[]{:S(2)}, u32[]{:S(2)}) collective-permute-start(bf16[256,512]{1,0:T(8,128)(2,1)S(1)} %collective-permute-done.7), channel_id=1, source_target_pairs={{0,15},{1,0},{2,1},{3,2},{4,3},{5,4},{6,5},{7,6},{8,7},{9,8},{10,9... | collective-permute-start | bytes 786440 | tf_op jit(solution)/shard_map/ppermute | solution.py:48
  95.1 1.9 %collective-permute-start.9 = (bf16[256,512]{1,0:T(8,128)(2,1)S(1)}, bf16[256,512]{1,0:T(8,128)(2,1)S(1)}, u32[]{:S(2)}, u32[]{:S(2)}) collective-permute-start(bf16[256,512]{1,0:T(8,128)(2,1)S(1)} %collective-permute-done.5), channel_id=1, source_target_pairs={{0,1},{1,2},{2,3},{3,4},{4,5},{5,6},{6,7},{7,8},{8,9},{9,10},{10,1... | collective-permute-start | bytes 786440 | tf_op jit(solution)/shard_map/ppermute | solution.py:48
  97.0 0.3 fusion.14
  97.3 0.3 select_reduce_fusion.1
  97.9 5.1 %collective-permute-start.14 = (bf16[256,512]{1,0:T(8,128)(2,1)S(1)}, bf16[256,512]{1,0:T(8,128)(2,1)S(1)}, u32[]{:S(2)}, u32[]{:S(2)}) collective-permute-start(bf16[256,512]{1,0:T(8,128)(2,1)S(1)} %collective-permute-done.10), channel_id=1, source_target_pairs={{0,15},{1,0},{2,1},{3,2},{4,3},{5,4},{6,5},{7,6},{8,7},{9,8},{10,9... | collective-permute-start | bytes 786440 | tf_op jit(solution)/shard_map/ppermute | solution.py:48
  103.0 1.9 %collective-permute-start.12 = (bf16[256,512]{1,0:T(8,128)(2,1)S(1)}, bf16[256,512]{1,0:T(8,128)(2,1)S(1)}, u32[]{:S(2)}, u32[]{:S(2)}) collective-permute-start(bf16[256,512]{1,0:T(8,128)(2,1)S(1)} %collective-permute-done.8), channel_id=1, source_target_pairs={{0,1},{1,2},{2,3},{3,4},{4,5},{5,6},{6,7},{7,8},{8,9},{9,10},{10,1... | collective-permute-start | bytes 786440 | tf_op jit(solution)/shard_map/ppermute | solution.py:48
  105.2 5.1 %collective-permute-start.15 = (bf16[256,512]{1,0:T(8,128)(2,1)S(1)}, bf16[256,512]{1,0:T(8,128)(2,1)S(1)}, u32[]{:S(2)}, u32[]{:S(2)}) collective-permute-start(bf16[256,512]{1,0:T(8,128)(2,1)S(1)} %collective-permute-done.11), channel_id=1, source_target_pairs={{0,15},{1,0},{2,1},{3,2},{4,3},{5,4},{6,5},{7,6},{8,7},{9,8},{10,9... | collective-permute-start | bytes 786440 | tf_op jit(solution)/shard_map/ppermute | solution.py:48
  111.8 1.9 %collective-permute-start.13 = (bf16[256,512]{1,0:T(8,128)(2,1)S(1)}, bf16[256,512]{1,0:T(8,128)(2,1)S(1)}, u32[]{:S(2)}, u32[]{:S(2)}) collective-permute-start(bf16[256,512]{1,0:T(8,128)(2,1)S(1)} %collective-permute-done.9), channel_id=1, source_target_pairs={{0,1},{1,2},{2,3},{3,4},{4,5},{5,6},{6,7},{7,8},{8,9},{9,10},{10,1... | collective-permute-start | bytes 786440 | tf_op jit(solution)/shard_map/ppermute | solution.py:48
  113.7 0.3 select_reduce_fusion
  114.0 0.3 fusion.21
  114.3 0.3 fusion.19
  114.5 0.3 fusion.15
  115.4 0.3 fusion.20
  115.7 1.9 %collective-permute-start.17 = (f32[256]{0:T(256)S(1)}, f32[256]{0:T(256)S(1)}, u32[]{:S(2)}, u32[]{:S(2)}) collective-permute-start(f32[256]{0:T(256)S(1)} %max.54), channel_id=1, source_target_pairs={{0,13},{1,14},{2,15},{3,0},{4,1},{5,2},{6,3},{7,4},{8,5},{9,6},{10... | collective-permute-start | bytes 3080 | tf_op jit(solution)/shard_map/ppermute | solution.py:48
  117.6 3.6 %collective-permute-done.13 = bf16[256,512]{1,0:T(8,128)(2,1)S(1)} collective-permute-done((bf16[256,512]{1,0:T(8,128)(2,1)S(1)}, bf16[256,512]{1,0:T(8,128)(2,1)S(1)}, u32[]{:S(2)}, u32[]{:S(2)}) %collective-permute-start.13) | collective-permute-done | bytes 262176 | tf_op jit(solution)/shard_map/ppermute | solution.py:48
  121.8 3.9 %collective-permute-start.18 = (f32[256]{0:T(256)S(1)}, f32[256]{0:T(256)S(1)}, u32[]{:S(2)}, u32[]{:S(2)}) collective-permute-start(f32[256]{0:T(256)S(1)} %max.56), channel_id=1, source_target_pairs={{0,2},{1,3},{2,4},{3,5},{4,6},{5,7},{6,8},{7,9},{8,10},{9,11},{10,... | collective-permute-start | bytes 3080 | tf_op jit(solution)/shard_map/ppermute | solution.py:48
  126.2 0.3 fusion.23
  126.5 0.3 fusion.24
  127.4 0.3 fusion.18
  127.7 3.6 %collective-permute-start.16 = (f32[1280]{0:T(1024)S(1)}, f32[1280]{0:T(1024)S(1)}, u32[]{:S(2)}, u32[]{:S(2)}) collective-permute-start(f32[1280]{0:T(1024)S(1)} %get-tuple-element.8), channel_id=1, source_target_pairs={{0,12},{1,13},{2,14},{3,15},{4,0},{5,1},{6,2},{7,3},{8,4},{9,5},{1... | collective-permute-start | bytes 15368 | tf_op jit(solution)/shard_map/ppermute | solution.py:48
  131.3 6.1 %collective-permute-start.19 = (f32[1280]{0:T(1024)S(1)}, f32[1280]{0:T(1024)S(1)}, u32[]{:S(2)}, u32[]{:S(2)}) collective-permute-start(f32[1280]{0:T(1024)S(1)} %get-tuple-element.9), channel_id=1, source_target_pairs={{0,4},{1,5},{2,6},{3,7},{4,8},{5,9},{6,10},{7,11},{8,12},{9,13},{1... | collective-permute-start | bytes 15368 | tf_op jit(solution)/shard_map/ppermute | solution.py:48
  138.0 0.3 fusion.17
  138.2 0.3 fusion.16
  138.5 2.2 %collective-permute-done.19 = f32[1280]{0:T(1024)S(1)} collective-permute-done((f32[1280]{0:T(1024)S(1)}, f32[1280]{0:T(1024)S(1)}, u32[]{:S(2)}, u32[]{:S(2)}) %collective-permute-start.19) | collective-permute-done | bytes 5152 | tf_op jit(solution)/shard_map/ppermute | solution.py:48
  140.8 0.6 multiply_reduce_fusion.2
  142.1 0.3 multiply_reduce_fusion
  142.5 0.6 reshape_select_fusion
  143.1 0.6 fusion.33
  (91 shorter events, 8.9 us)
Async XLA Ops:
  0.6 2.1 %copy-start = (bf16[128,1024]{1,0:T(8,128)(2,1)S(1)}, bf16[128,1024]{1,0:T(8,128)(2,1)}, u32[]{:S(2)}) copy-start(bf16[128,1024]{1,0:T(8,128)(2,1)} %param.2) | copy-start | bytes 786436
  1.8 0.7 copy-start.1
  4.0 29.6 %all-to-all-start = ((bf16[64,4,512]{2,1,0:T(4,128)(2,1)}), bf16[64,4,512]{2,1,0:T(4,128)(2,1)S(1)}, u32[]{:S(2)}, u32[]{:S(2)}) async-start(bf16[64,4,512]{2,1,0:T(4,128)(2,1)} %reshape.147), calls=%async_computation | async-start | bytes 524288 | tf_op jit(solution)/shard_map/all_to_all | solution.py:60
  33.5 19.8 %all-to-all-start.1 = ((bf16[64,4,512]{2,1,0:T(4,128)(2,1)}), bf16[64,4,512]{2,1,0:T(4,128)(2,1)S(1)}, u32[]{:S(2)}, u32[]{:S(2)}) async-start(bf16[64,4,512]{2,1,0:T(4,128)(2,1)} %reshape.149), calls=%async_computation.1 | async-start | bytes 524288 | tf_op jit(solution)/shard_map/all_to_all | solution.py:60
  39.4 26.0 %collective-permute-start.2 = (bf16[256,512]{1,0:T(8,128)(2,1)S(1)}, bf16[256,512]{1,0:T(8,128)(2,1)S(1)}, u32[]{:S(2)}, u32[]{:S(2)}) collective-permute-start(bf16[256,512]{1,0:T(8,128)(2,1)S(1)} %reshape.148), channel_id=1, source_target_pairs={{0,15},{1,0},{2,1},{3,2},{4,3},{5,4},{6,5},{7,6},{8,7},{9,8},{10,9... | collective-permute-start | bytes 786440 | tf_op jit(solution)/shard_map/ppermute | solution.py:48
  50.9 14.6 %collective-permute-start = (bf16[256,512]{1,0:T(8,128)(2,1)S(1)}, bf16[256,512]{1,0:T(8,128)(2,1)S(1)}, u32[]{:S(2)}, u32[]{:S(2)}) collective-permute-start(bf16[256,512]{1,0:T(8,128)(2,1)S(1)} %reshape.148), channel_id=1, source_target_pairs={{0,1},{1,2},{2,3},{3,4},{4,5},{5,6},{6,7},{7,8},{8,9},{9,10},{10,1... | collective-permute-start | bytes 786440 | tf_op jit(solution)/shard_map/ppermute | solution.py:48
  53.5 19.4 %collective-permute-start.3 = (bf16[256,512]{1,0:T(8,128)(2,1)S(1)}, bf16[256,512]{1,0:T(8,128)(2,1)S(1)}, u32[]{:S(2)}, u32[]{:S(2)}) collective-permute-start(bf16[256,512]{1,0:T(8,128)(2,1)S(1)} %reshape.150), channel_id=1, source_target_pairs={{0,15},{1,0},{2,1},{3,2},{4,3},{5,4},{6,5},{7,6},{8,7},{9,8},{10,9... | collective-permute-start | bytes 786440 | tf_op jit(solution)/shard_map/ppermute | solution.py:48
  63.2 15.4 %collective-permute-start.1 = (bf16[256,512]{1,0:T(8,128)(2,1)S(1)}, bf16[256,512]{1,0:T(8,128)(2,1)S(1)}, u32[]{:S(2)}, u32[]{:S(2)}) collective-permute-start(bf16[256,512]{1,0:T(8,128)(2,1)S(1)} %reshape.150), channel_id=1, source_target_pairs={{0,1},{1,2},{2,3},{3,4},{4,5},{5,6},{6,7},{7,8},{8,9},{9,10},{10,1... | collective-permute-start | bytes 786440 | tf_op jit(solution)/shard_map/ppermute | solution.py:48
  65.7 15.8 %collective-permute-start.6 = (bf16[256,512]{1,0:T(8,128)(2,1)S(1)}, bf16[256,512]{1,0:T(8,128)(2,1)S(1)}, u32[]{:S(2)}, u32[]{:S(2)}) collective-permute-start(bf16[256,512]{1,0:T(8,128)(2,1)S(1)} %collective-permute-done.2), channel_id=1, source_target_pairs={{0,15},{1,0},{2,1},{3,2},{4,3},{5,4},{6,5},{7,6},{8,7},{9,8},{10,9... | collective-permute-start | bytes 786440 | tf_op jit(solution)/shard_map/ppermute | solution.py:48
  70.8 10.8 %collective-permute-start.4 = (bf16[256,512]{1,0:T(8,128)(2,1)S(1)}, bf16[256,512]{1,0:T(8,128)(2,1)S(1)}, u32[]{:S(2)}, u32[]{:S(2)}) collective-permute-start(bf16[256,512]{1,0:T(8,128)(2,1)S(1)} %collective-permute-done), channel_id=1, source_target_pairs={{0,1},{1,2},{2,3},{3,4},{4,5},{5,6},{6,7},{7,8},{8,9},{9,10},{10,1... | collective-permute-start | bytes 786440 | tf_op jit(solution)/shard_map/ppermute | solution.py:48
  73.0 16.0 %collective-permute-start.7 = (bf16[256,512]{1,0:T(8,128)(2,1)S(1)}, bf16[256,512]{1,0:T(8,128)(2,1)S(1)}, u32[]{:S(2)}, u32[]{:S(2)}) collective-permute-start(bf16[256,512]{1,0:T(8,128)(2,1)S(1)} %collective-permute-done.3), channel_id=1, source_target_pairs={{0,15},{1,0},{2,1},{3,2},{4,3},{5,4},{6,5},{7,6},{8,7},{9,8},{10,9... | collective-permute-start | bytes 786440 | tf_op jit(solution)/shard_map/ppermute | solution.py:48
  79.0 15.7 %collective-permute-start.5 = (bf16[256,512]{1,0:T(8,128)(2,1)S(1)}, bf16[256,512]{1,0:T(8,128)(2,1)S(1)}, u32[]{:S(2)}, u32[]{:S(2)}) collective-permute-start(bf16[256,512]{1,0:T(8,128)(2,1)S(1)} %collective-permute-done.1), channel_id=1, source_target_pairs={{0,1},{1,2},{2,3},{3,4},{4,5},{5,6},{6,7},{7,8},{8,9},{9,10},{10,1... | collective-permute-start | bytes 786440 | tf_op jit(solution)/shard_map/ppermute | solution.py:48
  81.8 15.8 %collective-permute-start.10 = (bf16[256,512]{1,0:T(8,128)(2,1)S(1)}, bf16[256,512]{1,0:T(8,128)(2,1)S(1)}, u32[]{:S(2)}, u32[]{:S(2)}) collective-permute-start(bf16[256,512]{1,0:T(8,128)(2,1)S(1)} %collective-permute-done.6), channel_id=1, source_target_pairs={{0,15},{1,0},{2,1},{3,2},{4,3},{5,4},{6,5},{7,6},{8,7},{9,8},{10,9... | collective-permute-start | bytes 786440 | tf_op jit(solution)/shard_map/ppermute | solution.py:48
  86.9 10.8 %collective-permute-start.8 = (bf16[256,512]{1,0:T(8,128)(2,1)S(1)}, bf16[256,512]{1,0:T(8,128)(2,1)S(1)}, u32[]{:S(2)}, u32[]{:S(2)}) collective-permute-start(bf16[256,512]{1,0:T(8,128)(2,1)S(1)} %collective-permute-done.4), channel_id=1, source_target_pairs={{0,1},{1,2},{2,3},{3,4},{4,5},{5,6},{6,7},{7,8},{8,9},{9,10},{10,1... | collective-permute-start | bytes 786440 | tf_op jit(solution)/shard_map/ppermute | solution.py:48
  89.1 16.0 %collective-permute-start.11 = (bf16[256,512]{1,0:T(8,128)(2,1)S(1)}, bf16[256,512]{1,0:T(8,128)(2,1)S(1)}, u32[]{:S(2)}, u32[]{:S(2)}) collective-permute-start(bf16[256,512]{1,0:T(8,128)(2,1)S(1)} %collective-permute-done.7), channel_id=1, source_target_pairs={{0,15},{1,0},{2,1},{3,2},{4,3},{5,4},{6,5},{7,6},{8,7},{9,8},{10,9... | collective-permute-start | bytes 786440 | tf_op jit(solution)/shard_map/ppermute | solution.py:48
  95.1 15.7 %collective-permute-start.9 = (bf16[256,512]{1,0:T(8,128)(2,1)S(1)}, bf16[256,512]{1,0:T(8,128)(2,1)S(1)}, u32[]{:S(2)}, u32[]{:S(2)}) collective-permute-start(bf16[256,512]{1,0:T(8,128)(2,1)S(1)} %collective-permute-done.5), channel_id=1, source_target_pairs={{0,1},{1,2},{2,3},{3,4},{4,5},{5,6},{6,7},{7,8},{8,9},{9,10},{10,1... | collective-permute-start | bytes 786440 | tf_op jit(solution)/shard_map/ppermute | solution.py:48
  97.9 17.4 %collective-permute-start.14 = (bf16[256,512]{1,0:T(8,128)(2,1)S(1)}, bf16[256,512]{1,0:T(8,128)(2,1)S(1)}, u32[]{:S(2)}, u32[]{:S(2)}) collective-permute-start(bf16[256,512]{1,0:T(8,128)(2,1)S(1)} %collective-permute-done.10), channel_id=1, source_target_pairs={{0,15},{1,0},{2,1},{3,2},{4,3},{5,4},{6,5},{7,6},{8,7},{9,8},{10,9... | collective-permute-start | bytes 786440 | tf_op jit(solution)/shard_map/ppermute | solution.py:48
  103.0 11.8 %collective-permute-start.12 = (bf16[256,512]{1,0:T(8,128)(2,1)S(1)}, bf16[256,512]{1,0:T(8,128)(2,1)S(1)}, u32[]{:S(2)}, u32[]{:S(2)}) collective-permute-start(bf16[256,512]{1,0:T(8,128)(2,1)S(1)} %collective-permute-done.8), channel_id=1, source_target_pairs={{0,1},{1,2},{2,3},{3,4},{4,5},{5,6},{6,7},{7,8},{8,9},{9,10},{10,1... | collective-permute-start | bytes 786440 | tf_op jit(solution)/shard_map/ppermute | solution.py:48
  105.2 9.7 %collective-permute-start.15 = (bf16[256,512]{1,0:T(8,128)(2,1)S(1)}, bf16[256,512]{1,0:T(8,128)(2,1)S(1)}, u32[]{:S(2)}, u32[]{:S(2)}) collective-permute-start(bf16[256,512]{1,0:T(8,128)(2,1)S(1)} %collective-permute-done.11), channel_id=1, source_target_pairs={{0,15},{1,0},{2,1},{3,2},{4,3},{5,4},{6,5},{7,6},{8,7},{9,8},{10,9... | collective-permute-start | bytes 786440 | tf_op jit(solution)/shard_map/ppermute | solution.py:48
  111.8 9.5 %collective-permute-start.13 = (bf16[256,512]{1,0:T(8,128)(2,1)S(1)}, bf16[256,512]{1,0:T(8,128)(2,1)S(1)}, u32[]{:S(2)}, u32[]{:S(2)}) collective-permute-start(bf16[256,512]{1,0:T(8,128)(2,1)S(1)} %collective-permute-done.9), channel_id=1, source_target_pairs={{0,1},{1,2},{2,3},{3,4},{4,5},{5,6},{6,7},{7,8},{8,9},{9,10},{10,1... | collective-permute-start | bytes 786440 | tf_op jit(solution)/shard_map/ppermute | solution.py:48
  115.7 27.4 %collective-permute-start.17 = (f32[256]{0:T(256)S(1)}, f32[256]{0:T(256)S(1)}, u32[]{:S(2)}, u32[]{:S(2)}) collective-permute-start(f32[256]{0:T(256)S(1)} %max.54), channel_id=1, source_target_pairs={{0,13},{1,14},{2,15},{3,0},{4,1},{5,2},{6,3},{7,4},{8,5},{9,6},{10... | collective-permute-start | bytes 3080 | tf_op jit(solution)/shard_map/ppermute | solution.py:48
  121.8 21.3 %collective-permute-start.18 = (f32[256]{0:T(256)S(1)}, f32[256]{0:T(256)S(1)}, u32[]{:S(2)}, u32[]{:S(2)}) collective-permute-start(f32[256]{0:T(256)S(1)} %max.56), channel_id=1, source_target_pairs={{0,2},{1,3},{2,4},{3,5},{4,6},{5,7},{6,8},{7,9},{8,10},{9,11},{10,... | collective-permute-start | bytes 3080 | tf_op jit(solution)/shard_map/ppermute | solution.py:48
  127.7 10.9 %collective-permute-start.16 = (f32[1280]{0:T(1024)S(1)}, f32[1280]{0:T(1024)S(1)}, u32[]{:S(2)}, u32[]{:S(2)}) collective-permute-start(f32[1280]{0:T(1024)S(1)} %get-tuple-element.8), channel_id=1, source_target_pairs={{0,12},{1,13},{2,14},{3,15},{4,0},{5,1},{6,2},{7,3},{8,4},{9,5},{1... | collective-permute-start | bytes 15368 | tf_op jit(solution)/shard_map/ppermute | solution.py:48
  131.3 9.5 %collective-permute-start.19 = (f32[1280]{0:T(1024)S(1)}, f32[1280]{0:T(1024)S(1)}, u32[]{:S(2)}, u32[]{:S(2)}) collective-permute-start(f32[1280]{0:T(1024)S(1)} %get-tuple-element.9), channel_id=1, source_target_pairs={{0,4},{1,5},{2,6},{3,7},{4,8},{5,9},{6,10},{7,11},{8,12},{9,13},{1... | collective-permute-start | bytes 15368 | tf_op jit(solution)/shard_map/ppermute | solution.py:48

commit v3 on v2

v3 whole, which is shorter than its diff:
```python
import jax
import jax.numpy as jnp
from jax import lax
from jax.sharding import PartitionSpec as P

EPSILON = 1e-06
NEVER = -2.0
DEAD_MARK = 2.0
REACH = (5, 3)


def normalize_rows(values):
    as_float = values.astype(jnp.float32)
    return (
        as_float * lax.rsqrt(jnp.sum(as_float * as_float, axis=1, keepdims=True) + EPSILON)
    ).astype(jnp.bfloat16)


def outgoing_rows(embeddings, assignment, owners, per_owner):
    row_count = embeddings.shape[0]
    slot_count = owners * per_owner
    normed = normalize_rows(embeddings)
    same = assignment[:, None] == assignment[None, :]
    earlier = jnp.arange(row_count)[None, :] < jnp.arange(row_count)[:, None]
    rank = jnp.sum((same & earlier).astype(jnp.int32), axis=1)
    target = assignment * per_owner + rank
    table = target[None, :] == jnp.arange(slot_count, dtype=jnp.int32)[:, None]
    rows = jnp.dot(table.astype(jnp.bfloat16), normed, preferred_element_type=jnp.float32)
    filled = jnp.any(table, axis=1)
    first = jnp.arange(embeddings.shape[1], dtype=jnp.int32)[None, :] == 0
    rows = jnp.where(first & ~filled[:, None], DEAD_MARK, rows)
    return rows.astype(jnp.bfloat16)


def dots(a, b):
    return lax.dot_general(a, b, (((1,), (1,)), ((), ())), preferred_element_type=jnp.float32)


def alive_column(block):
    return block[:, 0:1] < 1.5


def best_over(far, rows):
    return jnp.max(jnp.where(alive_column(far), dots(far, rows), NEVER), axis=0)


def member_sum(block):
    weight = alive_column(block).astype(jnp.bfloat16)
    return lax.dot_general(
        weight, block, (((0,), (0,)), ((), ())), preferred_element_type=jnp.float32
    )[0]


def along_ring(value, by, owners, n):
    pairs = [
        (c * n + s, c * n + (s + (by if c % 2 == 0 else -by)) % n)
        for c in range(owners)
        for s in range(n)
    ]
    return lax.ppermute(value, ("cluster", "split"), pairs)


def to_partner(value, owners):
    return lax.ppermute(value, "cluster", [(c, c ^ 1) for c in range(owners)])


def local(embeddings, assignment):
    owners = lax.axis_size("cluster")
    n = lax.axis_size("split")
    width = embeddings.shape[1]
    per_owner = 2 * embeddings.shape[0] // owners
    slots = owners * per_owner
    send = outgoing_rows(embeddings, assignment, owners, per_owner)
    own = lax.all_to_all(
        send.reshape(owners, per_owner, width), "cluster", split_axis=0, concat_axis=0, tiled=True
    ).reshape(slots, width)

    mine = [own]
    other = [to_partner(own, owners)]
    for step in range(max(REACH)):
        if step < REACH[0]:
            mine.append(along_ring(mine[-1], 1, owners, n))
        if step < REACH[1]:
            other.append(along_ring(other[-1], 1, owners, n))
    ahead = {q: to_partner(other[q], owners) for q in (2, 3)}

    alive = own[:, 0] < 1.5
    index = jnp.arange(slots)
    usable = alive[:, None] & (index[None, :] != index[:, None])
    best = jnp.max(jnp.where(usable, dots(own, own), NEVER), axis=0)
    for p in range(1, 6):
        best = jnp.maximum(best, best_over(mine[p], own))
    for_partner = best_over(other[1], other[0])
    for q in (2, 3):
        for_partner = jnp.maximum(for_partner, best_over(other[q], other[0]))
    best = jnp.maximum(best, to_partner(for_partner, owners))

    to_four = jnp.maximum(best_over(own, mine[4]), best_over(ahead[2], mine[4]))
    to_two = jnp.maximum(best_over(mine[4], ahead[2]), best_over(mine[5], ahead[2]))

    behind = sum(member_sum(x) for x in mine)
    two = member_sum(ahead[2])
    four, ahead[3] = lax.optimization_barrier((jnp.concatenate([to_four, two]), ahead[3]))
    to_five = jnp.maximum(
        jnp.maximum(best_over(own, mine[5]), best_over(ahead[2], mine[5])),
        best_over(ahead[3], mine[5]),
    )
    messages = {
        -4: four,
        -5: jnp.concatenate([to_five, behind + two + member_sum(ahead[3])]),
        2: jnp.concatenate([to_two, behind]),
    }
    center = member_sum(mine[1])
    for by, message in messages.items():
        arrived = along_ring(message, by, owners, n)
        best = jnp.maximum(best, arrived[:slots])
        center = center + arrived[slots:]
    nearest = jnp.where(alive, best, 0.0)
    cosine = jnp.sum(own.astype(jnp.float32) * center[None, :], axis=1) * lax.rsqrt(
        jnp.sum(center * center) + EPSILON
    )
    distance = jnp.where(alive, 1.0 - cosine, 0.0)
    return nearest.reshape(1, 1, slots), distance.reshape(1, 1, slots)


def solution(mesh):
    in_specs = (P(("cluster", "split"), None), P(("cluster", "split")))
    out_specs = (P("cluster", "split", None), P("cluster", "split", None))
    return jax.shard_map(local, mesh=mesh, in_specs=in_specs, out_specs=out_specs, check_vma=False)
```

time: 145 us -> 142 us (0.979)
  the two profiles are of different devices: /device:TPU:2 before, /device:TPU:1 now
where the time goes in v3:
time: 142 us; the launch traced here: 141 us
  starting transfers between devices  56.3 us (40%)
  blocking collectives  35.2 us (25%)
  waiting for transfers between devices  34.4 us (24%)
  matrix products  7.52 us (5%)
  other arithmetic  4.88 us (3%)
  between operations  1.72 us (1%)
    ppermute x11, starting transfers between devices, along_ring(): return lax.ppermute(value, ('cluster', 'split'), pairs)  40.4 us
    all_to_all x1, blocking collectives, local(): lax.all_to_all(send.reshape(owners, per_owner, width), 'cluster', split_a...  35.2 us
    ppermute x11, waiting for transfers between devices, along_ring(): return lax.ppermute(value, ('cluster', 'split'), pairs)  34.4 us
    ppermute x4, starting transfers between devices, to_partner(): return lax.ppermute(value, 'cluster', [(c, c ^ 1) for c in range(owners)])  15.9 us
    dot_general x16, matrix products, dots(): lax.dot_general(a, b, (((1,), (1,)), ((), ())), preferred_element_type=jn...  5.69 us
  transfers between devices with their start and end apart: 15, of which 8 were waited for; matrix products, arithmetic and copies ran while one was open for 7% of the time, Pallas kernels for 0%

profile of v3, /device:TPU:1, one launch (start us, length us, event | category | flops | bytes accessed | tf_op | source)
XLA Modules:
  0.0 141.2 jit_solution(3113785826834489700)
XLA Ops:
  0.7 1.1 fusion.11
  1.8 0.6 copy-done.1
  2.8 0.4 fusion
  3.2 0.2 reshape.98
  3.4 35.2 %all_to_all.5 = bf16[64,4,1024]{2,1,0:T(4,128)(2,1)S(1)} all-to-all(bf16[64,4,1024]{2,1,0:T(4,128)(2,1)S(1)} %reshape.98), channel_id=1, replica_groups=mesh['cluster'=64,'split'=16] {'cluster'}, dimensions={0} | all-to-all | bytes 1048576 | tf_op jit(solution)/shard_map/all_to_all | solution.py:74
  38.7 2.3 %collective-permute-start.5 = (bf16[256,1024]{1,0:T(8,128)(2,1)S(1)}, bf16[256,1024]{1,0:T(8,128)(2,1)S(1)}, u32[]{:S(2)}, u32[]{:S(2)}) collective-permute-start(bf16[256,1024]{1,0:T(8,128)(2,1)S(1)} %reshape.99), channel_id=1, source_target_pairs={{0,16},{16,0},{32,48},{48,32},{64,80},{80,64},{96,112},{112,96},{1... | collective-permute-start | bytes 1572872 | tf_op jit(solution)/shard_map/ppermute | solution.py:64
  41.0 11.9 %collective-permute-start = (bf16[256,1024]{1,0:T(8,128)(2,1)S(1)}, bf16[256,1024]{1,0:T(8,128)(2,1)S(1)}, u32[]{:S(2)}, u32[]{:S(2)}) collective-permute-start(bf16[256,1024]{1,0:T(8,128)(2,1)S(1)} %reshape.99), channel_id=1, source_target_pairs={{0,1},{1,2},{2,3},{3,4},{4,5},{5,6},{6,7},{7,8},{8,9},{9,10},{10,1... | collective-permute-start | bytes 1572872 | tf_op jit(solution)/shard_map/ppermute | solution.py:60
  53.0 0.4 fusion.1
  53.4 0.2 fusion.21
  53.6 5.4 %collective-permute-done = bf16[256,1024]{1,0:T(8,128)(2,1)S(1)} collective-permute-done((bf16[256,1024]{1,0:T(8,128)(2,1)S(1)}, bf16[256,1024]{1,0:T(8,128)(2,1)S(1)}, u32[]{:S(2)}, u32[]{:S(2)}) %collective-permute-start) | collective-permute-done | bytes 524320 | tf_op jit(solution)/shard_map/ppermute | solution.py:60
  59.0 5.0 %collective-permute-start.1 = (bf16[256,1024]{1,0:T(8,128)(2,1)S(1)}, bf16[256,1024]{1,0:T(8,128)(2,1)S(1)}, u32[]{:S(2)}, u32[]{:S(2)}) collective-permute-start(bf16[256,1024]{1,0:T(8,128)(2,1)S(1)} %collective-permute-done), channel_id=1, source_target_pairs={{0,1},{1,2},{2,3},{3,4},{4,5},{5,6},{6,7},{7,8},{8,9},{9,10},{10,1... | collective-permute-start | bytes 1572872 | tf_op jit(solution)/shard_map/ppermute | solution.py:60
  64.1 1.9 %collective-permute-start.6 = (bf16[256,1024]{1,0:T(8,128)(2,1)S(1)}, bf16[256,1024]{1,0:T(8,128)(2,1)S(1)}, u32[]{:S(2)}, u32[]{:S(2)}) collective-permute-start(bf16[256,1024]{1,0:T(8,128)(2,1)S(1)} %collective-permute-done.5), channel_id=1, source_target_pairs={{0,1},{1,2},{2,3},{3,4},{4,5},{5,6},{6,7},{7,8},{8,9},{9,10},{10,1... | collective-permute-start | bytes 1572872 | tf_op jit(solution)/shard_map/ppermute | solution.py:60
  66.1 0.4 select_reduce_fusion.5
  66.6 3.5 %collective-permute-done.1 = bf16[256,1024]{1,0:T(8,128)(2,1)S(1)} collective-permute-done((bf16[256,1024]{1,0:T(8,128)(2,1)S(1)}, bf16[256,1024]{1,0:T(8,128)(2,1)S(1)}, u32[]{:S(2)}, u32[]{:S(2)}) %collective-permute-start.1) | collective-permute-done | bytes 524320 | tf_op jit(solution)/shard_map/ppermute | solution.py:60
  70.2 5.0 %collective-permute-start.2 = (bf16[256,1024]{1,0:T(8,128)(2,1)S(1)}, bf16[256,1024]{1,0:T(8,128)(2,1)S(1)}, u32[]{:S(2)}, u32[]{:S(2)}) collective-permute-start(bf16[256,1024]{1,0:T(8,128)(2,1)S(1)} %collective-permute-done.1), channel_id=1, source_target_pairs={{0,1},{1,2},{2,3},{3,4},{4,5},{5,6},{6,7},{7,8},{8,9},{9,10},{10,1... | collective-permute-start | bytes 1572872 | tf_op jit(solution)/shard_map/ppermute | solution.py:60
  75.3 0.4 select_reduce_fusion.4
  75.7 5.0 %collective-permute-start.7 = (bf16[256,1024]{1,0:T(8,128)(2,1)S(1)}, bf16[256,1024]{1,0:T(8,128)(2,1)S(1)}, u32[]{:S(2)}, u32[]{:S(2)}) collective-permute-start(bf16[256,1024]{1,0:T(8,128)(2,1)S(1)} %collective-permute-done.6), channel_id=1, source_target_pairs={{0,1},{1,2},{2,3},{3,4},{4,5},{5,6},{6,7},{7,8},{8,9},{9,10},{10,1... | collective-permute-start | bytes 1572872 | tf_op jit(solution)/shard_map/ppermute | solution.py:60
  80.9 0.4 select_reduce_fusion.2
  81.5 5.4 %collective-permute-done.7 = bf16[256,1024]{1,0:T(8,128)(2,1)S(1)} collective-permute-done((bf16[256,1024]{1,0:T(8,128)(2,1)S(1)}, bf16[256,1024]{1,0:T(8,128)(2,1)S(1)}, u32[]{:S(2)}, u32[]{:S(2)}) %collective-permute-start.7) | collective-permute-done | bytes 524320 | tf_op jit(solution)/shard_map/ppermute | solution.py:60
  87.0 5.6 %collective-permute-start.10 = (bf16[256,1024]{1,0:T(8,128)(2,1)S(1)}, bf16[256,1024]{1,0:T(8,128)(2,1)S(1)}, u32[]{:S(2)}, u32[]{:S(2)}) collective-permute-start(bf16[256,1024]{1,0:T(8,128)(2,1)S(1)} %collective-permute-done.7), channel_id=1, source_target_pairs={{0,16},{16,0},{32,48},{48,32},{64,80},{80,64},{96,112},{112,96},{1... | collective-permute-start | bytes 1572872 | tf_op jit(solution)/shard_map/ppermute | solution.py:64
  92.6 1.9 %collective-permute-start.8 = (bf16[256,1024]{1,0:T(8,128)(2,1)S(1)}, bf16[256,1024]{1,0:T(8,128)(2,1)S(1)}, u32[]{:S(2)}, u32[]{:S(2)}) collective-permute-start(bf16[256,1024]{1,0:T(8,128)(2,1)S(1)} %collective-permute-done.7), channel_id=1, source_target_pairs={{0,1},{1,2},{2,3},{3,4},{4,5},{5,6},{6,7},{7,8},{8,9},{9,10},{10,1... | collective-permute-start | bytes 1572872 | tf_op jit(solution)/shard_map/ppermute | solution.py:60
  94.6 0.4 select_reduce_fusion.3
  94.9 1.9 %collective-permute-start.3 = (bf16[256,1024]{1,0:T(8,128)(2,1)S(1)}, bf16[256,1024]{1,0:T(8,128)(2,1)S(1)}, u32[]{:S(2)}, u32[]{:S(2)}) collective-permute-start(bf16[256,1024]{1,0:T(8,128)(2,1)S(1)} %collective-permute-done.2), channel_id=1, source_target_pairs={{0,1},{1,2},{2,3},{3,4},{4,5},{5,6},{6,7},{7,8},{8,9},{9,10},{10,1... | collective-permute-start | bytes 1572872 | tf_op jit(solution)/shard_map/ppermute | solution.py:60
  97.0 0.4 select_reduce_fusion.1
  97.6 5.2 %collective-permute-done.8 = bf16[256,1024]{1,0:T(8,128)(2,1)S(1)} collective-permute-done((bf16[256,1024]{1,0:T(8,128)(2,1)S(1)}, bf16[256,1024]{1,0:T(8,128)(2,1)S(1)}, u32[]{:S(2)}, u32[]{:S(2)}) %collective-permute-start.8) | collective-permute-done | bytes 524320 | tf_op jit(solution)/shard_map/ppermute | solution.py:60
  103.0 0.4 select_reduce_fusion
  103.4 4.0 %collective-permute-start.9 = (f32[256]{0:T(256)S(1)}, f32[256]{0:T(256)S(1)}, u32[]{:S(2)}, u32[]{:S(2)}) collective-permute-start(f32[256]{0:T(256)S(1)} %maximum_maximum_fusion.1), channel_id=1, source_target_pairs={{0,16},{16,0},{32,48},{48,32},{64,80},{80,64},{96,112},{112,96},{1... | collective-permute-start | bytes 3080 | tf_op jit(solution)/shard_map/ppermute | solution.py:64
  107.3 1.1 collective-permute-done.3
  108.6 0.4 fusion.5
  109.0 0.4 fusion.4
  109.3 4.0 %collective-permute-start.11 = (bf16[256,1024]{1,0:T(8,128)(2,1)S(1)}, bf16[256,1024]{1,0:T(8,128)(2,1)S(1)}, u32[]{:S(2)}, u32[]{:S(2)}) collective-permute-start(bf16[256,1024]{1,0:T(8,128)(2,1)S(1)} %collective-permute-done.8), channel_id=1, source_target_pairs={{0,16},{16,0},{32,48},{48,32},{64,80},{80,64},{96,112},{112,96},{1... | collective-permute-start | bytes 1572872 | tf_op jit(solution)/shard_map/ppermute | solution.py:64
  113.3 0.4 fusion.9
  113.7 1.9 %collective-permute-start.4 = (bf16[256,1024]{1,0:T(8,128)(2,1)S(1)}, bf16[256,1024]{1,0:T(8,128)(2,1)S(1)}, u32[]{:S(2)}, u32[]{:S(2)}) collective-permute-start(bf16[256,1024]{1,0:T(8,128)(2,1)S(1)} %collective-permute-done.3), channel_id=1, source_target_pairs={{0,1},{1,2},{2,3},{3,4},{4,5},{5,6},{6,7},{7,8},{8,9},{9,10},{10,1... | collective-permute-start | bytes 1572872 | tf_op jit(solution)/shard_map/ppermute | solution.py:60
  116.0 0.4 fusion.2
  116.5 1.9 %collective-permute-start.12 = (f32[1280]{0:T(1024)S(1)}, f32[1280]{0:T(1024)S(1)}, u32[]{:S(2)}, u32[]{:S(2)}) collective-permute-start(f32[1280]{0:T(1024)S(1)} %pad_maximum_fusion), channel_id=1, source_target_pairs={{0,12},{1,13},{2,14},{3,15},{4,0},{5,1},{6,2},{7,3},{8,4},{9,5},{1... | collective-permute-start | bytes 15368 | tf_op jit(solution)/shard_map/ppermute | solution.py:60
  118.6 5.5 %collective-permute-done.4 = bf16[256,1024]{1,0:T(8,128)(2,1)S(1)} collective-permute-done((bf16[256,1024]{1,0:T(8,128)(2,1)S(1)}, bf16[256,1024]{1,0:T(8,128)(2,1)S(1)}, u32[]{:S(2)}, u32[]{:S(2)}) %collective-permute-start.4) | collective-permute-done | bytes 524320 | tf_op jit(solution)/shard_map/ppermute | solution.py:60
  124.2 0.4 fusion.10
  124.8 1.9 %collective-permute-start.14 = (f32[1280]{0:T(1024)S(1)}, f32[1280]{0:T(1024)S(1)}, u32[]{:S(2)}, u32[]{:S(2)}) collective-permute-start(f32[1280]{0:T(1024)S(1)} %pad_maximum_fusion.2), channel_id=1, source_target_pairs={{0,2},{1,3},{2,4},{3,5},{4,6},{5,7},{6,8},{7,9},{8,10},{9,11},{10,... | collective-permute-start | bytes 15368 | tf_op jit(solution)/shard_map/ppermute | solution.py:60
  126.7 0.4 fusion.8
  127.1 0.4 fusion.7
  127.4 0.4 fusion.6
  127.8 2.0 %collective-permute-start.13 = (f32[1280]{0:T(1024)S(1)}, f32[1280]{0:T(1024)S(1)}, u32[]{:S(2)}, u32[]{:S(2)}) collective-permute-start(f32[1280]{0:T(1024)S(1)} %pad_maximum_fusion.1), channel_id=1, source_target_pairs={{0,11},{1,12},{2,13},{3,14},{4,15},{5,0},{6,1},{7,2},{8,3},{9,4},{... | collective-permute-start | bytes 15368 | tf_op jit(solution)/shard_map/ppermute | solution.py:60
  129.8 0.4 fusion.3
  130.2 8.1 %collective-permute-done.13 = f32[1280]{0:T(1024)S(1)} collective-permute-done((f32[1280]{0:T(1024)S(1)}, f32[1280]{0:T(1024)S(1)}, u32[]{:S(2)}, u32[]{:S(2)}) %collective-permute-start.13) | collective-permute-done | bytes 5152 | tf_op jit(solution)/shard_map/ppermute | solution.py:60
  138.2 0.6 multiply_reduce_fusion.1
  139.5 0.3 multiply_reduce_fusion
  140.0 0.6 reshape_select_fusion
  140.6 0.6 fusion.19
  (54 shorter events, 3.3 us)
Async XLA Ops:
  0.6 2.1 %copy-start = (bf16[128,1024]{1,0:T(8,128)(2,1)S(1)}, bf16[128,1024]{1,0:T(8,128)(2,1)}, u32[]{:S(2)}) copy-start(bf16[128,1024]{1,0:T(8,128)(2,1)} %param.2) | copy-start | bytes 786436
  1.8 0.7 copy-start.1
  38.7 25.4 %collective-permute-start.5 = (bf16[256,1024]{1,0:T(8,128)(2,1)S(1)}, bf16[256,1024]{1,0:T(8,128)(2,1)S(1)}, u32[]{:S(2)}, u32[]{:S(2)}) collective-permute-start(bf16[256,1024]{1,0:T(8,128)(2,1)S(1)} %reshape.99), channel_id=1, source_target_pairs={{0,16},{16,0},{32,48},{48,32},{64,80},{80,64},{96,112},{112,96},{1... | collective-permute-start | bytes 1572872 | tf_op jit(solution)/shard_map/ppermute | solution.py:64
  41.0 18.0 %collective-permute-start = (bf16[256,1024]{1,0:T(8,128)(2,1)S(1)}, bf16[256,1024]{1,0:T(8,128)(2,1)S(1)}, u32[]{:S(2)}, u32[]{:S(2)}) collective-permute-start(bf16[256,1024]{1,0:T(8,128)(2,1)S(1)} %reshape.99), channel_id=1, source_target_pairs={{0,1},{1,2},{2,3},{3,4},{4,5},{5,6},{6,7},{7,8},{8,9},{9,10},{10,1... | collective-permute-start | bytes 1572872 | tf_op jit(solution)/shard_map/ppermute | solution.py:60
  59.0 11.1 %collective-permute-start.1 = (bf16[256,1024]{1,0:T(8,128)(2,1)S(1)}, bf16[256,1024]{1,0:T(8,128)(2,1)S(1)}, u32[]{:S(2)}, u32[]{:S(2)}) collective-permute-start(bf16[256,1024]{1,0:T(8,128)(2,1)S(1)} %collective-permute-done), channel_id=1, source_target_pairs={{0,1},{1,2},{2,3},{3,4},{4,5},{5,6},{6,7},{7,8},{8,9},{9,10},{10,1... | collective-permute-start | bytes 1572872 | tf_op jit(solution)/shard_map/ppermute | solution.py:60
  64.1 11.6 %collective-permute-start.6 = (bf16[256,1024]{1,0:T(8,128)(2,1)S(1)}, bf16[256,1024]{1,0:T(8,128)(2,1)S(1)}, u32[]{:S(2)}, u32[]{:S(2)}) collective-permute-start(bf16[256,1024]{1,0:T(8,128)(2,1)S(1)} %collective-permute-done.5), channel_id=1, source_target_pairs={{0,1},{1,2},{2,3},{3,4},{4,5},{5,6},{6,7},{7,8},{8,9},{9,10},{10,1... | collective-permute-start | bytes 1572872 | tf_op jit(solution)/shard_map/ppermute | solution.py:60
  70.2 11.2 %collective-permute-start.2 = (bf16[256,1024]{1,0:T(8,128)(2,1)S(1)}, bf16[256,1024]{1,0:T(8,128)(2,1)S(1)}, u32[]{:S(2)}, u32[]{:S(2)}) collective-permute-start(bf16[256,1024]{1,0:T(8,128)(2,1)S(1)} %collective-permute-done.1), channel_id=1, source_target_pairs={{0,1},{1,2},{2,3},{3,4},{4,5},{5,6},{6,7},{7,8},{8,9},{9,10},{10,1... | collective-permute-start | bytes 1572872 | tf_op jit(solution)/shard_map/ppermute | solution.py:60
  75.7 11.3 %collective-permute-start.7 = (bf16[256,1024]{1,0:T(8,128)(2,1)S(1)}, bf16[256,1024]{1,0:T(8,128)(2,1)S(1)}, u32[]{:S(2)}, u32[]{:S(2)}) collective-permute-start(bf16[256,1024]{1,0:T(8,128)(2,1)S(1)} %collective-permute-done.6), channel_id=1, source_target_pairs={{0,1},{1,2},{2,3},{3,4},{4,5},{5,6},{6,7},{7,8},{8,9},{9,10},{10,1... | collective-permute-start | bytes 1572872 | tf_op jit(solution)/shard_map/ppermute | solution.py:60
  87.0 10.5 %collective-permute-start.10 = (bf16[256,1024]{1,0:T(8,128)(2,1)S(1)}, bf16[256,1024]{1,0:T(8,128)(2,1)S(1)}, u32[]{:S(2)}, u32[]{:S(2)}) collective-permute-start(bf16[256,1024]{1,0:T(8,128)(2,1)S(1)} %collective-permute-done.7), channel_id=1, source_target_pairs={{0,16},{16,0},{32,48},{48,32},{64,80},{80,64},{96,112},{112,96},{1... | collective-permute-start | bytes 1572872 | tf_op jit(solution)/shard_map/ppermute | solution.py:64
  92.6 10.2 %collective-permute-start.8 = (bf16[256,1024]{1,0:T(8,128)(2,1)S(1)}, bf16[256,1024]{1,0:T(8,128)(2,1)S(1)}, u32[]{:S(2)}, u32[]{:S(2)}) collective-permute-start(bf16[256,1024]{1,0:T(8,128)(2,1)S(1)} %collective-permute-done.7), channel_id=1, source_target_pairs={{0,1},{1,2},{2,3},{3,4},{4,5},{5,6},{6,7},{7,8},{8,9},{9,10},{10,1... | collective-permute-start | bytes 1572872 | tf_op jit(solution)/shard_map/ppermute | solution.py:60
  94.9 13.6 %collective-permute-start.3 = (bf16[256,1024]{1,0:T(8,128)(2,1)S(1)}, bf16[256,1024]{1,0:T(8,128)(2,1)S(1)}, u32[]{:S(2)}, u32[]{:S(2)}) collective-permute-start(bf16[256,1024]{1,0:T(8,128)(2,1)S(1)} %collective-permute-done.2), channel_id=1, source_target_pairs={{0,1},{1,2},{2,3},{3,4},{4,5},{5,6},{6,7},{7,8},{8,9},{9,10},{10,1... | collective-permute-start | bytes 1572872 | tf_op jit(solution)/shard_map/ppermute | solution.py:60
  103.4 37.2 %collective-permute-start.9 = (f32[256]{0:T(256)S(1)}, f32[256]{0:T(256)S(1)}, u32[]{:S(2)}, u32[]{:S(2)}) collective-permute-start(f32[256]{0:T(256)S(1)} %maximum_maximum_fusion.1), channel_id=1, source_target_pairs={{0,16},{16,0},{32,48},{48,32},{64,80},{80,64},{96,112},{112,96},{1... | collective-permute-start | bytes 3080 | tf_op jit(solution)/shard_map/ppermute | solution.py:64
  109.3 7.0 %collective-permute-start.11 = (bf16[256,1024]{1,0:T(8,128)(2,1)S(1)}, bf16[256,1024]{1,0:T(8,128)(2,1)S(1)}, u32[]{:S(2)}, u32[]{:S(2)}) collective-permute-start(bf16[256,1024]{1,0:T(8,128)(2,1)S(1)} %collective-permute-done.8), channel_id=1, source_target_pairs={{0,16},{16,0},{32,48},{48,32},{64,80},{80,64},{96,112},{112,96},{1... | collective-permute-start | bytes 1572872 | tf_op jit(solution)/shard_map/ppermute | solution.py:64
  113.7 10.4 %collective-permute-start.4 = (bf16[256,1024]{1,0:T(8,128)(2,1)S(1)}, bf16[256,1024]{1,0:T(8,128)(2,1)S(1)}, u32[]{:S(2)}, u32[]{:S(2)}) collective-permute-start(bf16[256,1024]{1,0:T(8,128)(2,1)S(1)} %collective-permute-done.3), channel_id=1, source_target_pairs={{0,1},{1,2},{2,3},{3,4},{4,5},{5,6},{6,7},{7,8},{8,9},{9,10},{10,1... | collective-permute-start | bytes 1572872 | tf_op jit(solution)/shard_map/ppermute | solution.py:60
  116.5 13.7 %collective-permute-start.12 = (f32[1280]{0:T(1024)S(1)}, f32[1280]{0:T(1024)S(1)}, u32[]{:S(2)}, u32[]{:S(2)}) collective-permute-start(f32[1280]{0:T(1024)S(1)} %pad_maximum_fusion), channel_id=1, source_target_pairs={{0,12},{1,13},{2,14},{3,15},{4,0},{5,1},{6,2},{7,3},{8,4},{9,5},{1... | collective-permute-start | bytes 15368 | tf_op jit(solution)/shard_map/ppermute | solution.py:60
  124.8 5.4 %collective-permute-start.14 = (f32[1280]{0:T(1024)S(1)}, f32[1280]{0:T(1024)S(1)}, u32[]{:S(2)}, u32[]{:S(2)}) collective-permute-start(f32[1280]{0:T(1024)S(1)} %pad_maximum_fusion.2), channel_id=1, source_target_pairs={{0,2},{1,3},{2,4},{3,5},{4,6},{5,7},{6,8},{7,9},{8,10},{9,11},{10,... | collective-permute-start | bytes 15368 | tf_op jit(solution)/shard_map/ppermute | solution.py:60
  127.8 10.4 %collective-permute-start.13 = (f32[1280]{0:T(1024)S(1)}, f32[1280]{0:T(1024)S(1)}, u32[]{:S(2)}, u32[]{:S(2)}) collective-permute-start(f32[1280]{0:T(1024)S(1)} %pad_maximum_fusion.1), channel_id=1, source_target_pairs={{0,11},{1,12},{2,13},{3,14},{4,15},{5,0},{6,1},{7,2},{8,3},{9,4},{... | collective-permute-start | bytes 15368 | tf_op jit(solution)/shard_map/ppermute | solution.py:60

commit v4 on v3

v4 whole, which is shorter than its diff:
```python
import itertools

import jax
import jax.numpy as jnp
import numpy as np
from jax import lax
from jax.sharding import Mesh
from jax.sharding import PartitionSpec as P

EPSILON = 1e-06
NEVER = -2.0
DEAD_MARK = 2.0


def normalize_rows(values):
    as_float = values.astype(jnp.float32)
    return (
        as_float * lax.rsqrt(jnp.sum(as_float * as_float, axis=1, keepdims=True) + EPSILON)
    ).astype(jnp.bfloat16)


def outgoing_rows(embeddings, assignment, owners, per_owner):
    row_count = embeddings.shape[0]
    slot_count = owners * per_owner
    normed = normalize_rows(embeddings)
    same = assignment[:, None] == assignment[None, :]
    earlier = jnp.arange(row_count)[None, :] < jnp.arange(row_count)[:, None]
    rank = jnp.sum((same & earlier).astype(jnp.int32), axis=1)
    target = assignment * per_owner + rank
    table = target[None, :] == jnp.arange(slot_count, dtype=jnp.int32)[:, None]
    rows = jnp.dot(table.astype(jnp.bfloat16), normed, preferred_element_type=jnp.float32)
    filled = jnp.any(table, axis=1)
    first = jnp.arange(embeddings.shape[1], dtype=jnp.int32)[None, :] == 0
    rows = jnp.where(first & ~filled[:, None], DEAD_MARK, rows)
    return rows.astype(jnp.bfloat16)


DEAD_BEST = -8.0
ROWS = 16
HOME = (2, 4, 2)
HELD = ((0, 0, 0), (0, 0, 1), (0, 1, 0), (0, 3, 0), (1, 1, 0), (1, 3, 1))


def plus(a, b):
    return tuple((x + y) % d for x, y, d in zip(a, b, HOME))


def number(place):
    return (place[0] * HOME[1] + place[1]) * HOME[2] + place[2]


PLACES = list(itertools.product(*[range(d) for d in HOME]))


def choose_tiles():
    options = {}
    for p, q in itertools.permutations(HELD, 2):
        gap = plus(q, tuple(-x for x in p))
        options.setdefault(gap, []).append((p, q))
    for count in range(1, len(HELD) + 1):
        for rows in itertools.combinations(HELD, count):
            if rows[0] != HELD[0]:
                continue
            picks = [[t for t in options[gap] if t[0] in rows] for gap in sorted(options)]
            if len(picks) == len(PLACES) - 1 and all(picks):
                return rows, [t[0] for t in picks]
    raise ValueError("no cover")


TARGETS, TILES = choose_tiles()


def dots(a, b):
    return lax.dot_general(a, b, (((1,), (1,)), ((), ())), preferred_element_type=jnp.float32)


def best_and_sum(far, rows, diagonal):
    alive = far[:, 0:1] < 1.5
    scores = dots(far, rows)
    total = jnp.sum(jnp.where(alive, scores, 0.0), axis=0)
    if diagonal:
        index = jnp.arange(far.shape[0])
        alive = alive & (index[None, :] != index[:, None])
    return jnp.max(jnp.where(alive, scores, NEVER), axis=0), total


def exact_dot(a, b):
    return jnp.dot(a, b, precision=lax.Precision.HIGHEST, preferred_element_type=jnp.float32)


def local(embeddings, assignment):
    home = ("yl", "x", "core")
    far_y = lax.axis_size("yh")
    n = lax.axis_size("z")
    owners = far_y * len(PLACES)
    width = embeddings.shape[1]
    per_owner = 2 * embeddings.shape[0] // owners
    slots = owners * per_owner
    send = outgoing_rows(embeddings, assignment, owners, per_owner)
    own = lax.all_to_all(
        send.reshape(owners, per_owner, width),
        ("yh", "z"),
        split_axis=0,
        concat_axis=0,
        tiled=True,
    ).reshape(slots, width)
    block = {HELD[0]: own}
    for d in HELD[1:]:
        pairs = [(number(plus(u, d)), number(u)) for u in PLACES]
        block[d] = lax.ppermute(own, home, pairs)

    best, total = {}, {}
    best[HELD[0]], total[HELD[0]] = best_and_sum(own, own, True)
    for p, q in TILES:
        b, t = best_and_sum(block[q], block[p], False)
        best[p] = jnp.maximum(best[p], b) if p in best else b
        total[p] = total[p] + t if p in total else t
    square = 0.0
    for p in TARGETS:
        square = square + jnp.sum(jnp.where(block[p][:, 0] < 1.5, total[p], 0.0))
    best[HELD[0]] = jnp.where(own[:, 0] < 1.5, best[HELD[0]], DEAD_BEST)
    count = len(TARGETS)
    values = jnp.stack(
        [best[p] for p in TARGETS]
        + [total[p] for p in TARGETS]
        + [jnp.full((slots,), square)] * (ROWS - 2 * count)
    )

    lane = np.arange(slots)
    lane_z = (lane // per_owner) % n
    lane_c = (lane // (per_owner * n)) * per_owner + lane % per_owner
    cells = far_y * per_owner
    group = 128 // cells
    spread = jnp.asarray((lane_c[:, None] == np.arange(128)[None, :] % cells), jnp.float32)
    of_z = jnp.asarray(np.arange(n)[:, None] == lane_z[None, :])
    keep = jnp.asarray(np.arange(group)[:, None] == np.arange(128)[None, :] // cells)
    chosen = jnp.where(of_z[:, None, :], values[None], 0.0).reshape(n * ROWS, slots)
    message = jnp.sum(
        jnp.where(keep[None], exact_dot(chosen, spread).reshape(-1, group, 128), 0.0), axis=1
    )
    places = len(PLACES)
    message = lax.ppermute(
        message, home + ("z",), [(u * n + z, z * n + u) for u in range(places) for z in range(n)]
    )
    arrived = lax.all_to_all(
        message.reshape(n, ROWS // group, 128), "z", split_axis=0, concat_axis=0, tiled=True
    ).reshape(-1, 1, 128)

    rows = jnp.where(keep[None], arrived, 0.0).reshape(places * ROWS, 128)
    wide = exact_dot(rows, spread.T).reshape(places, ROWS, slots)
    moved = np.full((places, ROWS), -1)
    for v in range(2 * count):
        for u in PLACES:
            moved[number(u), v] = number(plus(u, TARGETS[v % count]))
    moved = jnp.asarray(moved)[:, :, None]
    lane_u = jnp.asarray((lane // per_owner) % places)[None, None, :]
    result = jnp.sum(jnp.where((moved == lane_u) | (moved < 0), wide, 0.0), axis=0)
    alive = result[0] > NEVER - 1.0
    nearest = jnp.where(alive, jnp.max(result[:count], axis=0), 0.0)
    cosine = jnp.sum(result[count : 2 * count], axis=0) * lax.rsqrt(result[2 * count] + EPSILON)
    distance = jnp.where(alive, 1.0 - cosine, 0.0)
    return nearest.reshape(1, 1, slots), distance.reshape(1, 1, slots)


def solution(mesh):
    names = ("yh", "yl", "x", "core", "z")
    n = mesh.shape["split"]
    parts = Mesh(mesh.devices.reshape(-1, *HOME, n), names)
    in_specs = (P(names, None), P(names))
    out_specs = (P(names[:4], "z", None), P(names[:4], "z", None))
    return jax.shard_map(local, mesh=parts, in_specs=in_specs, out_specs=out_specs, check_vma=False)
```

time: 142 us -> 140 us (0.986); the launches traced: 141 us -> 137 us
  blocking collectives: 35.2 us -> 81.6 us
  starting transfers between devices: 56.3 us -> 22.6 us
  waiting for transfers between devices: 34.4 us -> 14.8 us
  between operations: 1.72 us -> 4.25 us
  local copies, waits for them, and re-layouts: 1.13 us -> 2.63 us
    all_to_all x1 -> x2, blocking collectives: 35.2 us -> 81.6 us  [the longest x1 54.8 us: local(): lax.all_to_all(send.reshape(owners, per_owner, width), ('yh', 'z'), split...]
    ppermute x15 -> x6, starting transfers between devices: 56.3 us -> 22.6 us  [the longest x5 18.9 us: local(): block[d] = lax.ppermute(own, home, pairs)]
    ppermute x15 -> x6, waiting for transfers between devices: 34.4 us -> 14.8 us  [the longest x5 13.3 us: local(): block[d] = lax.ppermute(own, home, pairs)]
    unnamed x4 -> x16, local copies, waits for them, and re-layouts: 0.65 us -> 2.18 us
  transfers between devices with their start and end apart: 15 -> 6, of which waited for: 8 -> 4; matrix products, arithmetic and copies ran while one was open for 7% -> 2% of each run, Pallas kernels for 0% -> 0%
where the time goes in v4:
time: 140 us; the launch traced here: 137 us
  blocking collectives  81.6 us (58%)
  starting transfers between devices  22.6 us (16%)
  waiting for transfers between devices  14.8 us (11%)
  matrix products  6.8 us (5%)
  other arithmetic  4.64 us (3%)
  between operations  4.25 us (3%)
  local copies, waits for them, and re-layouts  2.63 us (2%)
    all_to_all x1, blocking collectives, local(): lax.all_to_all(send.reshape(owners, per_owner, width), ('yh', 'z'), split...  54.8 us
    all_to_all x1, blocking collectives, local(): lax.all_to_all(message.reshape(n, ROWS // group, 128), 'z', split_axis=0,...  26.9 us
    ppermute x5, starting transfers between devices, local(): block[d] = lax.ppermute(own, home, pairs)  18.9 us
    ppermute x5, waiting for transfers between devices, local(): block[d] = lax.ppermute(own, home, pairs)  13.3 us
    dot_general x16, matrix products, dots(): lax.dot_general(a, b, (((1,), (1,)), ((), ())), preferred_element_type=jn...  5.66 us
    ppermute x1, starting transfers between devices, local(): lax.ppermute(message, home + ('z',), [(u * n + z, z * n + u) for u in ran...  3.64 us
  transfers between devices with their start and end apart: 6, of which 4 were waited for; matrix products, arithmetic and copies ran while one was open for 2% of the time, Pallas kernels for 0%

profile of v4, /device:TPU:1, one launch (start us, length us, event | category | flops | bytes accessed | tf_op | source)
XLA Modules:
  0.0 137.3 jit_solution(12898917989366901430)
XLA Ops:
  0.7 0.6 copy-done.4
  1.3 0.2 convert_reduce_fusion
  1.5 0.1 fusion.10
  1.6 1.1 fusion.3
  2.7 0.4 fusion
  3.1 0.2 reshape.342
  3.3 54.8 %all_to_all.10 = bf16[64,4,1024]{2,1,0:T(4,128)(2,1)S(1)} all-to-all(bf16[64,4,1024]{2,1,0:T(4,128)(2,1)S(1)} %reshape.342), channel_id=1, replica_groups=mesh['yh'=4,'yl'=2,'x'=4,'core'=2,'z'=16] {'yh','z'}, dimensions={0} | all-to-all | bytes 1048576 | tf_op jit(solution)/shard_map/all_to_all | solution.py:100
  58.1 0.1 reshape.343
  58.2 6.4 %collective-permute-start.4 = (bf16[256,1024]{1,0:T(8,128)(2,1)S(1)}, bf16[256,1024]{1,0:T(8,128)(2,1)S(1)}, u32[]{:S(2)}, u32[]{:S(2)}) collective-permute-start(bf16[256,1024]{1,0:T(8,128)(2,1)S(1)} %reshape.343), channel_id=1, source_target_pairs={{240,0},{224,16},{144,32},{128,48},{176,64},{160,80},{208,96},{192... | collective-permute-start | bytes 1572872 | tf_op jit(solution)/shard_map/ppermute | solution.py:110
  64.7 1.9 %collective-permute-start = (bf16[256,1024]{1,0:T(8,128)(2,1)S(1)}, bf16[256,1024]{1,0:T(8,128)(2,1)S(1)}, u32[]{:S(2)}, u32[]{:S(2)}) collective-permute-start(bf16[256,1024]{1,0:T(8,128)(2,1)S(1)} %reshape.343), channel_id=1, source_target_pairs={{16,0},{0,16},{48,32},{32,48},{80,64},{64,80},{112,96},{96,112},{1... | collective-permute-start | bytes 1572872 | tf_op jit(solution)/shard_map/ppermute | solution.py:110
  66.6 3.4 %collective-permute-start.1 = (bf16[256,1024]{1,0:T(8,128)(2,1)S(1)}, bf16[256,1024]{1,0:T(8,128)(2,1)S(1)}, u32[]{:S(2)}, u32[]{:S(2)}) collective-permute-start(bf16[256,1024]{1,0:T(8,128)(2,1)S(1)} %reshape.343), channel_id=1, source_target_pairs={{32,0},{48,16},{64,32},{80,48},{96,64},{112,80},{0,96},{16,112},{1... | collective-permute-start | bytes 1572872 | tf_op jit(solution)/shard_map/ppermute | solution.py:110
  70.0 1.9 %collective-permute-start.2 = (bf16[256,1024]{1,0:T(8,128)(2,1)S(1)}, bf16[256,1024]{1,0:T(8,128)(2,1)S(1)}, u32[]{:S(2)}, u32[]{:S(2)}) collective-permute-start(bf16[256,1024]{1,0:T(8,128)(2,1)S(1)} %reshape.343), channel_id=1, source_target_pairs={{96,0},{112,16},{0,32},{16,48},{32,64},{48,80},{64,96},{80,112},{2... | collective-permute-start | bytes 1572872 | tf_op jit(solution)/shard_map/ppermute | solution.py:110
  71.9 5.4 %collective-permute-start.3 = (bf16[256,1024]{1,0:T(8,128)(2,1)S(1)}, bf16[256,1024]{1,0:T(8,128)(2,1)S(1)}, u32[]{:S(2)}, u32[]{:S(2)}) collective-permute-start(bf16[256,1024]{1,0:T(8,128)(2,1)S(1)} %reshape.343), channel_id=1, source_target_pairs={{160,0},{176,16},{192,32},{208,48},{224,64},{240,80},{128,96},{144... | collective-permute-start | bytes 1572872 | tf_op jit(solution)/shard_map/ppermute | solution.py:110
  77.3 0.1 compare_reduce_fusion.5
  77.4 0.4 select_reduce_fusion.15
  77.7 0.3 collective-permute-done.4
  78.0 0.3 fusion.21
  78.4 0.1 compare_reduce_fusion
  78.5 9.0 %collective-permute-done.3 = bf16[256,1024]{1,0:T(8,128)(2,1)S(1)} collective-permute-done((bf16[256,1024]{1,0:T(8,128)(2,1)S(1)}, bf16[256,1024]{1,0:T(8,128)(2,1)S(1)}, u32[]{:S(2)}, u32[]{:S(2)}) %collective-permute-start.3) | collective-permute-done | bytes 524320 | tf_op jit(solution)/shard_map/ppermute | solution.py:110
  87.5 0.3 fusion.20
  87.8 0.1 compare_reduce_fusion.1
  88.0 0.3 fusion.24
  88.3 0.3 fusion.23
  88.7 4.0 %collective-permute-done.1 = bf16[256,1024]{1,0:T(8,128)(2,1)S(1)} collective-permute-done((bf16[256,1024]{1,0:T(8,128)(2,1)S(1)}, bf16[256,1024]{1,0:T(8,128)(2,1)S(1)}, u32[]{:S(2)}, u32[]{:S(2)}) %collective-permute-start.1) | collective-permute-done | bytes 524320 | tf_op jit(solution)/shard_map/ppermute | solution.py:110
  92.7 0.3 fusion.26
  93.1 0.1 compare_reduce_fusion.3
  93.2 0.3 fusion.25
  93.5 0.3 fusion.18
  93.9 0.3 fusion.27
  94.2 0.1 compare_reduce_fusion.2
  94.3 0.3 fusion.19
  94.7 0.3 fusion.22
  95.2 0.4 select_reduce_fusion.14
  95.5 0.4 select_reduce_fusion.9
  95.9 0.4 select_reduce_fusion.5
  96.2 0.4 select_reduce_fusion.1
  96.6 0.4 select_reduce_fusion
  97.1 0.7 select_reduce_fusion.34
  97.8 0.6 select_reduce_fusion.36
  100.4 0.6 select_reduce_fusion.33
  102.4 0.9 copy-done.1
  103.3 0.4 fusion.2
  103.7 3.6 %collective-permute-start.5 = (f32[32,128]{1,0:T(8,128)S(1)}, f32[32,128]{1,0:T(8,128)S(1)}, u32[]{:S(2)}, u32[]{:S(2)}) collective-permute-start(f32[32,128]{1,0:T(8,128)S(1)} %fusion.2), channel_id=1, source_target_pairs={{0,0},{1,16},{2,32},{3,48},{4,64},{5,80},{6,96},{7,112},{8,128},{9... | collective-permute-start | bytes 49160 | tf_op jit(solution)/shard_map/ppermute | solution.py:142
  107.3 1.4 %collective-permute-done.5 = f32[32,128]{1,0:T(8,128)S(1)} collective-permute-done((f32[32,128]{1,0:T(8,128)S(1)}, f32[32,128]{1,0:T(8,128)S(1)}, u32[]{:S(2)}, u32[]{:S(2)}) %collective-permute-start.5) | collective-permute-done | bytes 16416 | tf_op jit(solution)/shard_map/ppermute | solution.py:142
  108.7 26.9 %all_to_all.11 = f32[16,2,128]{2,1,0:T(2,128)S(1)} all-to-all(f32[16,2,128]{2,1,0:T(2,128)S(1)} %bitcast.64), channel_id=1, replica_groups=mesh['yh'=4,'yl'=2,'x'=4,'core'=2,'z'=16] {'z'}, dimensions={0} | all-to-all | bytes 32768 | tf_op jit(solution)/shard_map/all_to_all | solution.py:145
  135.6 0.7 copy-done.5
  136.3 0.4 fusion.1
  136.7 0.6 bitcast_select_fusion
  (30 shorter events, 0.4 us)
Async XLA Ops:
  0.6 0.7 copy-start.4
  0.6 2.1 %copy-start = (bf16[128,1024]{1,0:T(8,128)(2,1)S(1)}, bf16[128,1024]{1,0:T(8,128)(2,1)}, u32[]{:S(2)}) copy-start(bf16[128,1024]{1,0:T(8,128)(2,1)} %param.7) | copy-start | bytes 786436
  58.1 6.5 %copy-start.3 = (pred[16,256]{1,0:T(8,128)(4,1)S(1)}, pred[16,256]{1,0:T(8,128)(4,1)}, u32[]{:S(2)}) copy-start(pred[16,256]{1,0:T(8,128)(4,1)} %constant.14.clone) | copy-start | bytes 12292
  58.2 19.8 %collective-permute-start.4 = (bf16[256,1024]{1,0:T(8,128)(2,1)S(1)}, bf16[256,1024]{1,0:T(8,128)(2,1)S(1)}, u32[]{:S(2)}, u32[]{:S(2)}) collective-permute-start(bf16[256,1024]{1,0:T(8,128)(2,1)S(1)} %reshape.343), channel_id=1, source_target_pairs={{240,0},{224,16},{144,32},{128,48},{176,64},{160,80},{208,96},{192... | collective-permute-start | bytes 1572872 | tf_op jit(solution)/shard_map/ppermute | solution.py:110
  64.7 23.3 %collective-permute-start = (bf16[256,1024]{1,0:T(8,128)(2,1)S(1)}, bf16[256,1024]{1,0:T(8,128)(2,1)S(1)}, u32[]{:S(2)}, u32[]{:S(2)}) collective-permute-start(bf16[256,1024]{1,0:T(8,128)(2,1)S(1)} %reshape.343), channel_id=1, source_target_pairs={{16,0},{0,16},{48,32},{32,48},{80,64},{64,80},{112,96},{96,112},{1... | collective-permute-start | bytes 1572872 | tf_op jit(solution)/shard_map/ppermute | solution.py:110
  66.6 26.1 %collective-permute-start.1 = (bf16[256,1024]{1,0:T(8,128)(2,1)S(1)}, bf16[256,1024]{1,0:T(8,128)(2,1)S(1)}, u32[]{:S(2)}, u32[]{:S(2)}) collective-permute-start(bf16[256,1024]{1,0:T(8,128)(2,1)S(1)} %reshape.343), channel_id=1, source_target_pairs={{32,0},{48,16},{64,32},{80,48},{96,64},{112,80},{0,96},{16,112},{1... | collective-permute-start | bytes 1572872 | tf_op jit(solution)/shard_map/ppermute | solution.py:110
  70.0 23.9 %collective-permute-start.2 = (bf16[256,1024]{1,0:T(8,128)(2,1)S(1)}, bf16[256,1024]{1,0:T(8,128)(2,1)S(1)}, u32[]{:S(2)}, u32[]{:S(2)}) collective-permute-start(bf16[256,1024]{1,0:T(8,128)(2,1)S(1)} %reshape.343), channel_id=1, source_target_pairs={{96,0},{112,16},{0,32},{16,48},{32,64},{48,80},{64,96},{80,112},{2... | collective-permute-start | bytes 1572872 | tf_op jit(solution)/shard_map/ppermute | solution.py:110
  71.9 15.6 %collective-permute-start.3 = (bf16[256,1024]{1,0:T(8,128)(2,1)S(1)}, bf16[256,1024]{1,0:T(8,128)(2,1)S(1)}, u32[]{:S(2)}, u32[]{:S(2)}) collective-permute-start(bf16[256,1024]{1,0:T(8,128)(2,1)S(1)} %reshape.343), channel_id=1, source_target_pairs={{160,0},{176,16},{192,32},{208,48},{224,64},{240,80},{128,96},{144... | collective-permute-start | bytes 1572872 | tf_op jit(solution)/shard_map/ppermute | solution.py:110
  102.4 0.9 copy-start.1
  102.4 0.9 copy-start.2
  103.7 5.1 %collective-permute-start.5 = (f32[32,128]{1,0:T(8,128)S(1)}, f32[32,128]{1,0:T(8,128)S(1)}, u32[]{:S(2)}, u32[]{:S(2)}) collective-permute-start(f32[32,128]{1,0:T(8,128)S(1)} %fusion.2), channel_id=1, source_target_pairs={{0,0},{1,16},{2,32},{3,48},{4,64},{5,80},{6,96},{7,112},{8,128},{9... | collective-permute-start | bytes 49160 | tf_op jit(solution)/shard_map/ppermute | solution.py:142
  135.6 0.7 copy-start.5
  135.6 0.7 copy-start.6
  135.6 0.7 copy-start.7

commit v5 on v4

v5 whole, which is shorter than its diff:
```python
import itertools

import jax
import jax.numpy as jnp
import numpy as np
from jax import lax
from jax.experimental import pallas as pl
from jax.experimental.pallas import tpu as pltpu
from jax.sharding import Mesh
from jax.sharding import PartitionSpec as P

EPSILON = 1e-06
NEVER = -2.0
DEAD_MARK = 2.0


def normalize_rows(values):
    as_float = values.astype(jnp.float32)
    return (
        as_float * lax.rsqrt(jnp.sum(as_float * as_float, axis=1, keepdims=True) + EPSILON)
    ).astype(jnp.bfloat16)


def outgoing_rows(embeddings, assignment, owners, per_owner):
    row_count = embeddings.shape[0]
    slot_count = owners * per_owner
    normed = normalize_rows(embeddings)
    same = assignment[:, None] == assignment[None, :]
    earlier = jnp.arange(row_count)[None, :] < jnp.arange(row_count)[:, None]
    rank = jnp.sum((same & earlier).astype(jnp.int32), axis=1)
    target = assignment * per_owner + rank
    table = target[None, :] == jnp.arange(slot_count, dtype=jnp.int32)[:, None]
    rows = jnp.dot(table.astype(jnp.bfloat16), normed, preferred_element_type=jnp.float32)
    filled = jnp.any(table, axis=1)
    first = jnp.arange(embeddings.shape[1], dtype=jnp.int32)[None, :] == 0
    rows = jnp.where(first & ~filled[:, None], DEAD_MARK, rows)
    return rows.astype(jnp.bfloat16)


DEAD_BEST = -8.0
ROWS = 16
HOME = (2, 4, 2)
OWN, C, Y, YC = (0, 0, 0), (0, 0, 1), (1, 0, 0), (1, 0, 1)
X1, X2 = (0, 1, 0), (0, 2, 0)
TARGETS = (OWN, C, Y, YC, X1)
COUNT = len(TARGETS)


def plus(a, b):
    return tuple((x + y) % d for x, y, d in zip(a, b, HOME))


def number(place):
    return (place[0] * HOME[1] + place[1]) * HOME[2] + place[2]


PLACES = list(itertools.product(*[range(d) for d in HOME]))


def from_place(value, d):
    pairs = [(number(plus(u, d)), number(u)) for u in PLACES]
    return lax.ppermute(value, ("yl", "x", "core"), pairs)


def dots(a, b):
    return lax.dot_general(a, b, (((1,), (1,)), ((), ())), preferred_element_type=jnp.float32)


def best_and_sum(far, rows, diagonal=False):
    alive = far[:, 0:1].astype(jnp.float32) < 1.5
    scores = dots(far, rows)
    total = jnp.sum(jnp.where(alive, scores, 0.0), axis=0, keepdims=True)
    if diagonal:
        same = lax.broadcasted_iota(jnp.int32, scores.shape, 0) == lax.broadcasted_iota(
            jnp.int32, scores.shape, 1
        )
        scores = jnp.where(same, NEVER, scores)
    return jnp.max(jnp.where(alive, scores, NEVER), axis=0, keepdims=True), total


def first_kernel(own, c, y, yc, x1, out):
    held = [own[...], c[...], y[...], yc[...], x1[...]]
    best, total = best_and_sum(held[0], held[0], True)
    best, total = [best], [total]
    pairs = [(0, 1), (0, 2), (0, 3), (0, 4), (1, 4), (2, 4), (3, 4), (4, 0), (4, 1), (4, 2), (4, 3)]
    for p, q in pairs:
        b, t = best_and_sum(held[q], held[p])
        if p < len(best):
            best[p], total[p] = jnp.maximum(best[p], b), total[p] + t
        else:
            best.append(b)
            total.append(t)
    first = (lax.broadcasted_iota(jnp.int32, (8, held[0].shape[1]), 1) == 0).astype(jnp.bfloat16)
    marks = [dots(first, x)[0:1] for x in held]
    out[...] = jnp.concatenate(best + total + marks + [marks[0]], axis=0)


def last_kernel(partial, own, c, y, yc, x2, spread, out):
    best = partial[0:COUNT, :]
    total = partial[COUNT : 2 * COUNT, :]
    alive = partial[2 * COUNT : 3 * COUNT, :] < 1.5
    far = x2[...]
    late = [best_and_sum(far, x[...]) for x in (own, c, y, yc)]
    best = jnp.concatenate(
        [jnp.maximum(best[i : i + 1], late[i][0]) for i in range(4)] + [best[4:5]], axis=0
    )
    total = jnp.concatenate([total[i : i + 1] + late[i][1] for i in range(4)] + [total[4:5]], axis=0)
    square = jnp.sum(jnp.where(alive, total, 0.0))
    best = jnp.concatenate([jnp.where(alive[0:1], best[0:1], DEAD_BEST), best[1:]], axis=0)
    slots = best.shape[1]
    values = jnp.concatenate(
        [best, total, jnp.full((ROWS - 2 * COUNT, slots), square, jnp.float32)], axis=0
    )
    n = out.shape[0] * 8 // ROWS
    lane_z = lax.broadcasted_iota(jnp.int32, (n, ROWS, slots), 2) // 4 % n
    of_z = lane_z == lax.broadcasted_iota(jnp.int32, (n, ROWS, slots), 0)
    chosen = jnp.where(of_z, values[None], 0.0).reshape(n * ROWS, slots)
    wide = jnp.dot(
        chosen,
        spread[...],
        precision=lax.Precision.HIGHEST,
        preferred_element_type=jnp.float32,
    ).reshape(n * ROWS // 8, 8, 128)
    cells = 128 // 8
    keep = lax.broadcasted_iota(jnp.int32, wide.shape, 2) // cells == lax.broadcasted_iota(
        jnp.int32, wide.shape, 1
    )
    out[...] = jnp.sum(jnp.where(keep, wide, 0.0), axis=1)


def local(embeddings, assignment):
    home = ("yl", "x", "core")
    far_y = lax.axis_size("yh")
    n = lax.axis_size("z")
    places = len(PLACES)
    owners = far_y * places
    width = embeddings.shape[1]
    per_owner = 2 * embeddings.shape[0] // owners
    slots = owners * per_owner
    send = outgoing_rows(embeddings, assignment, owners, per_owner)
    own = lax.all_to_all(
        send.reshape(owners, per_owner, width),
        ("yh", "z"),
        split_axis=0,
        concat_axis=0,
        tiled=True,
    ).reshape(slots, width)
    x1 = from_place(own, X1)
    y = from_place(own, Y)
    c = from_place(own, C)
    yc = from_place(y, C)
    x2 = from_place(x1, X1)

    lane = np.arange(slots)
    lane_c = (lane // (per_owner * n)) * per_owner + lane % per_owner
    group = 8
    cells = 128 // group
    spread = jnp.asarray((lane_c[:, None] == np.arange(128)[None, :] % cells), jnp.float32)
    partial = pl.pallas_call(
        first_kernel,
        out_shape=jax.ShapeDtypeStruct((ROWS, slots), jnp.float32),
        in_specs=[pl.BlockSpec(memory_space=pltpu.VMEM)] * 5,
        out_specs=pl.BlockSpec(memory_space=pltpu.VMEM),
        cost_estimate=pl.CostEstimate(
            flops=24 * slots * slots * width, bytes_accessed=5 * slots * width * 2, transcendentals=0
        ),
    )(own, c, y, yc, x1)
    message = pl.pallas_call(
        last_kernel,
        out_shape=jax.ShapeDtypeStruct((n * ROWS // group, 128), jnp.float32),
        in_specs=[pl.BlockSpec(memory_space=pltpu.VMEM)] * 7,
        out_specs=pl.BlockSpec(memory_space=pltpu.VMEM),
        cost_estimate=pl.CostEstimate(
            flops=8 * slots * slots * width, bytes_accessed=5 * slots * width * 2, transcendentals=0
        ),
    )(partial, own, c, y, yc, x2, spread)

    message = lax.all_to_all(
        message.reshape(n, ROWS // group, 128), "z", split_axis=0, concat_axis=0, tiled=True
    )
    arrived = lax.all_to_all(message, home, split_axis=0, concat_axis=0, tiled=True).reshape(
        -1, 1, 128
    )

    keep = jnp.asarray(np.arange(group)[:, None] == np.arange(128)[None, :] // cells)
    rows = jnp.where(keep[None], arrived, 0.0).reshape(places * ROWS, 128)
    wide = jnp.dot(
        rows, spread.T, precision=lax.Precision.HIGHEST, preferred_element_type=jnp.float32
    ).reshape(places, ROWS, slots)
    moved = np.full((places, ROWS), -1)
    for v in range(2 * COUNT):
        for u in PLACES:
            moved[number(u), v] = number(plus(u, TARGETS[v % COUNT]))
    moved = jnp.asarray(moved)[:, :, None]
    lane_u = jnp.asarray((lane // per_owner) % places)[None, None, :]
    result = jnp.sum(jnp.where((moved == lane_u) | (moved < 0), wide, 0.0), axis=0)
    alive = result[0] > NEVER - 1.0
    nearest = jnp.where(alive, jnp.max(result[:COUNT], axis=0), 0.0)
    cosine = jnp.sum(result[COUNT : 2 * COUNT], axis=0) * lax.rsqrt(result[2 * COUNT] + EPSILON)
    distance = jnp.where(alive, 1.0 - cosine, 0.0)
    return nearest.reshape(1, 1, slots), distance.reshape(1, 1, slots)


def solution(mesh):
    names = ("yh", "yl", "x", "core", "z")
    n = mesh.shape["split"]
    parts = Mesh(mesh.devices.reshape(-1, *HOME, n), names)
    in_specs = (P(names, None), P(names))
    out_specs = (P(names[:4], "z", None), P(names[:4], "z", None))
    return jax.shard_map(local, mesh=parts, in_specs=in_specs, out_specs=out_specs, check_vma=False)
```

time: 140 us -> 132 us (0.943); the launches traced: 137 us -> 131 us
  waiting for transfers between devices: 14.8 us -> 3.91 us
  Pallas kernels: 0 us -> 8.75 us
  blocking collectives: 81.6 us -> 87.9 us
  matrix products: 6.8 us -> 0.76 us
  between operations: 4.25 us -> 0.86 us
  other arithmetic: 4.64 us -> 2.06 us
  local copies, waits for them, and re-layouts: 2.63 us -> 4.67 us
    all_to_all x0 -> x1, blocking collectives: none -> 13.9 us  [local(): lax.all_to_all(message, home, split_axis=0, concat_axis=0, tiled=True)]
    ppermute x6 -> x5, waiting for transfers between devices: 14.8 us -> 3.91 us  [from_place(): return lax.ppermute(value, ('yl', 'x', 'core'), pairs)]
    pallas_call x0 -> x2, Pallas kernels: none -> 8.75 us  [the longest x1 4.82 us: local(): pl.pallas_call(first_kernel, out_shape=jax.ShapeDtypeStruct((ROWS, slots)...]
    all_to_all x1, blocking collectives: 26.9 us -> 19.2 us  [local(): lax.all_to_all(message.reshape(n, ROWS // group, 128), 'z', split_axis=0,...]
    dot_general x18 -> x1, matrix products: 6.43 us -> 0.39 us  [local(): jnp.dot(rows, spread.T, precision=lax.Precision.HIGHEST, preferred_elemen...]
    unnamed x16 -> x26, local copies, waits for them, and re-layouts: 2.18 us -> 4.35 us
    reduce_sum x4 -> x1, other arithmetic: 1.92 us -> 0.02 us  [local(): jnp.sum(result[COUNT:2 * COUNT], axis=0)]
    ppermute x6 -> x5, starting transfers between devices: 22.6 us -> 22.5 us  [from_place(): return lax.ppermute(value, ('yl', 'x', 'core'), pairs)]
  transfers between devices with their start and end apart: 6 -> 5, of which waited for: 4 -> 1; matrix products, arithmetic and copies ran while one was open for 2% -> 0% of each run, Pallas kernels for 0% -> 4%
where the time goes in v5:
time: 132 us; the launch traced here: 131 us
  blocking collectives  87.9 us (67%)
  starting transfers between devices  22.5 us (17%)
  Pallas kernels  8.75 us (7%)
  local copies, waits for them, and re-layouts  4.67 us (4%)
  waiting for transfers between devices  3.91 us (3%)
  other arithmetic  2.06 us (2%)
    all_to_all x1, blocking collectives, local(): lax.all_to_all(send.reshape(owners, per_owner, width), ('yh', 'z'), split...  54.8 us
    ppermute x5, starting transfers between devices, from_place(): return lax.ppermute(value, ('yl', 'x', 'core'), pairs)  22.5 us
    all_to_all x1, blocking collectives, local(): lax.all_to_all(message.reshape(n, ROWS // group, 128), 'z', split_axis=0,...  19.2 us
    all_to_all x1, blocking collectives, local(): lax.all_to_all(message, home, split_axis=0, concat_axis=0, tiled=True)  13.9 us
    pallas_call x1, Pallas kernels, local(): pl.pallas_call(first_kernel, out_shape=jax.ShapeDtypeStruct((ROWS, slots)...  4.82 us
    unnamed x26, local copies, waits for them, and re-layouts  4.35 us
    pallas_call x1, Pallas kernels, local(): pl.pallas_call(last_kernel, out_shape=jax.ShapeDtypeStruct((n * ROWS // g...  3.93 us
    ppermute x5, waiting for transfers between devices, from_place(): return lax.ppermute(value, ('yl', 'x', 'core'), pairs)  3.91 us
  transfers between devices with their start and end apart: 5, of which 1 were waited for; matrix products, arithmetic and copies ran while one was open for 0% of the time, Pallas kernels for 4%

profile of v5, /device:TPU:1, one launch (start us, length us, event | category | flops | bytes accessed | tf_op | source)
XLA Modules:
  0.0 131.4 jit_solution(6349346375695068527)
XLA Ops:
  0.6 0.0 copy-start.5
  0.7 1.1 fusion.2
  1.8 0.0 copy-start.8
  1.8 0.6 copy-done.8
  2.4 0.2 convert_reduce_fusion
  2.6 0.1 fusion.6
  2.8 0.0 copy-done.5
  2.8 0.4 fusion
  3.2 0.2 reshape.101
  3.4 54.8 %all_to_all.15 = bf16[64,4,1024]{2,1,0:T(4,128)(2,1)S(1)} all-to-all(bf16[64,4,1024]{2,1,0:T(4,128)(2,1)S(1)} %reshape.101), channel_id=1, replica_groups=mesh['yh'=4,'yl'=2,'x'=4,'core'=2,'z'=16] {'yh','z'}, dimensions={0} | all-to-all | bytes 1048576 | tf_op jit(solution)/shard_map/all_to_all | solution.py:141
  58.1 0.1 reshape.102.own
  58.3 0.0 copy-start
  58.3 2.3 %collective-permute-start.1 = (bf16[256,1024]{1,0:T(8,128)(2,1)S(1)}, bf16[256,1024]{1,0:T(8,128)(2,1)S(1)}, u32[]{:S(2)}, u32[]{:S(2)}) collective-permute-start(bf16[256,1024]{1,0:T(8,128)(2,1)S(1)} %reshape.102.own), channel_id=1, source_target_pairs={{128,0},{144,16},{160,32},{176,48},{192,64},{208,80},{224,96},{240... | collective-permute-start | bytes 1572872 | tf_op jit(solution)/shard_map/ppermute | solution.py:62
  60.6 4.4 %collective-permute-start.3 = (bf16[256,1024]{1,0:T(8,128)(2,1)S(1)}, bf16[256,1024]{1,0:T(8,128)(2,1)S(1)}, u32[]{:S(2)}, u32[]{:S(2)}) collective-permute-start(bf16[256,1024]{1,0:T(8,128)(2,1)S(1)} %reshape.102.own), channel_id=1, source_target_pairs={{32,0},{48,16},{64,32},{80,48},{96,64},{112,80},{0,96},{16,112},{1... | collective-permute-start | bytes 1572872 | tf_op jit(solution)/shard_map/ppermute | solution.py:62
  65.0 5.7 %collective-permute-start = (bf16[256,1024]{1,0:T(8,128)(2,1)S(1)}, bf16[256,1024]{1,0:T(8,128)(2,1)S(1)}, u32[]{:S(2)}, u32[]{:S(2)}) collective-permute-start(bf16[256,1024]{1,0:T(8,128)(2,1)S(1)} %reshape.102.own), channel_id=1, source_target_pairs={{16,0},{0,16},{48,32},{32,48},{80,64},{64,80},{112,96},{96,112},{1... | collective-permute-start | bytes 1572872 | tf_op jit(solution)/shard_map/ppermute | solution.py:62
  70.7 0.0 collective-permute-done.1.y
  70.7 0.0 copy-start.1
  70.7 5.7 %collective-permute-start.2 = (bf16[256,1024]{1,0:T(8,128)(2,1)S(1)}, bf16[256,1024]{1,0:T(8,128)(2,1)S(1)}, u32[]{:S(2)}, u32[]{:S(2)}) collective-permute-start(bf16[256,1024]{1,0:T(8,128)(2,1)S(1)} %collective-permute-done.1.y), channel_id=1, source_target_pairs={{16,0},{0,16},{48,32},{32,48},{80,64},{64,80},{112,96},{96,112},{1... | collective-permute-start | bytes 1572872 | tf_op jit(solution)/shard_map/ppermute | solution.py:62
  76.4 0.0 collective-permute-done.3.x1
  76.4 0.0 copy-start.7
  76.4 4.4 %collective-permute-start.4 = (bf16[256,1024]{1,0:T(8,128)(2,1)S(1)}, bf16[256,1024]{1,0:T(8,128)(2,1)S(1)}, u32[]{:S(2)}, u32[]{:S(2)}) collective-permute-start(bf16[256,1024]{1,0:T(8,128)(2,1)S(1)} %collective-permute-done.3.x1), channel_id=1, source_target_pairs={{32,0},{48,16},{64,32},{80,48},{96,64},{112,80},{0,96},{16,112},{1... | collective-permute-start | bytes 1572872 | tf_op jit(solution)/shard_map/ppermute | solution.py:62
  80.8 0.0 collective-permute-done.c
  80.8 0.0 copy-start.2
  80.8 0.0 collective-permute-done.2.yc
  80.9 0.0 copy-done
  80.9 0.0 copy-done.1
  80.9 0.0 copy-done.7
  80.9 0.7 copy-done.2
  81.6 0.0 copy-start.3
  81.6 0.8 copy-done.3
  82.4 4.8 %shard_map.77.partial = f32[16,256]{1,0:T(8,128)} custom-call(bf16[256,1024]{1,0:T(8,128)(2,1)} %copy-done, bf16[256,1024]{1,0:T(8,128)(2,1)} %copy-done.2, bf16[256,1024]{1,0:T(8,128)(2,1)} %copy-done.1, bf16[256,1024]{1,0:T(8,128)(2,1)} %copy-done.3, bf16[256,1024]{1,0:T(8,128)(2,1)} %copy-done.7), custom_call_target="tpu_custom_call" | custom-call | flops 1610612736 | bytes 2621440 | tf_op jit(solution)/shard_map/pallas_call | solution.py:159
  87.3 3.9 %collective-permute-done.4.x2 = bf16[256,1024]{1,0:T(8,128)(2,1)S(1)} collective-permute-done((bf16[256,1024]{1,0:T(8,128)(2,1)S(1)}, bf16[256,1024]{1,0:T(8,128)(2,1)S(1)}, u32[]{:S(2)}, u32[]{:S(2)}) %collective-permute-start.4) | collective-permute-done | bytes 524320 | tf_op jit(solution)/shard_map/ppermute | solution.py:62
  91.1 0.0 copy-start.4
  91.2 0.8 copy-done.4
  91.9 0.0 copy-start.9
  91.9 3.9 %shard_map.78 = f32[32,128]{1,0:T(8,128)} custom-call(f32[16,256]{1,0:T(8,128)} %shard_map.77.partial, bf16[256,1024]{1,0:T(8,128)(2,1)} %copy-done, bf16[256,1024]{1,0:T(8,128)(2,1)} %copy-done.2, bf16[256,1024]{1,0:T(8,128)(2,1)} %copy-done.1, bf16[256,1024]{1,0:T(8,128)(2,1)} %copy-done.3, bf16[256,1024]{1,0:T(8,128)(2,1)} %copy-done.4, ...), custom_call_target="tpu_custom_call" | custom-call | flops 536870912 | bytes 2621440 | tf_op jit(solution)/shard_map/pallas_call | solution.py:168
  95.9 19.2 %all_to_all.16 = f32[16,2,128]{2,1,0:T(2,128)S(1)} all-to-all(f32[16,2,128]{2,1,0:T(2,128)} %bitcast.18), channel_id=1, replica_groups=mesh['yh'=4,'yl'=2,'x'=4,'core'=2,'z'=16] {'z'}, dimensions={0} | all-to-all | bytes 32768 | tf_op jit(solution)/shard_map/all_to_all | solution.py:178
  115.1 13.9 %all_to_all.17 = f32[16,2,128]{2,1,0:T(2,128)S(1)} all-to-all(f32[16,2,128]{2,1,0:T(2,128)S(1)} %all_to_all.16), channel_id=1, replica_groups=mesh['yh'=4,'yl'=2,'x'=4,'core'=2,'z'=16] {'yl','x','core'}, dimensions={0} | all-to-all | bytes 32768 | tf_op jit(solution)/shard_map/all_to_all | solution.py:181
  129.0 0.0 copy-start.6
  129.0 0.7 copy-done.6
  129.7 0.0 copy-start.10
  129.7 0.0 copy-start.12
  129.7 0.0 copy-done.9
  129.7 0.7 copy-done.10
  130.4 0.0 copy-done.11
  130.4 0.0 copy-done.12
  130.4 0.4 fusion.1
  130.8 0.6 bitcast_select_fusion
  (7 shorter events, 0.1 us)
Async XLA Ops:
  0.6 2.1 %copy-start.5 = (bf16[128,1024]{1,0:T(8,128)(2,1)S(1)}, bf16[128,1024]{1,0:T(8,128)(2,1)}, u32[]{:S(2)}) copy-start(bf16[128,1024]{1,0:T(8,128)(2,1)} %param.6) | copy-start | bytes 786436
  1.8 0.7 copy-start.8
  58.3 22.6 %copy-start = (bf16[256,1024]{1,0:T(8,128)(2,1)}, bf16[256,1024]{1,0:T(8,128)(2,1)S(1)}, u32[]{:S(2)}) copy-start(bf16[256,1024]{1,0:T(8,128)(2,1)S(1)} %reshape.102.own) | copy-start | bytes 1572868
  58.3 12.4 %collective-permute-start.1 = (bf16[256,1024]{1,0:T(8,128)(2,1)S(1)}, bf16[256,1024]{1,0:T(8,128)(2,1)S(1)}, u32[]{:S(2)}, u32[]{:S(2)}) collective-permute-start(bf16[256,1024]{1,0:T(8,128)(2,1)S(1)} %reshape.102.own), channel_id=1, source_target_pairs={{128,0},{144,16},{160,32},{176,48},{192,64},{208,80},{224,96},{240... | collective-permute-start | bytes 1572872 | tf_op jit(solution)/shard_map/ppermute | solution.py:62
  60.6 15.8 %collective-permute-start.3 = (bf16[256,1024]{1,0:T(8,128)(2,1)S(1)}, bf16[256,1024]{1,0:T(8,128)(2,1)S(1)}, u32[]{:S(2)}, u32[]{:S(2)}) collective-permute-start(bf16[256,1024]{1,0:T(8,128)(2,1)S(1)} %reshape.102.own), channel_id=1, source_target_pairs={{32,0},{48,16},{64,32},{80,48},{96,64},{112,80},{0,96},{16,112},{1... | collective-permute-start | bytes 1572872 | tf_op jit(solution)/shard_map/ppermute | solution.py:62
  65.0 15.8 %collective-permute-start = (bf16[256,1024]{1,0:T(8,128)(2,1)S(1)}, bf16[256,1024]{1,0:T(8,128)(2,1)S(1)}, u32[]{:S(2)}, u32[]{:S(2)}) collective-permute-start(bf16[256,1024]{1,0:T(8,128)(2,1)S(1)} %reshape.102.own), channel_id=1, source_target_pairs={{16,0},{0,16},{48,32},{32,48},{80,64},{64,80},{112,96},{96,112},{1... | collective-permute-start | bytes 1572872 | tf_op jit(solution)/shard_map/ppermute | solution.py:62
  70.7 10.1 %copy-start.1 = (bf16[256,1024]{1,0:T(8,128)(2,1)}, bf16[256,1024]{1,0:T(8,128)(2,1)S(1)}, u32[]{:S(2)}) copy-start(bf16[256,1024]{1,0:T(8,128)(2,1)S(1)} %collective-permute-done.1.y) | copy-start | bytes 1572868
  70.7 10.1 %collective-permute-start.2 = (bf16[256,1024]{1,0:T(8,128)(2,1)S(1)}, bf16[256,1024]{1,0:T(8,128)(2,1)S(1)}, u32[]{:S(2)}, u32[]{:S(2)}) collective-permute-start(bf16[256,1024]{1,0:T(8,128)(2,1)S(1)} %collective-permute-done.1.y), channel_id=1, source_target_pairs={{16,0},{0,16},{48,32},{32,48},{80,64},{64,80},{112,96},{96,112},{1... | collective-permute-start | bytes 1572872 | tf_op jit(solution)/shard_map/ppermute | solution.py:62
  76.4 4.5 %copy-start.7 = (bf16[256,1024]{1,0:T(8,128)(2,1)}, bf16[256,1024]{1,0:T(8,128)(2,1)S(1)}, u32[]{:S(2)}) copy-start(bf16[256,1024]{1,0:T(8,128)(2,1)S(1)} %collective-permute-done.3.x1) | copy-start | bytes 1572868
  76.4 14.7 %collective-permute-start.4 = (bf16[256,1024]{1,0:T(8,128)(2,1)S(1)}, bf16[256,1024]{1,0:T(8,128)(2,1)S(1)}, u32[]{:S(2)}, u32[]{:S(2)}) collective-permute-start(bf16[256,1024]{1,0:T(8,128)(2,1)S(1)} %collective-permute-done.3.x1), channel_id=1, source_target_pairs={{32,0},{48,16},{64,32},{80,48},{96,64},{112,80},{0,96},{16,112},{1... | collective-permute-start | bytes 1572872 | tf_op jit(solution)/shard_map/ppermute | solution.py:62
  80.8 0.8 copy-start.2
  81.6 0.8 copy-start.3
  91.1 0.8 copy-start.4
  91.9 37.8 %copy-start.9 = (f32[256,128,1]{1,0,2:T(8,128)S(1)}, f32[256,128,1]{1,0,2:T(8,128)}, u32[]{:S(2)}) copy-start(f32[256,128,1]{1,0,2:T(8,128)} %constant.36) | copy-start | bytes 393220
  129.0 0.7 copy-start.6
  129.7 0.7 copy-start.10
  129.7 0.7 copy-start.11
  129.7 0.7 copy-start.12

commit v6 on v5

v6 whole, which is shorter than its diff:
```python
import itertools

import jax
import jax.numpy as jnp
from jax import lax
from jax.experimental import pallas as pl
from jax.experimental.pallas import tpu as pltpu
from jax.sharding import Mesh
from jax.sharding import PartitionSpec as P

EPSILON = 1e-06
NEVER = -2.0
DEAD_MARK = 2.0


def normalize_rows(values):
    as_float = values.astype(jnp.float32)
    return (
        as_float * lax.rsqrt(jnp.sum(as_float * as_float, axis=1, keepdims=True) + EPSILON)
    ).astype(jnp.bfloat16)


def outgoing_rows(embeddings, assignment, owners, per_owner):
    row_count = embeddings.shape[0]
    slot_count = owners * per_owner
    normed = normalize_rows(embeddings)
    same = assignment[:, None] == assignment[None, :]
    earlier = jnp.arange(row_count)[None, :] < jnp.arange(row_count)[:, None]
    rank = jnp.sum((same & earlier).astype(jnp.int32), axis=1)
    target = assignment * per_owner + rank
    table = target[None, :] == jnp.arange(slot_count, dtype=jnp.int32)[:, None]
    rows = jnp.dot(table.astype(jnp.bfloat16), normed, preferred_element_type=jnp.float32)
    filled = jnp.any(table, axis=1)
    first = jnp.arange(embeddings.shape[1], dtype=jnp.int32)[None, :] == 0
    rows = jnp.where(first & ~filled[:, None], DEAD_MARK, rows)
    return rows.astype(jnp.bfloat16)


DEAD_BEST = -8.0
ROWS = 16
HOME = (2, 4, 2)
OWN, C, Y, YC = (0, 0, 0), (0, 0, 1), (1, 0, 0), (1, 0, 1)
X1, X2 = (0, 1, 0), (0, 2, 0)
TARGETS = (OWN, C, Y, YC, X1)
COUNT = len(TARGETS)


def plus(a, b):
    return tuple((x + y) % d for x, y, d in zip(a, b, HOME))


def number(place):
    return (place[0] * HOME[1] + place[1]) * HOME[2] + place[2]


PLACES = list(itertools.product(*[range(d) for d in HOME]))


def from_place(value, d):
    pairs = [(number(plus(u, d)), number(u)) for u in PLACES]
    return lax.ppermute(value, ("yl", "x", "core"), pairs)


def dots(a, b):
    return lax.dot_general(a, b, (((1,), (1,)), ((), ())), preferred_element_type=jnp.float32)


def best_and_sum(far, rows, diagonal=False):
    alive = far[:, 0:1].astype(jnp.float32) < 1.5
    scores = dots(far, rows)
    total = jnp.sum(jnp.where(alive, scores, 0.0), axis=0, keepdims=True)
    if diagonal:
        same = lax.broadcasted_iota(jnp.int32, scores.shape, 0) == lax.broadcasted_iota(
            jnp.int32, scores.shape, 1
        )
        scores = jnp.where(same, NEVER, scores)
    return jnp.max(jnp.where(alive, scores, NEVER), axis=0, keepdims=True), total


def own_kernel(own, out):
    best, total = best_and_sum(own[...], own[...], True)
    out[...] = jnp.concatenate([best, total] * 4, axis=0)


def first_kernel(mine, own, y, swapped, x1, out):
    slots = own.shape[0]
    held = [own[...], swapped[:slots, :], y[...], swapped[slots:, :], x1[...]]
    best, total = [mine[0:1, :]], [mine[1:2, :]]
    pairs = [(0, 1), (0, 2), (0, 3), (0, 4), (1, 4), (2, 4), (3, 4), (4, 0), (4, 1), (4, 2), (4, 3)]
    for p, q in pairs:
        b, t = best_and_sum(held[q], held[p])
        if p < len(best):
            best[p], total[p] = jnp.maximum(best[p], b), total[p] + t
        else:
            best.append(b)
            total.append(t)
    first = (lax.broadcasted_iota(jnp.int32, (8, held[0].shape[1]), 1) == 0).astype(jnp.bfloat16)
    marks = [dots(first, x)[0:1] for x in held]
    out[...] = jnp.concatenate(best + total + marks + [marks[0]], axis=0)


def iota(shape, axis):
    return lax.broadcasted_iota(jnp.int32, shape, axis)


def exact_dot(a, b):
    return lax.dot_general(
        a,
        b,
        (((1,), (0,)), ((), ())),
        precision=lax.Precision.HIGHEST,
        preferred_element_type=jnp.float32,
    )


GROUP = 8
CELLS = 16


def cell_of(slot):
    return slot // 64 * 4 + slot % 4


def place_of(slot):
    return slot // 4 % 16


def last_kernel(partial, own, y, swapped, x2, out):
    best = partial[0:COUNT, :]
    total = partial[COUNT : 2 * COUNT, :]
    alive = partial[2 * COUNT : 3 * COUNT, :] < 1.5
    far = x2[...]
    slots = own.shape[0]
    targets = (own[...], swapped[:slots, :], y[...], swapped[slots:, :])
    late = [best_and_sum(far, x) for x in targets]
    best = jnp.concatenate(
        [jnp.maximum(best[i : i + 1], late[i][0]) for i in range(4)] + [best[4:5]], axis=0
    )
    total = jnp.concatenate([total[i : i + 1] + late[i][1] for i in range(4)] + [total[4:5]], axis=0)
    square = jnp.sum(jnp.where(alive, total, 0.0))
    best = jnp.concatenate([jnp.where(alive[0:1], best[0:1], DEAD_BEST), best[1:]], axis=0)
    values = jnp.concatenate(
        [best, total, jnp.full((ROWS - 2 * COUNT, slots), square, jnp.float32)], axis=0
    )
    n = out.shape[0] * GROUP // ROWS
    shape = (n, ROWS, slots)
    chosen = jnp.where(place_of(iota(shape, 2)) == iota(shape, 0), values[None], 0.0)
    shape = (slots, GROUP * CELLS)
    spread = (cell_of(iota(shape, 0)) == iota(shape, 1) % CELLS).astype(jnp.float32)
    wide = exact_dot(chosen.reshape(n * ROWS, slots), spread).reshape(-1, GROUP, GROUP * CELLS)
    keep = iota(wide.shape, 2) // CELLS == iota(wide.shape, 1)
    out[...] = jnp.sum(jnp.where(keep, wide, 0.0), axis=1)


def finish_kernel(arrived, nearest, distance):
    slots = nearest.shape[1]
    places = arrived.shape[0] * GROUP // ROWS
    shape = (arrived.shape[0], GROUP, GROUP * CELLS)
    keep = iota(shape, 2) // CELLS == iota(shape, 1)
    rows = jnp.where(keep, arrived[...][:, None, :], 0.0).reshape(places * ROWS, GROUP * CELLS)
    shape = (GROUP * CELLS, slots)
    spread = (cell_of(iota(shape, 1)) == iota(shape, 0) % CELLS).astype(jnp.float32)
    wide = exact_dot(rows, spread).reshape(places, ROWS, slots)
    u, v, to = (iota(wide.shape, axis) for axis in range(3))
    target = v % COUNT
    core = (u ^ jnp.where((target == 1) | (target == 3), 1, 0)) & 1
    low = (u ^ jnp.where((target == 2) | (target == 3), 8, 0)) & 8
    across = (u + jnp.where(target == 4, 2, 0)) & 6
    here = (core + low + across == place_of(to)) | (v >= 2 * COUNT)
    result = jnp.sum(jnp.where(here, wide, 0.0), axis=0)
    alive = result[0:1] > NEVER - 1.0
    best = jnp.max(result[0:COUNT], axis=0, keepdims=True)
    nearest[...] = jnp.where(alive, best, 0.0)
    cosine = jnp.sum(result[COUNT : 2 * COUNT], axis=0, keepdims=True) * lax.rsqrt(
        result[2 * COUNT : 2 * COUNT + 1] + EPSILON
    )
    distance[...] = jnp.where(alive, 1.0 - cosine, 0.0)


def on_chip(kernel, out_shape, flops, *operands):
    vmem = pl.BlockSpec(memory_space=pltpu.VMEM)
    single = isinstance(out_shape, jax.ShapeDtypeStruct)
    return pl.pallas_call(
        kernel,
        out_shape=out_shape,
        in_specs=[vmem] * len(operands),
        out_specs=vmem if single else [vmem] * len(out_shape),
        compiler_params=pltpu.CompilerParams(vmem_limit_bytes=16 * 2**20),
        cost_estimate=pl.CostEstimate(
            flops=flops, bytes_accessed=sum(x.size * 2 for x in operands), transcendentals=0
        ),
    )(*operands)


def local(embeddings, assignment):
    home = ("yl", "x", "core")
    far_y = lax.axis_size("yh")
    n = lax.axis_size("z")
    places = len(PLACES)
    owners = far_y * places
    width = embeddings.shape[1]
    per_owner = 2 * embeddings.shape[0] // owners
    slots = owners * per_owner
    send = outgoing_rows(embeddings, assignment, owners, per_owner)
    own = lax.all_to_all(
        send.reshape(owners, per_owner, width),
        ("yh", "z"),
        split_axis=0,
        concat_axis=0,
        tiled=True,
    ).reshape(slots, width)
    tile = 2 * slots * slots * width
    x1 = from_place(own, X1)
    mine = on_chip(own_kernel, jax.ShapeDtypeStruct((8, slots), jnp.float32), tile, own)
    y = from_place(own, Y)
    x2 = from_place(x1, X1)
    y, x1, mine = lax.optimization_barrier((y, x1, mine))
    swapped = from_place(jnp.concatenate([own, y]), C)
    partial = on_chip(
        first_kernel,
        jax.ShapeDtypeStruct((ROWS, slots), jnp.float32),
        0,
        mine,
        own,
        y,
        swapped,
        x1,
    )
    message = on_chip(
        last_kernel,
        jax.ShapeDtypeStruct((n * ROWS // GROUP, GROUP * CELLS), jnp.float32),
        4 * tile,
        partial,
        own,
        y,
        swapped,
        x2,
    )
    message = message.reshape(n, ROWS // GROUP, GROUP * CELLS)
    message = lax.all_to_all(message, "z", split_axis=0, concat_axis=0, tiled=True)
    message = lax.all_to_all(message, home, split_axis=0, concat_axis=0, tiled=True)
    row = jax.ShapeDtypeStruct((1, slots), jnp.float32)
    nearest, distance = on_chip(
        finish_kernel, (row, row), 0, message.reshape(places * ROWS // GROUP, GROUP * CELLS)
    )
    return nearest.reshape(1, 1, slots), distance.reshape(1, 1, slots)


def solution(mesh):
    names = ("yh", "yl", "x", "core", "z")
    n = mesh.shape["split"]
    parts = Mesh(mesh.devices.reshape(-1, *HOME, n), names)
    in_specs = (P(names, None), P(names))
    out_specs = (P(names[:4], "z", None), P(names[:4], "z", None))
    return jax.shard_map(local, mesh=parts, in_specs=in_specs, out_specs=out_specs, check_vma=False)
```

time: 132 us -> 131 us (level)
  waiting for transfers between devices: 3.91 us -> 19.7 us
  starting transfers between devices: 22.5 us -> 15.5 us
  local copies, waits for them, and re-layouts: 4.67 us -> 0.31 us
  Pallas kernels: 8.75 us -> 5.3 us
  blocking collectives: 87.9 us -> 85.1 us
    ppermute x5 -> x4, waiting for transfers between devices: 3.91 us -> 19.7 us  [from_place(): return lax.ppermute(value, ('yl', 'x', 'core'), pairs)]
    ppermute x5 -> x4, starting transfers between devices: 22.5 us -> 15.5 us  [from_place(): return lax.ppermute(value, ('yl', 'x', 'core'), pairs)]
    unnamed x26 -> x0, local copies, waits for them, and re-layouts: 4.35 us -> none
    pallas_call x2 -> x4, Pallas kernels: 8.75 us -> 5.3 us  [on_chip(): pl.pallas_call(kernel, out_shape=out_shape, in_specs=[vmem] * len(operand...]
    all_to_all x1, blocking collectives: 13.9 us -> 11.2 us  [local(): lax.all_to_all(message, home, split_axis=0, concat_axis=0, tiled=True)]
  transfers between devices with their start and end apart: 5 -> 4, of which waited for: 1 -> 3; matrix products, arithmetic and copies ran while one was open for 0% -> 0% of each run, Pallas kernels for 4% -> 2%
where the time goes in v6:
time: 131 us
  blocking collectives  85.1 us (65%)
  waiting for transfers between devices  19.7 us (15%)
  starting transfers between devices  15.5 us (12%)
  Pallas kernels  5.3 us (4%)
  other arithmetic  2.86 us (2%)
  matrix products  1.33 us (1%)
    all_to_all x1, blocking collectives, local(): lax.all_to_all(send.reshape(owners, per_owner, width), ('yh', 'z'), split...  54.8 us
    ppermute x4, waiting for transfers between devices, from_place(): return lax.ppermute(value, ('yl', 'x', 'core'), pairs)  19.7 us
    all_to_all x1, blocking collectives, local(): lax.all_to_all(message, 'z', split_axis=0, concat_axis=0, tiled=True)  19.1 us
    ppermute x4, starting transfers between devices, from_place(): return lax.ppermute(value, ('yl', 'x', 'core'), pairs)  15.5 us
    all_to_all x1, blocking collectives, local(): lax.all_to_all(message, home, split_axis=0, concat_axis=0, tiled=True)  11.2 us
    pallas_call x4, Pallas kernels, on_chip(): pl.pallas_call(kernel, out_shape=out_shape, in_specs=[vmem] * len(operand...  5.3 us
  transfers between devices with their start and end apart: 4, of which 3 were waited for; matrix products, arithmetic and copies ran while one was open for 0% of the time, Pallas kernels for 2%

profile of v6, /device:TPU:1, one launch (start us, length us, event | category | flops | bytes accessed | tf_op | source)
XLA Modules:
  0.0 130.8 jit_solution(13471631658909872604)
XLA Ops:
  0.6 0.9 convert_reduce_fusion
  1.5 0.7 multiply_add_fusion
  2.2 0.1 fusion.5
  2.3 1.1 fusion.1
  3.4 1.3 %fusion = bf16[256,1024]{1,0:T(8,128)(2,1)S(1)} fusion(pred[1024]{0:T(1024)(128)(4,1)S(1)} %iota_compare_fusion.3, pred[256]{0:T(512)(128)(4,1)S(1)} %not.8, bf16[128,1024]{1,0:T(8,128)(2,1)} %param.2, f32[128]{0:T(128)S(1)} %add_rsqrt_fusion, s32[128]{0:T(128)S(1)} %multiply_add_fusion), kind=kOutput, calls=%fused_computation.1 | convolution fusion | flops 68321280 | bytes 788736 | tf_op jit(solution)/shard_map/dot_general | solution.py:32
  4.8 0.2 reshape.40
  5.0 54.8 %all_to_all.15 = bf16[64,4,1024]{2,1,0:T(4,128)(2,1)S(1)} all-to-all(bf16[64,4,1024]{2,1,0:T(4,128)(2,1)S(1)} %reshape.40), channel_id=1, replica_groups=mesh['yh'=4,'yl'=2,'x'=4,'core'=2,'z'=16] {'yh','z'}, dimensions={0} | all-to-all | bytes 1048576 | tf_op jit(solution)/shard_map/all_to_all | solution.py:205
  59.8 0.1 reshape.41.own
  59.9 4.4 %collective-permute-start.1 = (bf16[256,1024]{1,0:T(8,128)(2,1)S(1)}, bf16[256,1024]{1,0:T(8,128)(2,1)S(1)}, u32[]{:S(2)}, u32[]{:S(2)}) collective-permute-start(bf16[256,1024]{1,0:T(8,128)(2,1)S(1)} %reshape.41.own), channel_id=1, source_target_pairs={{32,0},{48,16},{64,32},{80,48},{96,64},{112,80},{0,96},{16,112},{1... | collective-permute-start | bytes 1572872 | tf_op jit(solution)/shard_map/ppermute | solution.py:61
  64.3 2.3 %collective-permute-start = (bf16[256,1024]{1,0:T(8,128)(2,1)S(1)}, bf16[256,1024]{1,0:T(8,128)(2,1)S(1)}, u32[]{:S(2)}, u32[]{:S(2)}) collective-permute-start(bf16[256,1024]{1,0:T(8,128)(2,1)S(1)} %reshape.41.own), channel_id=1, source_target_pairs={{128,0},{144,16},{160,32},{176,48},{192,64},{208,80},{224,96},{240... | collective-permute-start | bytes 1572872 | tf_op jit(solution)/shard_map/ppermute | solution.py:61
  66.6 0.4 shard_map.41.mine
  67.0 5.3 %collective-permute-done.1.x1 = bf16[256,1024]{1,0:T(8,128)(2,1)S(1)} collective-permute-done((bf16[256,1024]{1,0:T(8,128)(2,1)S(1)}, bf16[256,1024]{1,0:T(8,128)(2,1)S(1)}, u32[]{:S(2)}, u32[]{:S(2)}) %collective-permute-start.1) | collective-permute-done | bytes 524320 | tf_op jit(solution)/shard_map/ppermute | solution.py:61
  72.2 3.8 %collective-permute-done.y = bf16[256,1024]{1,0:T(8,128)(2,1)S(1)} collective-permute-done((bf16[256,1024]{1,0:T(8,128)(2,1)S(1)}, bf16[256,1024]{1,0:T(8,128)(2,1)S(1)}, u32[]{:S(2)}, u32[]{:S(2)}) %collective-permute-start) | collective-permute-done | bytes 524320 | tf_op jit(solution)/shard_map/ppermute | solution.py:61
  76.0 0.1 pad_maximum_fusion
  76.1 6.4 %collective-permute-start.2 = (bf16[512,1024]{1,0:T(8,128)(2,1)S(1)}, bf16[512,1024]{1,0:T(8,128)(2,1)S(1)}, u32[]{:S(2)}, u32[]{:S(2)}) collective-permute-start(bf16[512,1024]{1,0:T(8,128)(2,1)S(1)} %pad_maximum_fusion), channel_id=1, source_target_pairs={{16,0},{0,16},{48,32},{32,48},{80,64},{64,80},{112,96},{96,112},{1... | collective-permute-start | bytes 3145736 | tf_op jit(solution)/shard_map/ppermute | solution.py:61
  82.5 2.5 %collective-permute-start.3 = (bf16[256,1024]{1,0:T(8,128)(2,1)S(1)}, bf16[256,1024]{1,0:T(8,128)(2,1)S(1)}, u32[]{:S(2)}, u32[]{:S(2)}) collective-permute-start(bf16[256,1024]{1,0:T(8,128)(2,1)S(1)} %collective-permute-done.1.x1), channel_id=1, source_target_pairs={{32,0},{48,16},{64,32},{80,48},{96,64},{112,80},{0,96},{16,112},{1... | collective-permute-start | bytes 1572872 | tf_op jit(solution)/shard_map/ppermute | solution.py:61
  85.0 0.0 collective-permute-done.2.swapped
  85.0 2.4 %shard_map.42.partial = f32[16,256]{1,0:T(8,128)S(1)} custom-call(f32[8,256]{1,0:T(8,128)S(1)} %shard_map.41.mine, bf16[256,1024]{1,0:T(8,128)(2,1)S(1)} %reshape.41.own, bf16[256,1024]{1,0:T(8,128)(2,1)S(1)} %collective-permute-done.y, bf16[512,1024]{1,0:T(8,128)(2,1)S(1)} %collective-permute-done.2.swapped, bf16[256,1024]{1,0:T(8,128)(2,1)S(1)} %collective-permute-done.1.x1), custom_call_target="tpu_custom_call" | custom-call | bytes 2625536 | tf_op jit(solution)/shard_map/pallas_call | solution.py:183
  87.4 10.6 %collective-permute-done.3.x2 = bf16[256,1024]{1,0:T(8,128)(2,1)S(1)} collective-permute-done((bf16[256,1024]{1,0:T(8,128)(2,1)S(1)}, bf16[256,1024]{1,0:T(8,128)(2,1)S(1)}, u32[]{:S(2)}, u32[]{:S(2)}) %collective-permute-start.3) | collective-permute-done | bytes 524320 | tf_op jit(solution)/shard_map/ppermute | solution.py:61
  97.9 1.6 %shard_map.43 = f32[32,128]{1,0:T(8,128)S(1)} custom-call(f32[16,256]{1,0:T(8,128)S(1)} %shard_map.42.partial, bf16[256,1024]{1,0:T(8,128)(2,1)S(1)} %reshape.41.own, bf16[256,1024]{1,0:T(8,128)(2,1)S(1)} %collective-permute-done.y, bf16[512,1024]{1,0:T(8,128)(2,1)S(1)} %collective-permute-done.2.swapped, bf16[256,1024]{1,0:T(8,128)(2,1)S(1)} %collective-permute-done.3.x2), custom_call_target="tpu_custom_call" | custom-call | flops 536870912 | bytes 2629632 | tf_op jit(solution)/shard_map/pallas_call | solution.py:183
  99.5 19.1 %all_to_all.16 = f32[16,2,128]{2,1,0:T(2,128)S(1)} all-to-all(f32[16,2,128]{2,1,0:T(2,128)S(1)} %bitcast.5), channel_id=1, replica_groups=mesh['yh'=4,'yl'=2,'x'=4,'core'=2,'z'=16] {'z'}, dimensions={0} | all-to-all | bytes 32768 | tf_op jit(solution)/shard_map/all_to_all | solution.py:240
  118.6 11.2 %all_to_all.17 = f32[16,2,128]{2,1,0:T(2,128)S(1)} all-to-all(f32[16,2,128]{2,1,0:T(2,128)S(1)} %all_to_all.16), channel_id=1, replica_groups=mesh['yh'=4,'yl'=2,'x'=4,'core'=2,'z'=16] {'yl','x','core'}, dimensions={0} | all-to-all | bytes 32768 | tf_op jit(solution)/shard_map/all_to_all | solution.py:241
  129.8 0.9 shard_map.44
  (3 shorter events, 0.0 us)
Async XLA Ops:
  59.9 12.3 %collective-permute-start.1 = (bf16[256,1024]{1,0:T(8,128)(2,1)S(1)}, bf16[256,1024]{1,0:T(8,128)(2,1)S(1)}, u32[]{:S(2)}, u32[]{:S(2)}) collective-permute-start(bf16[256,1024]{1,0:T(8,128)(2,1)S(1)} %reshape.41.own), channel_id=1, source_target_pairs={{32,0},{48,16},{64,32},{80,48},{96,64},{112,80},{0,96},{16,112},{1... | collective-permute-start | bytes 1572872 | tf_op jit(solution)/shard_map/ppermute | solution.py:61
  64.3 11.8 %collective-permute-start = (bf16[256,1024]{1,0:T(8,128)(2,1)S(1)}, bf16[256,1024]{1,0:T(8,128)(2,1)S(1)}, u32[]{:S(2)}, u32[]{:S(2)}) collective-permute-start(bf16[256,1024]{1,0:T(8,128)(2,1)S(1)} %reshape.41.own), channel_id=1, source_target_pairs={{128,0},{144,16},{160,32},{176,48},{192,64},{208,80},{224,96},{240... | collective-permute-start | bytes 1572872 | tf_op jit(solution)/shard_map/ppermute | solution.py:61
  76.1 8.8 %collective-permute-start.2 = (bf16[512,1024]{1,0:T(8,128)(2,1)S(1)}, bf16[512,1024]{1,0:T(8,128)(2,1)S(1)}, u32[]{:S(2)}, u32[]{:S(2)}) collective-permute-start(bf16[512,1024]{1,0:T(8,128)(2,1)S(1)} %pad_maximum_fusion), channel_id=1, source_target_pairs={{16,0},{0,16},{48,32},{32,48},{80,64},{64,80},{112,96},{96,112},{1... | collective-permute-start | bytes 3145736 | tf_op jit(solution)/shard_map/ppermute | solution.py:61
  82.5 15.4 %collective-permute-start.3 = (bf16[256,1024]{1,0:T(8,128)(2,1)S(1)}, bf16[256,1024]{1,0:T(8,128)(2,1)S(1)}, u32[]{:S(2)}, u32[]{:S(2)}) collective-permute-start(bf16[256,1024]{1,0:T(8,128)(2,1)S(1)} %collective-permute-done.1.x1), channel_id=1, source_target_pairs={{32,0},{48,16},{64,32},{80,48},{96,64},{112,80},{0,96},{16,112},{1... | collective-permute-start | bytes 1572872 | tf_op jit(solution)/shard_map/ppermute | solution.py:61

commit v7 on v6

--- a/solution.py
+++ b/solution.py
@@ -11,29 +11,6 @@
 EPSILON = 1e-06
 NEVER = -2.0
 DEAD_MARK = 2.0
-
-
-def normalize_rows(values):
-    as_float = values.astype(jnp.float32)
-    return (
-        as_float * lax.rsqrt(jnp.sum(as_float * as_float, axis=1, keepdims=True) + EPSILON)
-    ).astype(jnp.bfloat16)
-
-
-def outgoing_rows(embeddings, assignment, owners, per_owner):
-    row_count = embeddings.shape[0]
-    slot_count = owners * per_owner
-    normed = normalize_rows(embeddings)
-    same = assignment[:, None] == assignment[None, :]
-    earlier = jnp.arange(row_count)[None, :] < jnp.arange(row_count)[:, None]
-    rank = jnp.sum((same & earlier).astype(jnp.int32), axis=1)
-    target = assignment * per_owner + rank
-    table = target[None, :] == jnp.arange(slot_count, dtype=jnp.int32)[:, None]
-    rows = jnp.dot(table.astype(jnp.bfloat16), normed, preferred_element_type=jnp.float32)
-    filled = jnp.any(table, axis=1)
-    first = jnp.arange(embeddings.shape[1], dtype=jnp.int32)[None, :] == 0
-    rows = jnp.where(first & ~filled[:, None], DEAD_MARK, rows)
-    return rows.astype(jnp.bfloat16)
 
 
 DEAD_BEST = -8.0
@@ -77,26 +54,42 @@
     return jnp.max(jnp.where(alive, scores, NEVER), axis=0, keepdims=True), total
 
 
-def own_kernel(own, out):
-    best, total = best_and_sum(own[...], own[...], True)
-    out[...] = jnp.concatenate([best, total] * 4, axis=0)
-
-
-def first_kernel(mine, own, y, swapped, x1, out):
-    slots = own.shape[0]
-    held = [own[...], swapped[:slots, :], y[...], swapped[slots:, :], x1[...]]
-    best, total = [mine[0:1, :]], [mine[1:2, :]]
-    pairs = [(0, 1), (0, 2), (0, 3), (0, 4), (1, 4), (2, 4), (3, 4), (4, 0), (4, 1), (4, 2), (4, 3)]
-    for p, q in pairs:
-        b, t = best_and_sum(held[q], held[p])
-        if p < len(best):
-            best[p], total[p] = jnp.maximum(best[p], b), total[p] + t
-        else:
-            best.append(b)
-            total.append(t)
-    first = (lax.broadcasted_iota(jnp.int32, (8, held[0].shape[1]), 1) == 0).astype(jnp.bfloat16)
-    marks = [dots(first, x)[0:1] for x in held]
-    out[...] = jnp.concatenate(best + total + marks + [marks[0]], axis=0)
+def send_kernel(embeddings, assignment, out):
+    values = embeddings[...].astype(jnp.float32)
+    scale = lax.rsqrt(jnp.sum(values * values, axis=1, keepdims=True) + EPSILON)
+    normed = (values * scale).astype(jnp.bfloat16)
+    rows, slots = values.shape[0], out.shape[0]
+    along = jnp.broadcast_to(assignment[...].astype(jnp.float32), (rows, rows))
+    earlier = iota((rows, rows), 0) < iota((rows, rows), 1)
+    rank = jnp.sum(jnp.where((along == along.T) & earlier, 1.0, 0.0), axis=0, keepdims=True)
+    slot = along[0:1] * (slots // 64) + rank
+    table = (slot == iota((slots, rows), 0).astype(jnp.float32)).astype(jnp.float32)
+    placed = jnp.dot(table.astype(jnp.bfloat16), normed, preferred_element_type=jnp.float32)
+    empty = jnp.sum(table, axis=1, keepdims=True) < 0.5
+    mark = empty & (iota(placed.shape, 1) == 0)
+    out[...] = jnp.where(mark, DEAD_MARK, placed).astype(jnp.bfloat16)
+
+
+def merge(old, new):
+    return (jnp.maximum(old[0], new[0]), old[1] + new[1])
+
+
+def near_kernel(own, y, x1, out):
+    a, b, d = own[...], y[...], x1[...]
+    stats = [
+        merge(merge(best_and_sum(a, a, True), best_and_sum(b, a)), best_and_sum(d, a)),
+        best_and_sum(d, b),
+        merge(best_and_sum(a, d), best_and_sum(b, d)),
+    ]
+    out[...] = jnp.concatenate([b for b, _ in stats] + [t for _, t in stats] + [stats[0][0]] * 2)
+
+
+def far_kernel(near, own, y, x2, out):
+    far = x2[...]
+    a, b = best_and_sum(far, own[...]), best_and_sum(far, y[...])
+    best = jnp.maximum(near[0:2, :], jnp.concatenate([a[0], b[0]]))
+    total = near[3:5, :] + jnp.concatenate([a[1], b[1]])
+    out[...] = jnp.concatenate([best, near[2:3, :], total, near[5:8, :]])
 
 
 def iota(shape, axis):
@@ -125,18 +118,23 @@
     return slot // 4 % 16
 
 
-def last_kernel(partial, own, y, swapped, x2, out):
-    best = partial[0:COUNT, :]
-    total = partial[COUNT : 2 * COUNT, :]
-    alive = partial[2 * COUNT : 3 * COUNT, :] < 1.5
+def last_kernel(seen, own, y, c, yc, x1, x2, out):
+    held = [own[...], c[...], y[...], yc[...], x1[...]]
     far = x2[...]
-    slots = own.shape[0]
-    targets = (own[...], swapped[:slots, :], y[...], swapped[slots:, :])
-    late = [best_and_sum(far, x) for x in targets]
-    best = jnp.concatenate(
-        [jnp.maximum(best[i : i + 1], late[i][0]) for i in range(4)] + [best[4:5]], axis=0
-    )
-    total = jnp.concatenate([total[i : i + 1] + late[i][1] for i in range(4)] + [total[4:5]], axis=0)
+    stats = [
+        merge(best_and_sum(held[1], held[0]), best_and_sum(held[3], held[0])),
+        merge(best_and_sum(held[4], held[1]), best_and_sum(far, held[1])),
+        (seen[1:2, :], seen[4:5, :]),
+        merge(best_and_sum(held[4], held[3]), best_and_sum(far, held[3])),
+        merge(best_and_sum(held[1], held[4]), best_and_sum(held[3], held[4])),
+    ]
+    stats[0] = merge(stats[0], (seen[0:1, :], seen[3:4, :]))
+    stats[4] = merge(stats[4], (seen[2:3, :], seen[5:6, :]))
+    best = jnp.concatenate([b for b, _ in stats])
+    total = jnp.concatenate([t for _, t in stats])
+    slots = best.shape[1]
+    first = (iota((8, own.shape[1]), 1) == 0).astype(jnp.bfloat16)
+    alive = jnp.concatenate([dots(first, x)[0:1] for x in held]) < 1.5
     square = jnp.sum(jnp.where(alive, total, 0.0))
     best = jnp.concatenate([jnp.where(alive[0:1], best[0:1], DEAD_BEST), best[1:]], axis=0)
     values = jnp.concatenate(
@@ -201,7 +199,14 @@
     width = embeddings.shape[1]
     per_owner = 2 * embeddings.shape[0] // owners
     slots = owners * per_owner
-    send = outgoing_rows(embeddings, assignment, owners, per_owner)
+    rows = embeddings.shape[0]
+    send = on_chip(
+        send_kernel,
+        jax.ShapeDtypeStruct((slots, width), jnp.bfloat16),
+        2 * slots * rows * width,
+        embeddings,
+        assignment.reshape(1, rows),
+    )
     own = lax.all_to_all(
         send.reshape(owners, per_owner, width),
         ("yh", "z"),
@@ -211,29 +216,24 @@
     ).reshape(slots, width)
     tile = 2 * slots * slots * width
     x1 = from_place(own, X1)
-    mine = on_chip(own_kernel, jax.ShapeDtypeStruct((8, slots), jnp.float32), tile, own)
     y = from_place(own, Y)
     x2 = from_place(x1, X1)
-    y, x1, mine = lax.optimization_barrier((y, x1, mine))
-    swapped = from_place(jnp.concatenate([own, y]), C)
-    partial = on_chip(
-        first_kernel,
-        jax.ShapeDtypeStruct((ROWS, slots), jnp.float32),
-        0,
-        mine,
-        own,
-        y,
-        swapped,
-        x1,
-    )
+    stats = jax.ShapeDtypeStruct((8, slots), jnp.float32)
+    near = on_chip(near_kernel, stats, 6 * tile, own, y, x1)
+    first, later, near = lax.optimization_barrier((own, y, near))
+    c = from_place(first, C)
+    yc = from_place(later, C)
+    seen = on_chip(far_kernel, stats, 2 * tile, near, own, y, x2)
     message = on_chip(
         last_kernel,
         jax.ShapeDtypeStruct((n * ROWS // GROUP, GROUP * CELLS), jnp.float32),
-        4 * tile,
-        partial,
+        8 * tile,
+        seen,
         own,
         y,
-        swapped,
+        c,
+        yc,
+        x1,
         x2,
     )
     message = message.reshape(n, ROWS // GROUP, GROUP * CELLS)

time: 131 us -> 125 us (0.954)
  waiting for transfers between devices: 19.7 us -> 6.97 us
  starting transfers between devices: 15.5 us -> 20.3 us
  blocking collectives: 85.1 us -> 88.5 us
  other arithmetic: 2.86 us -> 0 us
  local copies, waits for them, and re-layouts: 0.31 us -> 1.91 us
  matrix products: 1.33 us -> 0 us
    ppermute x4 -> x5, waiting for transfers between devices: 19.7 us -> 6.97 us  [from_place(): return lax.ppermute(value, ('yl', 'x', 'core'), pairs)]
    ppermute x4 -> x5, starting transfers between devices: 15.5 us -> 20.3 us  [from_place(): return lax.ppermute(value, ('yl', 'x', 'core'), pairs)]
    all_to_all x1, blocking collectives: 11.2 us -> 14.6 us  [local(): lax.all_to_all(message, home, split_axis=0, concat_axis=0, tiled=True)]
    reduce_sum x2 -> x0, other arithmetic: 1.99 us -> none  [the longest x1 1.09 us: normalize_rows(): jnp.sum(as_float * as_float, axis=1, keepdims=True) + EPSILON]
    unnamed x0 -> x4, local copies, waits for them, and re-layouts: none -> 1.6 us
    dot_general x1 -> x0, matrix products: 1.33 us -> none  [outgoing_rows(): jnp.dot(table.astype(jnp.bfloat16), normed, preferred_element_type=jnp.fl...]
    pallas_call x4 -> x5, Pallas kernels: 5.3 us -> 5.72 us  [on_chip(): pl.pallas_call(kernel, out_shape=out_shape, in_specs=[vmem] * len(operand...]
  transfers between devices with their start and end apart: 4 -> 5, of which waited for: 3 -> 2; matrix products, arithmetic and copies ran while one was open for 0% -> 0% of each run, Pallas kernels for 2% -> 1%
where the time goes in v7:
time: 125 us; the launch traced here: 124 us
  blocking collectives  88.5 us (71%)
  starting transfers between devices  20.3 us (16%)
  waiting for transfers between devices  6.97 us (6%)
  Pallas kernels  5.72 us (5%)
  local copies, waits for them, and re-layouts  1.91 us (2%)
    all_to_all x1, blocking collectives, local(): lax.all_to_all(send.reshape(owners, per_owner, width), ('yh', 'z'), split...  54.8 us
    ppermute x5, starting transfers between devices, from_place(): return lax.ppermute(value, ('yl', 'x', 'core'), pairs)  20.3 us
    all_to_all x1, blocking collectives, local(): lax.all_to_all(message, 'z', split_axis=0, concat_axis=0, tiled=True)  19.1 us
    all_to_all x1, blocking collectives, local(): lax.all_to_all(message, home, split_axis=0, concat_axis=0, tiled=True)  14.6 us
    ppermute x5, waiting for transfers between devices, from_place(): return lax.ppermute(value, ('yl', 'x', 'core'), pairs)  6.97 us
    pallas_call x5, Pallas kernels, on_chip(): pl.pallas_call(kernel, out_shape=out_shape, in_specs=[vmem] * len(operand...  5.72 us
  transfers between devices with their start and end apart: 5, of which 2 were waited for; matrix products, arithmetic and copies ran while one was open for 0% of the time, Pallas kernels for 1%

profile of v7, /device:TPU:1, one launch (start us, length us, event | category | flops | bytes accessed | tf_op | source)
XLA Modules:
  0.0 124.2 jit_solution(2504848142389588205)
XLA Ops:
  0.6 0.0 copy-start.1
  0.6 0.6 copy-done.1
  1.3 0.0 copy-start
  1.3 0.9 copy-done
  2.2 0.5 shard_map.41
  2.7 0.2 reshape.26
  2.9 54.8 %all_to_all.15 = bf16[64,4,1024]{2,1,0:T(4,128)(2,1)S(1)} all-to-all(bf16[64,4,1024]{2,1,0:T(4,128)(2,1)S(1)} %reshape.26), channel_id=1, replica_groups=mesh['yh'=4,'yl'=2,'x'=4,'core'=2,'z'=16] {'yh','z'}, dimensions={0} | all-to-all | bytes 1048576 | tf_op jit(solution)/shard_map/all_to_all | solution.py:210
  57.7 0.1 reshape.27.own
  57.8 4.4 %collective-permute-start.1 = (bf16[256,1024]{1,0:T(8,128)(2,1)S(1)}, bf16[256,1024]{1,0:T(8,128)(2,1)S(1)}, u32[]{:S(2)}, u32[]{:S(2)}) collective-permute-start(bf16[256,1024]{1,0:T(8,128)(2,1)S(1)} %reshape.27.own), channel_id=1, source_target_pairs={{32,0},{48,16},{64,32},{80,48},{96,64},{112,80},{0,96},{16,112},{1... | collective-permute-start | bytes 1572872 | tf_op jit(solution)/shard_map/ppermute | solution.py:38
  62.2 2.3 %collective-permute-start = (bf16[256,1024]{1,0:T(8,128)(2,1)S(1)}, bf16[256,1024]{1,0:T(8,128)(2,1)S(1)}, u32[]{:S(2)}, u32[]{:S(2)}) collective-permute-start(bf16[256,1024]{1,0:T(8,128)(2,1)S(1)} %reshape.27.own), channel_id=1, source_target_pairs={{128,0},{144,16},{160,32},{176,48},{192,64},{208,80},{224,96},{240... | collective-permute-start | bytes 1572872 | tf_op jit(solution)/shard_map/ppermute | solution.py:38
  64.5 5.6 %collective-permute-done.1.x1 = bf16[256,1024]{1,0:T(8,128)(2,1)S(1)} collective-permute-done((bf16[256,1024]{1,0:T(8,128)(2,1)S(1)}, bf16[256,1024]{1,0:T(8,128)(2,1)S(1)}, u32[]{:S(2)}, u32[]{:S(2)}) %collective-permute-start.1) | collective-permute-done | bytes 524320 | tf_op jit(solution)/shard_map/ppermute | solution.py:38
  70.1 5.3 %collective-permute-start.2 = (bf16[256,1024]{1,0:T(8,128)(2,1)S(1)}, bf16[256,1024]{1,0:T(8,128)(2,1)S(1)}, u32[]{:S(2)}, u32[]{:S(2)}) collective-permute-start(bf16[256,1024]{1,0:T(8,128)(2,1)S(1)} %collective-permute-done.1.x1), channel_id=1, source_target_pairs={{32,0},{48,16},{64,32},{80,48},{96,64},{112,80},{0,96},{16,112},{1... | collective-permute-start | bytes 1572872 | tf_op jit(solution)/shard_map/ppermute | solution.py:38
  75.4 0.0 collective-permute-done.y
  75.4 1.1 shard_map.42.near
  76.5 6.4 %collective-permute-start.3 = (bf16[256,1024]{1,0:T(8,128)(2,1)S(1)}, bf16[256,1024]{1,0:T(8,128)(2,1)S(1)}, u32[]{:S(2)}, u32[]{:S(2)}) collective-permute-start(bf16[256,1024]{1,0:T(8,128)(2,1)S(1)} %reshape.27.own), channel_id=1, source_target_pairs={{16,0},{0,16},{48,32},{32,48},{80,64},{64,80},{112,96},{96,112},{1... | collective-permute-start | bytes 1572872 | tf_op jit(solution)/shard_map/ppermute | solution.py:38
  82.9 1.9 %collective-permute-start.4 = (bf16[256,1024]{1,0:T(8,128)(2,1)S(1)}, bf16[256,1024]{1,0:T(8,128)(2,1)S(1)}, u32[]{:S(2)}, u32[]{:S(2)}) collective-permute-start(bf16[256,1024]{1,0:T(8,128)(2,1)S(1)} %collective-permute-done.y), channel_id=1, source_target_pairs={{16,0},{0,16},{48,32},{32,48},{80,64},{64,80},{112,96},{96,112},{1... | collective-permute-start | bytes 1572872 | tf_op jit(solution)/shard_map/ppermute | solution.py:38
  84.9 0.0 collective-permute-done.2.x2
  84.9 0.5 shard_map.43.seen
  85.4 0.0 collective-permute-done.3.c
  85.4 1.4 %collective-permute-done.4.yc = bf16[256,1024]{1,0:T(8,128)(2,1)S(1)} collective-permute-done((bf16[256,1024]{1,0:T(8,128)(2,1)S(1)}, bf16[256,1024]{1,0:T(8,128)(2,1)S(1)}, u32[]{:S(2)}, u32[]{:S(2)}) %collective-permute-start.4) | collective-permute-done | bytes 524320 | tf_op jit(solution)/shard_map/ppermute | solution.py:38
  86.7 2.8 %shard_map.44 = f32[32,128]{1,0:T(8,128)S(1)} custom-call(f32[8,256]{1,0:T(8,128)S(1)} %shard_map.43.seen, bf16[256,1024]{1,0:T(8,128)(2,1)S(1)} %reshape.27.own, bf16[256,1024]{1,0:T(8,128)(2,1)S(1)} %collective-permute-done.y, bf16[256,1024]{1,0:T(8,128)(2,1)S(1)} %collective-permute-done.3.c, bf16[256,1024]{1,0:T(8,128)(2,1)S(1)} %collective-permute-done.4.yc, ...), custom_call_target="tpu_custom_call" | custom-call | flops 1073741824 | bytes 3149824 | tf_op jit(solution)/shard_map/pallas_call | solution.py:181
  89.5 19.1 %all_to_all.16 = f32[16,2,128]{2,1,0:T(2,128)S(1)} all-to-all(f32[16,2,128]{2,1,0:T(2,128)S(1)} %bitcast.6), channel_id=1, replica_groups=mesh['yh'=4,'yl'=2,'x'=4,'core'=2,'z'=16] {'z'}, dimensions={0} | all-to-all | bytes 32768 | tf_op jit(solution)/shard_map/all_to_all | solution.py:240
  108.6 14.6 %all_to_all.17 = f32[16,2,128]{2,1,0:T(2,128)S(1)} all-to-all(f32[16,2,128]{2,1,0:T(2,128)S(1)} %all_to_all.16), channel_id=1, replica_groups=mesh['yh'=4,'yl'=2,'x'=4,'core'=2,'z'=16] {'yl','x','core'}, dimensions={0} | all-to-all | bytes 32768 | tf_op jit(solution)/shard_map/all_to_all | solution.py:241
  123.2 0.9 shard_map.45
Async XLA Ops:
  0.6 0.7 copy-start.1
  1.3 0.9 copy-start
  57.8 12.3 %collective-permute-start.1 = (bf16[256,1024]{1,0:T(8,128)(2,1)S(1)}, bf16[256,1024]{1,0:T(8,128)(2,1)S(1)}, u32[]{:S(2)}, u32[]{:S(2)}) collective-permute-start(bf16[256,1024]{1,0:T(8,128)(2,1)S(1)} %reshape.27.own), channel_id=1, source_target_pairs={{32,0},{48,16},{64,32},{80,48},{96,64},{112,80},{0,96},{16,112},{1... | collective-permute-start | bytes 1572872 | tf_op jit(solution)/shard_map/ppermute | solution.py:38
  62.2 13.2 %collective-permute-start = (bf16[256,1024]{1,0:T(8,128)(2,1)S(1)}, bf16[256,1024]{1,0:T(8,128)(2,1)S(1)}, u32[]{:S(2)}, u32[]{:S(2)}) collective-permute-start(bf16[256,1024]{1,0:T(8,128)(2,1)S(1)} %reshape.27.own), channel_id=1, source_target_pairs={{128,0},{144,16},{160,32},{176,48},{192,64},{208,80},{224,96},{240... | collective-permute-start | bytes 1572872 | tf_op jit(solution)/shard_map/ppermute | solution.py:38
  70.1 14.8 %collective-permute-start.2 = (bf16[256,1024]{1,0:T(8,128)(2,1)S(1)}, bf16[256,1024]{1,0:T(8,128)(2,1)S(1)}, u32[]{:S(2)}, u32[]{:S(2)}) collective-permute-start(bf16[256,1024]{1,0:T(8,128)(2,1)S(1)} %collective-permute-done.1.x1), channel_id=1, source_target_pairs={{32,0},{48,16},{64,32},{80,48},{96,64},{112,80},{0,96},{16,112},{1... | collective-permute-start | bytes 1572872 | tf_op jit(solution)/shard_map/ppermute | solution.py:38
  76.5 8.8 %collective-permute-start.3 = (bf16[256,1024]{1,0:T(8,128)(2,1)S(1)}, bf16[256,1024]{1,0:T(8,128)(2,1)S(1)}, u32[]{:S(2)}, u32[]{:S(2)}) collective-permute-start(bf16[256,1024]{1,0:T(8,128)(2,1)S(1)} %reshape.27.own), channel_id=1, source_target_pairs={{16,0},{0,16},{48,32},{32,48},{80,64},{64,80},{112,96},{96,112},{1... | collective-permute-start | bytes 1572872 | tf_op jit(solution)/shard_map/ppermute | solution.py:38
  82.9 3.8 %collective-permute-start.4 = (bf16[256,1024]{1,0:T(8,128)(2,1)S(1)}, bf16[256,1024]{1,0:T(8,128)(2,1)S(1)}, u32[]{:S(2)}, u32[]{:S(2)}) collective-permute-start(bf16[256,1024]{1,0:T(8,128)(2,1)S(1)} %collective-permute-done.y), channel_id=1, source_target_pairs={{16,0},{0,16},{48,32},{32,48},{80,64},{64,80},{112,96},{96,112},{1... | collective-permute-start | bytes 1572872 | tf_op jit(solution)/shard_map/ppermute | solution.py:38

commit v8 on v7

--- a/solution.py
+++ b/solution.py
@@ -150,8 +150,8 @@
     out[...] = jnp.sum(jnp.where(keep, wide, 0.0), axis=1)
 
 
-def finish_kernel(arrived, nearest, distance):
-    slots = nearest.shape[1]
+def finish_kernel(arrived, out):
+    slots = out.shape[1]
     places = arrived.shape[0] * GROUP // ROWS
     shape = (arrived.shape[0], GROUP, GROUP * CELLS)
     keep = iota(shape, 2) // CELLS == iota(shape, 1)
@@ -168,11 +168,12 @@
     result = jnp.sum(jnp.where(here, wide, 0.0), axis=0)
     alive = result[0:1] > NEVER - 1.0
     best = jnp.max(result[0:COUNT], axis=0, keepdims=True)
-    nearest[...] = jnp.where(alive, best, 0.0)
+    nearest = jnp.where(alive, best, 0.0)
     cosine = jnp.sum(result[COUNT : 2 * COUNT], axis=0, keepdims=True) * lax.rsqrt(
         result[2 * COUNT : 2 * COUNT + 1] + EPSILON
     )
-    distance[...] = jnp.where(alive, 1.0 - cosine, 0.0)
+    distance = jnp.where(alive, 1.0 - cosine, 0.0)
+    out[...] = jnp.concatenate([nearest, distance])
 
 
 def on_chip(kernel, out_shape, flops, *operands):
@@ -237,13 +238,16 @@
         x2,
     )
     message = message.reshape(n, ROWS // GROUP, GROUP * CELLS)
-    message = lax.all_to_all(message, "z", split_axis=0, concat_axis=0, tiled=True)
     message = lax.all_to_all(message, home, split_axis=0, concat_axis=0, tiled=True)
-    row = jax.ShapeDtypeStruct((1, slots), jnp.float32)
-    nearest, distance = on_chip(
-        finish_kernel, (row, row), 0, message.reshape(places * ROWS // GROUP, GROUP * CELLS)
-    )
-    return nearest.reshape(1, 1, slots), distance.reshape(1, 1, slots)
+    found = on_chip(
+        finish_kernel,
+        jax.ShapeDtypeStruct((2, slots), jnp.float32),
+        0,
+        message.reshape(places * ROWS // GROUP, GROUP * CELLS),
+    )
+    pairs = [(u * n + z, z * n + u) for u in range(places) for z in range(n)]
+    found = lax.ppermute(found, home + ("z",), pairs)
+    return found[0].reshape(1, 1, slots), found[1].reshape(1, 1, slots)
 
 
 def solution(mesh):

time: 125 us -> 119 us (0.952)
  the two profiles are of different devices: /device:TPU:1 before, /device:TPU:105 now
where the time goes in v8:
time: 119 us; the launch traced here: 118 us
  blocking collectives  67.9 us (57%)
  starting transfers between devices  22.8 us (19%)
  waiting for transfers between devices  19.1 us (16%)
  Pallas kernels  5.18 us (4%)
  local copies, waits for them, and re-layouts  2.48 us (2%)
    all_to_all x1, blocking collectives, local(): lax.all_to_all(send.reshape(owners, per_owner, width), ('yh', 'z'), split...  54.4 us
    ppermute x5, starting transfers between devices, from_place(): return lax.ppermute(value, ('yl', 'x', 'core'), pairs)  18.7 us
    all_to_all x1, blocking collectives, local(): lax.all_to_all(message, home, split_axis=0, concat_axis=0, tiled=True)  13.5 us
    ppermute x1, waiting for transfers between devices, local(): found = lax.ppermute(found, home + ('z',), pairs)  9.91 us
    ppermute x5, waiting for transfers between devices, from_place(): return lax.ppermute(value, ('yl', 'x', 'core'), pairs)  9.18 us
    pallas_call x5, Pallas kernels, on_chip(): pl.pallas_call(kernel, out_shape=out_shape, in_specs=[vmem] * len(operand...  5.18 us
    ppermute x1, starting transfers between devices, local(): found = lax.ppermute(found, home + ('z',), pairs)  4.02 us
  transfers between devices with their start and end apart: 6, of which 3 were waited for; matrix products, arithmetic and copies ran while one was open for 0% of the time, Pallas kernels for 1%

profile of v8, /device:TPU:105, one launch (start us, length us, event | category | flops | bytes accessed | tf_op | source)
XLA Modules:
  0.0 118.1 jit_solution(7638999425422835074)
XLA Ops:
  0.6 0.0 copy-start.1
  0.6 0.6 copy-done.1
  1.3 0.0 copy-start
  1.3 0.9 copy-done
  2.2 0.5 shard_map.41
  2.7 0.2 reshape.20
  2.9 54.4 %all_to_all.10 = bf16[64,4,1024]{2,1,0:T(4,128)(2,1)S(1)} all-to-all(bf16[64,4,1024]{2,1,0:T(4,128)(2,1)S(1)} %reshape.20), channel_id=1, replica_groups=mesh['yh'=4,'yl'=2,'x'=4,'core'=2,'z'=16] {'yh','z'}, dimensions={0} | all-to-all | bytes 1048576 | tf_op jit(solution)/shard_map/all_to_all | solution.py:211
  57.3 0.1 reshape.21.own
  57.4 4.4 %collective-permute-start.1 = (bf16[256,1024]{1,0:T(8,128)(2,1)S(1)}, bf16[256,1024]{1,0:T(8,128)(2,1)S(1)}, u32[]{:S(2)}, u32[]{:S(2)}) collective-permute-start(bf16[256,1024]{1,0:T(8,128)(2,1)S(1)} %reshape.21.own), channel_id=1, source_target_pairs={{32,0},{48,16},{64,32},{80,48},{96,64},{112,80},{0,96},{16,112},{1... | collective-permute-start | bytes 1572872 | tf_op jit(solution)/shard_map/ppermute | solution.py:38
  61.8 3.0 %collective-permute-start = (bf16[256,1024]{1,0:T(8,128)(2,1)S(1)}, bf16[256,1024]{1,0:T(8,128)(2,1)S(1)}, u32[]{:S(2)}, u32[]{:S(2)}) collective-permute-start(bf16[256,1024]{1,0:T(8,128)(2,1)S(1)} %reshape.21.own), channel_id=1, source_target_pairs={{128,0},{144,16},{160,32},{176,48},{192,64},{208,80},{224,96},{240... | collective-permute-start | bytes 1572872 | tf_op jit(solution)/shard_map/ppermute | solution.py:38
  64.8 7.2 %collective-permute-done.1.x1 = bf16[256,1024]{1,0:T(8,128)(2,1)S(1)} collective-permute-done((bf16[256,1024]{1,0:T(8,128)(2,1)S(1)}, bf16[256,1024]{1,0:T(8,128)(2,1)S(1)}, u32[]{:S(2)}, u32[]{:S(2)}) %collective-permute-start.1) | collective-permute-done | bytes 524320 | tf_op jit(solution)/shard_map/ppermute | solution.py:38
  72.0 5.3 %collective-permute-start.2 = (bf16[256,1024]{1,0:T(8,128)(2,1)S(1)}, bf16[256,1024]{1,0:T(8,128)(2,1)S(1)}, u32[]{:S(2)}, u32[]{:S(2)}) collective-permute-start(bf16[256,1024]{1,0:T(8,128)(2,1)S(1)} %collective-permute-done.1.x1), channel_id=1, source_target_pairs={{32,0},{48,16},{64,32},{80,48},{96,64},{112,80},{0,96},{16,112},{1... | collective-permute-start | bytes 1572872 | tf_op jit(solution)/shard_map/ppermute | solution.py:38
  77.3 0.0 collective-permute-done.y
  77.3 1.1 shard_map.42.near
  78.4 4.2 %collective-permute-start.3 = (bf16[256,1024]{1,0:T(8,128)(2,1)S(1)}, bf16[256,1024]{1,0:T(8,128)(2,1)S(1)}, u32[]{:S(2)}, u32[]{:S(2)}) collective-permute-start(bf16[256,1024]{1,0:T(8,128)(2,1)S(1)} %reshape.21.own), channel_id=1, source_target_pairs={{16,0},{0,16},{48,32},{32,48},{80,64},{64,80},{112,96},{96,112},{1... | collective-permute-start | bytes 1572872 | tf_op jit(solution)/shard_map/ppermute | solution.py:38
  82.6 1.9 %collective-permute-start.4 = (bf16[256,1024]{1,0:T(8,128)(2,1)S(1)}, bf16[256,1024]{1,0:T(8,128)(2,1)S(1)}, u32[]{:S(2)}, u32[]{:S(2)}) collective-permute-start(bf16[256,1024]{1,0:T(8,128)(2,1)S(1)} %collective-permute-done.y), channel_id=1, source_target_pairs={{16,0},{0,16},{48,32},{32,48},{80,64},{64,80},{112,96},{96,112},{1... | collective-permute-start | bytes 1572872 | tf_op jit(solution)/shard_map/ppermute | solution.py:38
  84.5 2.0 %collective-permute-done.2.x2 = bf16[256,1024]{1,0:T(8,128)(2,1)S(1)} collective-permute-done((bf16[256,1024]{1,0:T(8,128)(2,1)S(1)}, bf16[256,1024]{1,0:T(8,128)(2,1)S(1)}, u32[]{:S(2)}, u32[]{:S(2)}) %collective-permute-start.2) | collective-permute-done | bytes 524320 | tf_op jit(solution)/shard_map/ppermute | solution.py:38
  86.5 0.5 shard_map.43.seen
  87.0 0.0 collective-permute-done.3.c
  87.0 0.0 collective-permute-done.4.yc
  87.0 2.8 %shard_map.44 = f32[32,128]{1,0:T(8,128)S(1)} custom-call(f32[8,256]{1,0:T(8,128)S(1)} %shard_map.43.seen, bf16[256,1024]{1,0:T(8,128)(2,1)S(1)} %reshape.21.own, bf16[256,1024]{1,0:T(8,128)(2,1)S(1)} %collective-permute-done.y, bf16[256,1024]{1,0:T(8,128)(2,1)S(1)} %collective-permute-done.3.c, bf16[256,1024]{1,0:T(8,128)(2,1)S(1)} %collective-permute-done.4.yc, ...), custom_call_target="tpu_custom_call" | custom-call | flops 1073741824 | bytes 3149824 | tf_op jit(solution)/shard_map/pallas_call | solution.py:182
  89.8 13.5 %all_to_all.11 = f32[16,2,128]{2,1,0:T(2,128)S(1)} all-to-all(f32[16,2,128]{2,1,0:T(2,128)S(1)} %bitcast.8), channel_id=1, replica_groups=mesh['yh'=4,'yl'=2,'x'=4,'core'=2,'z'=16] {'yl','x','core'}, dimensions={0} | all-to-all | bytes 32768 | tf_op jit(solution)/shard_map/all_to_all | solution.py:241
  103.2 0.4 shard_map.45
  103.6 4.0 %collective-permute-start.5 = (f32[2,256]{1,0:T(2,128)S(1)}, f32[2,256]{1,0:T(2,128)S(1)}, u32[]{:S(2)}, u32[]{:S(2)}) collective-permute-start(f32[2,256]{1,0:T(2,128)S(1)} %shard_map.45), channel_id=1, source_target_pairs={{0,0},{1,16},{2,32},{3,48},{4,64},{5,80},{6,96},{7,112},{8,128},{9... | collective-permute-start | bytes 6152 | tf_op jit(solution)/shard_map/ppermute | solution.py:249
  107.7 9.9 %collective-permute-done.5 = f32[2,256]{1,0:T(2,128)S(1)} collective-permute-done((f32[2,256]{1,0:T(2,128)S(1)}, f32[2,256]{1,0:T(2,128)S(1)}, u32[]{:S(2)}, u32[]{:S(2)}) %collective-permute-start.5) | collective-permute-done | bytes 2080 | tf_op jit(solution)/shard_map/ppermute | solution.py:249
  117.6 0.6 slice_bitcast_fusion
Async XLA Ops:
  0.6 0.7 copy-start.1
  1.3 0.9 copy-start
  57.4 14.5 %collective-permute-start.1 = (bf16[256,1024]{1,0:T(8,128)(2,1)S(1)}, bf16[256,1024]{1,0:T(8,128)(2,1)S(1)}, u32[]{:S(2)}, u32[]{:S(2)}) collective-permute-start(bf16[256,1024]{1,0:T(8,128)(2,1)S(1)} %reshape.21.own), channel_id=1, source_target_pairs={{32,0},{48,16},{64,32},{80,48},{96,64},{112,80},{0,96},{16,112},{1... | collective-permute-start | bytes 1572872 | tf_op jit(solution)/shard_map/ppermute | solution.py:38
  61.8 15.5 %collective-permute-start = (bf16[256,1024]{1,0:T(8,128)(2,1)S(1)}, bf16[256,1024]{1,0:T(8,128)(2,1)S(1)}, u32[]{:S(2)}, u32[]{:S(2)}) collective-permute-start(bf16[256,1024]{1,0:T(8,128)(2,1)S(1)} %reshape.21.own), channel_id=1, source_target_pairs={{128,0},{144,16},{160,32},{176,48},{192,64},{208,80},{224,96},{240... | collective-permute-start | bytes 1572872 | tf_op jit(solution)/shard_map/ppermute | solution.py:38
  72.0 14.5 %collective-permute-start.2 = (bf16[256,1024]{1,0:T(8,128)(2,1)S(1)}, bf16[256,1024]{1,0:T(8,128)(2,1)S(1)}, u32[]{:S(2)}, u32[]{:S(2)}) collective-permute-start(bf16[256,1024]{1,0:T(8,128)(2,1)S(1)} %collective-permute-done.1.x1), channel_id=1, source_target_pairs={{32,0},{48,16},{64,32},{80,48},{96,64},{112,80},{0,96},{16,112},{1... | collective-permute-start | bytes 1572872 | tf_op jit(solution)/shard_map/ppermute | solution.py:38
  78.4 8.6 %collective-permute-start.3 = (bf16[256,1024]{1,0:T(8,128)(2,1)S(1)}, bf16[256,1024]{1,0:T(8,128)(2,1)S(1)}, u32[]{:S(2)}, u32[]{:S(2)}) collective-permute-start(bf16[256,1024]{1,0:T(8,128)(2,1)S(1)} %reshape.21.own), channel_id=1, source_target_pairs={{16,0},{0,16},{48,32},{32,48},{80,64},{64,80},{112,96},{96,112},{1... | collective-permute-start | bytes 1572872 | tf_op jit(solution)/shard_map/ppermute | solution.py:38
  82.6 4.4 %collective-permute-start.4 = (bf16[256,1024]{1,0:T(8,128)(2,1)S(1)}, bf16[256,1024]{1,0:T(8,128)(2,1)S(1)}, u32[]{:S(2)}, u32[]{:S(2)}) collective-permute-start(bf16[256,1024]{1,0:T(8,128)(2,1)S(1)} %collective-permute-done.y), channel_id=1, source_target_pairs={{16,0},{0,16},{48,32},{32,48},{80,64},{64,80},{112,96},{96,112},{1... | collective-permute-start | bytes 1572872 | tf_op jit(solution)/shard_map/ppermute | solution.py:38
  103.6 13.9 %collective-permute-start.5 = (f32[2,256]{1,0:T(2,128)S(1)}, f32[2,256]{1,0:T(2,128)S(1)}, u32[]{:S(2)}, u32[]{:S(2)}) collective-permute-start(f32[2,256]{1,0:T(2,128)S(1)} %shard_map.45), channel_id=1, source_target_pairs={{0,0},{1,16},{2,32},{3,48},{4,64},{5,80},{6,96},{7,112},{8,128},{9... | collective-permute-start | bytes 6152 | tf_op jit(solution)/shard_map/ppermute | solution.py:249

commit v9 on v8

--- a/solution.py
+++ b/solution.py
@@ -59,11 +59,12 @@
     scale = lax.rsqrt(jnp.sum(values * values, axis=1, keepdims=True) + EPSILON)
     normed = (values * scale).astype(jnp.bfloat16)
     rows, slots = values.shape[0], out.shape[0]
-    along = jnp.broadcast_to(assignment[...].astype(jnp.float32), (rows, rows))
+    cluster = assignment[...]
+    along = jnp.broadcast_to(cluster.astype(jnp.float32), (rows, rows))
     earlier = iota((rows, rows), 0) < iota((rows, rows), 1)
     rank = jnp.sum(jnp.where((along == along.T) & earlier, 1.0, 0.0), axis=0, keepdims=True)
-    slot = along[0:1] * (slots // 64) + rank
-    table = (slot == iota((slots, rows), 0).astype(jnp.float32)).astype(jnp.float32)
+    slot = (cluster % 16 * 4 + cluster // 16) * (slots // 64) + rank.astype(jnp.int32)
+    table = (slot == iota((slots, rows), 0)).astype(jnp.float32)
     placed = jnp.dot(table.astype(jnp.bfloat16), normed, preferred_element_type=jnp.float32)
     empty = jnp.sum(table, axis=1, keepdims=True) < 0.5
     mark = empty & (iota(placed.shape, 1) == 0)
@@ -74,22 +75,23 @@
     return (jnp.maximum(old[0], new[0]), old[1] + new[1])
 
 
-def near_kernel(own, y, x1, out):
-    a, b, d = own[...], y[...], x1[...]
+def near_kernel(own, c, y, x1, out):
+    a, b, d, e = own[...], c[...], y[...], x1[...]
     stats = [
-        merge(merge(best_and_sum(a, a, True), best_and_sum(b, a)), best_and_sum(d, a)),
-        best_and_sum(d, b),
-        merge(best_and_sum(a, d), best_and_sum(b, d)),
+        merge(merge(best_and_sum(a, a, True), best_and_sum(b, a)), merge(best_and_sum(d, a), best_and_sum(e, a))),
+        best_and_sum(e, b),
+        best_and_sum(e, d),
+        merge(merge(best_and_sum(a, e), best_and_sum(b, e)), best_and_sum(d, e)),
     ]
-    out[...] = jnp.concatenate([b for b, _ in stats] + [t for _, t in stats] + [stats[0][0]] * 2)
-
-
-def far_kernel(near, own, y, x2, out):
+    out[...] = jnp.concatenate([b for b, _ in stats] + [t for _, t in stats])
+
+
+def far_kernel(near, own, c, y, x2, out):
     far = x2[...]
-    a, b = best_and_sum(far, own[...]), best_and_sum(far, y[...])
-    best = jnp.maximum(near[0:2, :], jnp.concatenate([a[0], b[0]]))
-    total = near[3:5, :] + jnp.concatenate([a[1], b[1]])
-    out[...] = jnp.concatenate([best, near[2:3, :], total, near[5:8, :]])
+    late = [best_and_sum(far, x[...]) for x in (own, c, y)]
+    best = jnp.maximum(near[0:3, :], jnp.concatenate([b for b, _ in late]))
+    total = near[4:7, :] + jnp.concatenate([t for _, t in late])
+    out[...] = jnp.concatenate([best, near[3:4, :], total, near[7:8, :]])
 
 
 def iota(shape, axis):
@@ -110,26 +112,24 @@
 CELLS = 16
 
 
-def cell_of(slot):
+def owner_cell(slot):
     return slot // 64 * 4 + slot % 4
 
 
-def place_of(slot):
+def owner_place(slot):
     return slot // 4 % 16
 
 
-def last_kernel(seen, own, y, c, yc, x1, x2, out):
+def last_kernel(seen, own, c, y, yc, x1, x2, out):
     held = [own[...], c[...], y[...], yc[...], x1[...]]
     far = x2[...]
     stats = [
-        merge(best_and_sum(held[1], held[0]), best_and_sum(held[3], held[0])),
-        merge(best_and_sum(held[4], held[1]), best_and_sum(far, held[1])),
-        (seen[1:2, :], seen[4:5, :]),
+        merge(best_and_sum(held[3], held[0]), (seen[0:1, :], seen[4:5, :])),
+        (seen[1:2, :], seen[5:6, :]),
+        (seen[2:3, :], seen[6:7, :]),
         merge(best_and_sum(held[4], held[3]), best_and_sum(far, held[3])),
-        merge(best_and_sum(held[1], held[4]), best_and_sum(held[3], held[4])),
+        merge(best_and_sum(held[3], held[4]), (seen[3:4, :], seen[7:8, :])),
     ]
-    stats[0] = merge(stats[0], (seen[0:1, :], seen[3:4, :]))
-    stats[4] = merge(stats[4], (seen[2:3, :], seen[5:6, :]))
     best = jnp.concatenate([b for b, _ in stats])
     total = jnp.concatenate([t for _, t in stats])
     slots = best.shape[1]
@@ -142,9 +142,9 @@
     )
     n = out.shape[0] * GROUP // ROWS
     shape = (n, ROWS, slots)
-    chosen = jnp.where(place_of(iota(shape, 2)) == iota(shape, 0), values[None], 0.0)
+    chosen = jnp.where(iota(shape, 2) // CELLS == iota(shape, 0), values[None], 0.0)
     shape = (slots, GROUP * CELLS)
-    spread = (cell_of(iota(shape, 0)) == iota(shape, 1) % CELLS).astype(jnp.float32)
+    spread = (iota(shape, 0) % CELLS == iota(shape, 1) % CELLS).astype(jnp.float32)
     wide = exact_dot(chosen.reshape(n * ROWS, slots), spread).reshape(-1, GROUP, GROUP * CELLS)
     keep = iota(wide.shape, 2) // CELLS == iota(wide.shape, 1)
     out[...] = jnp.sum(jnp.where(keep, wide, 0.0), axis=1)
@@ -157,14 +157,14 @@
     keep = iota(shape, 2) // CELLS == iota(shape, 1)
     rows = jnp.where(keep, arrived[...][:, None, :], 0.0).reshape(places * ROWS, GROUP * CELLS)
     shape = (GROUP * CELLS, slots)
-    spread = (cell_of(iota(shape, 1)) == iota(shape, 0) % CELLS).astype(jnp.float32)
+    spread = (owner_cell(iota(shape, 1)) == iota(shape, 0) % CELLS).astype(jnp.float32)
     wide = exact_dot(rows, spread).reshape(places, ROWS, slots)
     u, v, to = (iota(wide.shape, axis) for axis in range(3))
     target = v % COUNT
     core = (u ^ jnp.where((target == 1) | (target == 3), 1, 0)) & 1
     low = (u ^ jnp.where((target == 2) | (target == 3), 8, 0)) & 8
     across = (u + jnp.where(target == 4, 2, 0)) & 6
-    here = (core + low + across == place_of(to)) | (v >= 2 * COUNT)
+    here = (core + low + across == owner_place(to)) | (v >= 2 * COUNT)
     result = jnp.sum(jnp.where(here, wide, 0.0), axis=0)
     alive = result[0:1] > NEVER - 1.0
     best = jnp.max(result[0:COUNT], axis=0, keepdims=True)
@@ -210,7 +210,7 @@
     )
     own = lax.all_to_all(
         send.reshape(owners, per_owner, width),
-        ("yh", "z"),
+        ("z", "yh"),
         split_axis=0,
         concat_axis=0,
         tiled=True,
@@ -220,19 +220,19 @@
     y = from_place(own, Y)
     x2 = from_place(x1, X1)
     stats = jax.ShapeDtypeStruct((8, slots), jnp.float32)
-    near = on_chip(near_kernel, stats, 6 * tile, own, y, x1)
-    first, later, near = lax.optimization_barrier((own, y, near))
-    c = from_place(first, C)
+    c = from_place(own, C)
+    near = on_chip(near_kernel, stats, 9 * tile, own, c, y, x1)
+    later, near = lax.optimization_barrier((y, near))
     yc = from_place(later, C)
-    seen = on_chip(far_kernel, stats, 2 * tile, near, own, y, x2)
+    seen = on_chip(far_kernel, stats, 3 * tile, near, own, c, y, x2)
     message = on_chip(
         last_kernel,
         jax.ShapeDtypeStruct((n * ROWS // GROUP, GROUP * CELLS), jnp.float32),
-        8 * tile,
+        4 * tile,
         seen,
         own,
+        c,
         y,
-        c,
         yc,
         x1,
         x2,

time: 119 us -> 120 us (level)
  the two profiles are of different devices: /device:TPU:105 before, /device:TPU:56 now
where the time goes in v9:
time: 120 us
  blocking collectives  67.9 us (57%)
  waiting for transfers between devices  22.5 us (19%)
  starting transfers between devices  21.2 us (18%)
  Pallas kernels  5.2 us (4%)
  local copies, waits for them, and re-layouts  2.48 us (2%)
    all_to_all x1, blocking collectives, local(): lax.all_to_all(send.reshape(owners, per_owner, width), ('z', 'yh'), split...  57 us
    ppermute x5, starting transfers between devices, from_place(): return lax.ppermute(value, ('yl', 'x', 'core'), pairs)  17.4 us
    ppermute x1, waiting for transfers between devices, local(): found = lax.ppermute(found, home + ('z',), pairs)  11.3 us
    ppermute x5, waiting for transfers between devices, from_place(): return lax.ppermute(value, ('yl', 'x', 'core'), pairs)  11.3 us
    all_to_all x1, blocking collectives, local(): lax.all_to_all(message, home, split_axis=0, concat_axis=0, tiled=True)  11 us
    pallas_call x5, Pallas kernels, on_chip(): pl.pallas_call(kernel, out_shape=out_shape, in_specs=[vmem] * len(operand...  5.2 us
    ppermute x1, starting transfers between devices, local(): found = lax.ppermute(found, home + ('z',), pairs)  3.83 us
  transfers between devices with their start and end apart: 6, of which 4 were waited for; matrix products, arithmetic and copies ran while one was open for 0% of the time, Pallas kernels for 2%

profile of v9, /device:TPU:56, one launch (start us, length us, event | category | flops | bytes accessed | tf_op | source)
XLA Modules:
  0.0 120.1 jit_solution(14798308747330612208)
XLA Ops:
  0.6 0.0 copy-start.1
  0.6 0.6 copy-done.1
  1.3 0.0 copy-start
  1.3 0.9 copy-done
  2.2 0.5 shard_map.41
  2.7 0.2 reshape.20
  2.9 57.0 %all_to_all.10 = bf16[64,4,1024]{2,1,0:T(4,128)(2,1)S(1)} all-to-all(bf16[64,4,1024]{2,1,0:T(4,128)(2,1)S(1)} %reshape.20), channel_id=1, replica_groups=mesh['yh'=4,'yl'=2,'x'=4,'core'=2,'z'=16] {'z','yh'}, dimensions={0} | all-to-all | bytes 1048576 | tf_op jit(solution)/shard_map/all_to_all | solution.py:211
  59.9 0.1 reshape.21.own
  60.0 4.7 %collective-permute-start.2 = (bf16[256,1024]{1,0:T(8,128)(2,1)S(1)}, bf16[256,1024]{1,0:T(8,128)(2,1)S(1)}, u32[]{:S(2)}, u32[]{:S(2)}) collective-permute-start(bf16[256,1024]{1,0:T(8,128)(2,1)S(1)} %reshape.21.own), channel_id=1, source_target_pairs={{32,0},{48,16},{64,32},{80,48},{96,64},{112,80},{0,96},{16,112},{1... | collective-permute-start | bytes 1572872 | tf_op jit(solution)/shard_map/ppermute | solution.py:38
  64.7 1.9 %collective-permute-start.1 = (bf16[256,1024]{1,0:T(8,128)(2,1)S(1)}, bf16[256,1024]{1,0:T(8,128)(2,1)S(1)}, u32[]{:S(2)}, u32[]{:S(2)}) collective-permute-start(bf16[256,1024]{1,0:T(8,128)(2,1)S(1)} %reshape.21.own), channel_id=1, source_target_pairs={{16,0},{0,16},{48,32},{32,48},{80,64},{64,80},{112,96},{96,112},{1... | collective-permute-start | bytes 1572872 | tf_op jit(solution)/shard_map/ppermute | solution.py:38
  66.6 3.3 %collective-permute-start = (bf16[256,1024]{1,0:T(8,128)(2,1)S(1)}, bf16[256,1024]{1,0:T(8,128)(2,1)S(1)}, u32[]{:S(2)}, u32[]{:S(2)}) collective-permute-start(bf16[256,1024]{1,0:T(8,128)(2,1)S(1)} %reshape.21.own), channel_id=1, source_target_pairs={{128,0},{144,16},{160,32},{176,48},{192,64},{208,80},{224,96},{240... | collective-permute-start | bytes 1572872 | tf_op jit(solution)/shard_map/ppermute | solution.py:38
  69.9 5.2 %collective-permute-done.2.x1 = bf16[256,1024]{1,0:T(8,128)(2,1)S(1)} collective-permute-done((bf16[256,1024]{1,0:T(8,128)(2,1)S(1)}, bf16[256,1024]{1,0:T(8,128)(2,1)S(1)}, u32[]{:S(2)}, u32[]{:S(2)}) %collective-permute-start.2) | collective-permute-done | bytes 524320 | tf_op jit(solution)/shard_map/ppermute | solution.py:38
  75.1 5.6 %collective-permute-start.3 = (bf16[256,1024]{1,0:T(8,128)(2,1)S(1)}, bf16[256,1024]{1,0:T(8,128)(2,1)S(1)}, u32[]{:S(2)}, u32[]{:S(2)}) collective-permute-start(bf16[256,1024]{1,0:T(8,128)(2,1)S(1)} %collective-permute-done.2.x1), channel_id=1, source_target_pairs={{32,0},{48,16},{64,32},{80,48},{96,64},{112,80},{0,96},{16,112},{1... | collective-permute-start | bytes 1572872 | tf_op jit(solution)/shard_map/ppermute | solution.py:38
  80.7 0.0 collective-permute-done.1.c
  80.7 2.1 %collective-permute-done.y = bf16[256,1024]{1,0:T(8,128)(2,1)S(1)} collective-permute-done((bf16[256,1024]{1,0:T(8,128)(2,1)S(1)}, bf16[256,1024]{1,0:T(8,128)(2,1)S(1)}, u32[]{:S(2)}, u32[]{:S(2)}) %collective-permute-start) | collective-permute-done | bytes 524320 | tf_op jit(solution)/shard_map/ppermute | solution.py:38
  82.8 1.5 %shard_map.42.near = f32[8,256]{1,0:T(8,128)S(1)} custom-call(bf16[256,1024]{1,0:T(8,128)(2,1)S(1)} %reshape.21.own, bf16[256,1024]{1,0:T(8,128)(2,1)S(1)} %collective-permute-done.1.c, bf16[256,1024]{1,0:T(8,128)(2,1)S(1)} %collective-permute-done.y, bf16[256,1024]{1,0:T(8,128)(2,1)S(1)} %collective-permute-done.2.x1), custom_call_target="tpu_custom_call" | custom-call | flops 1207959552 | bytes 2097152 | tf_op jit(solution)/shard_map/pallas_call | solution.py:182
  84.4 1.9 %collective-permute-start.4 = (bf16[256,1024]{1,0:T(8,128)(2,1)S(1)}, bf16[256,1024]{1,0:T(8,128)(2,1)S(1)}, u32[]{:S(2)}, u32[]{:S(2)}) collective-permute-start(bf16[256,1024]{1,0:T(8,128)(2,1)S(1)} %collective-permute-done.y), channel_id=1, source_target_pairs={{16,0},{0,16},{48,32},{32,48},{80,64},{64,80},{112,96},{96,112},{1... | collective-permute-start | bytes 1572872 | tf_op jit(solution)/shard_map/ppermute | solution.py:38
  86.3 3.9 %collective-permute-done.3.x2 = bf16[256,1024]{1,0:T(8,128)(2,1)S(1)} collective-permute-done((bf16[256,1024]{1,0:T(8,128)(2,1)S(1)}, bf16[256,1024]{1,0:T(8,128)(2,1)S(1)}, u32[]{:S(2)}, u32[]{:S(2)}) %collective-permute-start.3) | collective-permute-done | bytes 524320 | tf_op jit(solution)/shard_map/ppermute | solution.py:38
  90.2 0.6 shard_map.43.seen
  90.8 0.0 collective-permute-done.4.yc
  90.9 2.2 %shard_map.44 = f32[32,128]{1,0:T(8,128)S(1)} custom-call(f32[8,256]{1,0:T(8,128)S(1)} %shard_map.43.seen, bf16[256,1024]{1,0:T(8,128)(2,1)S(1)} %reshape.21.own, bf16[256,1024]{1,0:T(8,128)(2,1)S(1)} %collective-permute-done.1.c, bf16[256,1024]{1,0:T(8,128)(2,1)S(1)} %collective-permute-done.y, bf16[256,1024]{1,0:T(8,128)(2,1)S(1)} %collective-permute-done.4.yc, ...), custom_call_target="tpu_custom_call" | custom-call | flops 536870912 | bytes 3149824 | tf_op jit(solution)/shard_map/pallas_call | solution.py:182
  93.1 11.0 %all_to_all.11 = f32[16,2,128]{2,1,0:T(2,128)S(1)} all-to-all(f32[16,2,128]{2,1,0:T(2,128)S(1)} %bitcast.7), channel_id=1, replica_groups=mesh['yh'=4,'yl'=2,'x'=4,'core'=2,'z'=16] {'yl','x','core'}, dimensions={0} | all-to-all | bytes 32768 | tf_op jit(solution)/shard_map/all_to_all | solution.py:241
  104.0 0.4 shard_map.45
  104.4 3.8 %collective-permute-start.5 = (f32[2,256]{1,0:T(2,128)S(1)}, f32[2,256]{1,0:T(2,128)S(1)}, u32[]{:S(2)}, u32[]{:S(2)}) collective-permute-start(f32[2,256]{1,0:T(2,128)S(1)} %shard_map.45), channel_id=1, source_target_pairs={{0,0},{1,16},{2,32},{3,48},{4,64},{5,80},{6,96},{7,112},{8,128},{9... | collective-permute-start | bytes 6152 | tf_op jit(solution)/shard_map/ppermute | solution.py:249
  108.2 11.3 %collective-permute-done.5 = f32[2,256]{1,0:T(2,128)S(1)} collective-permute-done((f32[2,256]{1,0:T(2,128)S(1)}, f32[2,256]{1,0:T(2,128)S(1)}, u32[]{:S(2)}, u32[]{:S(2)}) %collective-permute-start.5) | collective-permute-done | bytes 2080 | tf_op jit(solution)/shard_map/ppermute | solution.py:249
  119.5 0.6 slice_bitcast_fusion
Async XLA Ops:
  0.6 0.7 copy-start.1
  1.3 0.9 copy-start
  60.0 15.1 %collective-permute-start.2 = (bf16[256,1024]{1,0:T(8,128)(2,1)S(1)}, bf16[256,1024]{1,0:T(8,128)(2,1)S(1)}, u32[]{:S(2)}, u32[]{:S(2)}) collective-permute-start(bf16[256,1024]{1,0:T(8,128)(2,1)S(1)} %reshape.21.own), channel_id=1, source_target_pairs={{32,0},{48,16},{64,32},{80,48},{96,64},{112,80},{0,96},{16,112},{1... | collective-permute-start | bytes 1572872 | tf_op jit(solution)/shard_map/ppermute | solution.py:38
  64.7 16.0 %collective-permute-start.1 = (bf16[256,1024]{1,0:T(8,128)(2,1)S(1)}, bf16[256,1024]{1,0:T(8,128)(2,1)S(1)}, u32[]{:S(2)}, u32[]{:S(2)}) collective-permute-start(bf16[256,1024]{1,0:T(8,128)(2,1)S(1)} %reshape.21.own), channel_id=1, source_target_pairs={{16,0},{0,16},{48,32},{32,48},{80,64},{64,80},{112,96},{96,112},{1... | collective-permute-start | bytes 1572872 | tf_op jit(solution)/shard_map/ppermute | solution.py:38
  66.6 16.2 %collective-permute-start = (bf16[256,1024]{1,0:T(8,128)(2,1)S(1)}, bf16[256,1024]{1,0:T(8,128)(2,1)S(1)}, u32[]{:S(2)}, u32[]{:S(2)}) collective-permute-start(bf16[256,1024]{1,0:T(8,128)(2,1)S(1)} %reshape.21.own), channel_id=1, source_target_pairs={{128,0},{144,16},{160,32},{176,48},{192,64},{208,80},{224,96},{240... | collective-permute-start | bytes 1572872 | tf_op jit(solution)/shard_map/ppermute | solution.py:38
  75.1 15.1 %collective-permute-start.3 = (bf16[256,1024]{1,0:T(8,128)(2,1)S(1)}, bf16[256,1024]{1,0:T(8,128)(2,1)S(1)}, u32[]{:S(2)}, u32[]{:S(2)}) collective-permute-start(bf16[256,1024]{1,0:T(8,128)(2,1)S(1)} %collective-permute-done.2.x1), channel_id=1, source_target_pairs={{32,0},{48,16},{64,32},{80,48},{96,64},{112,80},{0,96},{16,112},{1... | collective-permute-start | bytes 1572872 | tf_op jit(solution)/shard_map/ppermute | solution.py:38
  84.4 6.5 %collective-permute-start.4 = (bf16[256,1024]{1,0:T(8,128)(2,1)S(1)}, bf16[256,1024]{1,0:T(8,128)(2,1)S(1)}, u32[]{:S(2)}, u32[]{:S(2)}) collective-permute-start(bf16[256,1024]{1,0:T(8,128)(2,1)S(1)} %collective-permute-done.y), channel_id=1, source_target_pairs={{16,0},{0,16},{48,32},{32,48},{80,64},{64,80},{112,96},{96,112},{1... | collective-permute-start | bytes 1572872 | tf_op jit(solution)/shard_map/ppermute | solution.py:38
  104.4 15.1 %collective-permute-start.5 = (f32[2,256]{1,0:T(2,128)S(1)}, f32[2,256]{1,0:T(2,128)S(1)}, u32[]{:S(2)}, u32[]{:S(2)}) collective-permute-start(f32[2,256]{1,0:T(2,128)S(1)} %shard_map.45), channel_id=1, source_target_pairs={{0,0},{1,16},{2,32},{3,48},{4,64},{5,80},{6,96},{7,112},{8,128},{9... | collective-permute-start | bytes 6152 | tf_op jit(solution)/shard_map/ppermute | solution.py:249

commit v10 on v8

--- a/solution.py
+++ b/solution.py
@@ -31,6 +31,19 @@
 
 
 PLACES = list(itertools.product(*[range(d) for d in HOME]))
+
+
+def steps_to(place):
+    return place[0] + min(place[1], HOME[1] - place[1])
+
+
+N = 16
+OFFSETS = dict(
+    zip(
+        sorted(PLACES, key=lambda d: (steps_to(d), d)),
+        sorted(range(N), key=lambda o: (-min(o, N - o), o)),
+    )
+)
 
 
 def from_place(value, d):
@@ -118,7 +131,14 @@
     return slot // 4 % 16
 
 
-def last_kernel(seen, own, y, c, yc, x1, x2, out):
+def member_for(plane, z):
+    offset = (plane - z) % N
+    d = sum(jnp.where(offset == o, number(d), 0) for d, o in OFFSETS.items())
+    low, across, core = d // 8, d // 2 % 4, d % 2
+    return (z // 8 ^ low) * 8 + (z // 2 + across) % 4 * 2 + (z ^ core) % 2
+
+
+def last_kernel(z, seen, own, y, c, yc, x1, x2, out):
     held = [own[...], c[...], y[...], yc[...], x1[...]]
     far = x2[...]
     stats = [
@@ -142,7 +162,8 @@
     )
     n = out.shape[0] * GROUP // ROWS
     shape = (n, ROWS, slots)
-    chosen = jnp.where(place_of(iota(shape, 2)) == iota(shape, 0), values[None], 0.0)
+    member = member_for(place_of(iota((1, slots), 1)), z[0])
+    chosen = jnp.where(member[None] == iota(shape, 0), values[None], 0.0)
     shape = (slots, GROUP * CELLS)
     spread = (cell_of(iota(shape, 0)) == iota(shape, 1) % CELLS).astype(jnp.float32)
     wide = exact_dot(chosen.reshape(n * ROWS, slots), spread).reshape(-1, GROUP, GROUP * CELLS)
@@ -178,12 +199,12 @@
 
 def on_chip(kernel, out_shape, flops, *operands):
     vmem = pl.BlockSpec(memory_space=pltpu.VMEM)
-    single = isinstance(out_shape, jax.ShapeDtypeStruct)
+    smem = pl.BlockSpec(memory_space=pltpu.SMEM)
     return pl.pallas_call(
         kernel,
         out_shape=out_shape,
-        in_specs=[vmem] * len(operands),
-        out_specs=vmem if single else [vmem] * len(out_shape),
+        in_specs=[smem if x.size == 1 else vmem for x in operands],
+        out_specs=vmem,
         compiler_params=pltpu.CompilerParams(vmem_limit_bytes=16 * 2**20),
         cost_estimate=pl.CostEstimate(
             flops=flops, bytes_accessed=sum(x.size * 2 for x in operands), transcendentals=0
@@ -229,6 +250,7 @@
         last_kernel,
         jax.ShapeDtypeStruct((n * ROWS // GROUP, GROUP * CELLS), jnp.float32),
         8 * tile,
+        lax.axis_index("z").astype(jnp.int32).reshape(1),
         seen,
         own,
         y,
@@ -245,7 +267,10 @@
         0,
         message.reshape(places * ROWS // GROUP, GROUP * CELLS),
     )
-    pairs = [(u * n + z, z * n + u) for u in range(places) for z in range(n)]
+    pairs = []
+    for z in range(n):
+        for d, offset in OFFSETS.items():
+            pairs.append((number(plus(PLACES[z], d)) * n + z, z * n + (z + offset) % n))
     found = lax.ppermute(found, home + ("z",), pairs)
     return found[0].reshape(1, 1, slots), found[1].reshape(1, 1, slots)
 

time: 119 us -> 119 us (level)
  the two profiles are of different devices: /device:TPU:105 before, /device:TPU:104 now
where the time goes in v10:
time: 119 us; the launch traced here: 118 us
  blocking collectives  65.8 us (55%)
  waiting for transfers between devices  24.2 us (20%)
  starting transfers between devices  19.8 us (17%)
  Pallas kernels  5.16 us (4%)
  local copies, waits for them, and re-layouts  2.48 us (2%)
    all_to_all x1, blocking collectives, local(): lax.all_to_all(send.reshape(owners, per_owner, width), ('yh', 'z'), split...  54.8 us
    ppermute x5, starting transfers between devices, from_place(): return lax.ppermute(value, ('yl', 'x', 'core'), pairs)  17.8 us
    ppermute x1, waiting for transfers between devices, local(): found = lax.ppermute(found, home + ('z',), pairs)  12.3 us
    ppermute x5, waiting for transfers between devices, from_place(): return lax.ppermute(value, ('yl', 'x', 'core'), pairs)  11.9 us
    all_to_all x1, blocking collectives, local(): lax.all_to_all(message, home, split_axis=0, concat_axis=0, tiled=True)  11 us
    pallas_call x5, Pallas kernels, on_chip(): pl.pallas_call(kernel, out_shape=out_shape, in_specs=[smem if x.size == 1...  5.16 us
  transfers between devices with their start and end apart: 6, of which 3 were waited for; matrix products, arithmetic and copies ran while one was open for 0% of the time, Pallas kernels for 1%

profile of v10, /device:TPU:104, one launch (start us, length us, event | category | flops | bytes accessed | tf_op | source)
XLA Modules:
  0.0 118.1 jit_solution(6997372604970483958)
XLA Ops:
  0.6 0.0 copy-start.1
  0.6 0.6 copy-done.1
  1.3 0.0 copy-start
  1.3 0.9 copy-done
  2.2 0.5 shard_map.41
  2.7 0.2 reshape.24
  2.9 54.8 %all_to_all.10 = bf16[64,4,1024]{2,1,0:T(4,128)(2,1)S(1)} all-to-all(bf16[64,4,1024]{2,1,0:T(4,128)(2,1)S(1)} %reshape.24), channel_id=1, replica_groups=mesh['yh'=4,'yl'=2,'x'=4,'core'=2,'z'=16] {'yh','z'}, dimensions={0} | all-to-all | bytes 1048576 | tf_op jit(solution)/shard_map/all_to_all | solution.py:232
  57.7 0.1 reshape.25.own
  57.8 4.7 %collective-permute-start.1 = (bf16[256,1024]{1,0:T(8,128)(2,1)S(1)}, bf16[256,1024]{1,0:T(8,128)(2,1)S(1)}, u32[]{:S(2)}, u32[]{:S(2)}) collective-permute-start(bf16[256,1024]{1,0:T(8,128)(2,1)S(1)} %reshape.25.own), channel_id=1, source_target_pairs={{32,0},{48,16},{64,32},{80,48},{96,64},{112,80},{0,96},{16,112},{1... | collective-permute-start | bytes 1572872 | tf_op jit(solution)/shard_map/ppermute | solution.py:51
  62.5 3.3 %collective-permute-start = (bf16[256,1024]{1,0:T(8,128)(2,1)S(1)}, bf16[256,1024]{1,0:T(8,128)(2,1)S(1)}, u32[]{:S(2)}, u32[]{:S(2)}) collective-permute-start(bf16[256,1024]{1,0:T(8,128)(2,1)S(1)} %reshape.25.own), channel_id=1, source_target_pairs={{128,0},{144,16},{160,32},{176,48},{192,64},{208,80},{224,96},{240... | collective-permute-start | bytes 1572872 | tf_op jit(solution)/shard_map/ppermute | solution.py:51
  65.8 7.5 %collective-permute-done.1.x1 = bf16[256,1024]{1,0:T(8,128)(2,1)S(1)} collective-permute-done((bf16[256,1024]{1,0:T(8,128)(2,1)S(1)}, bf16[256,1024]{1,0:T(8,128)(2,1)S(1)}, u32[]{:S(2)}, u32[]{:S(2)}) %collective-permute-start.1) | collective-permute-done | bytes 524320 | tf_op jit(solution)/shard_map/ppermute | solution.py:51
  73.3 5.6 %collective-permute-start.2 = (bf16[256,1024]{1,0:T(8,128)(2,1)S(1)}, bf16[256,1024]{1,0:T(8,128)(2,1)S(1)}, u32[]{:S(2)}, u32[]{:S(2)}) collective-permute-start(bf16[256,1024]{1,0:T(8,128)(2,1)S(1)} %collective-permute-done.1.x1), channel_id=1, source_target_pairs={{32,0},{48,16},{64,32},{80,48},{96,64},{112,80},{0,96},{16,112},{1... | collective-permute-start | bytes 1572872 | tf_op jit(solution)/shard_map/ppermute | solution.py:51
  78.9 0.0 collective-permute-done.y
  78.9 1.1 shard_map.42.near
  80.0 1.9 %collective-permute-start.3 = (bf16[256,1024]{1,0:T(8,128)(2,1)S(1)}, bf16[256,1024]{1,0:T(8,128)(2,1)S(1)}, u32[]{:S(2)}, u32[]{:S(2)}) collective-permute-start(bf16[256,1024]{1,0:T(8,128)(2,1)S(1)} %reshape.25.own), channel_id=1, source_target_pairs={{16,0},{0,16},{48,32},{32,48},{80,64},{64,80},{112,96},{96,112},{1... | collective-permute-start | bytes 1572872 | tf_op jit(solution)/shard_map/ppermute | solution.py:51
  81.9 2.4 %collective-permute-start.4 = (bf16[256,1024]{1,0:T(8,128)(2,1)S(1)}, bf16[256,1024]{1,0:T(8,128)(2,1)S(1)}, u32[]{:S(2)}, u32[]{:S(2)}) collective-permute-start(bf16[256,1024]{1,0:T(8,128)(2,1)S(1)} %collective-permute-done.y), channel_id=1, source_target_pairs={{16,0},{0,16},{48,32},{32,48},{80,64},{64,80},{112,96},{96,112},{1... | collective-permute-start | bytes 1572872 | tf_op jit(solution)/shard_map/ppermute | solution.py:51
  84.3 4.4 %collective-permute-done.2.x2 = bf16[256,1024]{1,0:T(8,128)(2,1)S(1)} collective-permute-done((bf16[256,1024]{1,0:T(8,128)(2,1)S(1)}, bf16[256,1024]{1,0:T(8,128)(2,1)S(1)}, u32[]{:S(2)}, u32[]{:S(2)}) %collective-permute-start.2) | collective-permute-done | bytes 524320 | tf_op jit(solution)/shard_map/ppermute | solution.py:51
  88.7 0.5 shard_map.43.seen
  89.2 0.0 collective-permute-done.3.c
  89.2 0.0 collective-permute-done.4.yc
  89.2 2.8 %shard_map.44 = f32[32,128]{1,0:T(8,128)S(1)} custom-call(s32[1]{0:T(128)} %bitcast.z, f32[8,256]{1,0:T(8,128)S(1)} %shard_map.43.seen, bf16[256,1024]{1,0:T(8,128)(2,1)S(1)} %reshape.25.own, bf16[256,1024]{1,0:T(8,128)(2,1)S(1)} %collective-permute-done.y, bf16[256,1024]{1,0:T(8,128)(2,1)S(1)} %collective-permute-done.3.c, ...), custom_call_target="tpu_custom_call" | custom-call | flops 1073741824 | bytes 3149826 | tf_op jit(solution)/shard_map/pallas_call | solution.py:203
  92.0 11.0 %all_to_all.11 = f32[16,2,128]{2,1,0:T(2,128)S(1)} all-to-all(f32[16,2,128]{2,1,0:T(2,128)S(1)} %bitcast.9), channel_id=1, replica_groups=mesh['yh'=4,'yl'=2,'x'=4,'core'=2,'z'=16] {'yl','x','core'}, dimensions={0} | all-to-all | bytes 32768 | tf_op jit(solution)/shard_map/all_to_all | solution.py:263
  103.0 0.4 shard_map.45
  103.4 1.9 %collective-permute-start.5 = (f32[2,256]{1,0:T(2,128)S(1)}, f32[2,256]{1,0:T(2,128)S(1)}, u32[]{:S(2)}, u32[]{:S(2)}) collective-permute-start(f32[2,256]{1,0:T(2,128)S(1)} %shard_map.45), channel_id=1, source_target_pairs={{0,8},{16,7},{32,9},{48,6},{96,10},{112,5},{128,11},{144,4},{64,12... | collective-permute-start | bytes 6152 | tf_op jit(solution)/shard_map/ppermute | solution.py:274
  105.3 12.3 %collective-permute-done.5 = f32[2,256]{1,0:T(2,128)S(1)} collective-permute-done((f32[2,256]{1,0:T(2,128)S(1)}, f32[2,256]{1,0:T(2,128)S(1)}, u32[]{:S(2)}, u32[]{:S(2)}) %collective-permute-start.5) | collective-permute-done | bytes 2080 | tf_op jit(solution)/shard_map/ppermute | solution.py:274
  117.5 0.6 slice_bitcast_fusion
Async XLA Ops:
  0.6 0.7 copy-start.1
  1.3 0.9 copy-start
  57.8 15.5 %collective-permute-start.1 = (bf16[256,1024]{1,0:T(8,128)(2,1)S(1)}, bf16[256,1024]{1,0:T(8,128)(2,1)S(1)}, u32[]{:S(2)}, u32[]{:S(2)}) collective-permute-start(bf16[256,1024]{1,0:T(8,128)(2,1)S(1)} %reshape.25.own), channel_id=1, source_target_pairs={{32,0},{48,16},{64,32},{80,48},{96,64},{112,80},{0,96},{16,112},{1... | collective-permute-start | bytes 1572872 | tf_op jit(solution)/shard_map/ppermute | solution.py:51
  62.5 16.4 %collective-permute-start = (bf16[256,1024]{1,0:T(8,128)(2,1)S(1)}, bf16[256,1024]{1,0:T(8,128)(2,1)S(1)}, u32[]{:S(2)}, u32[]{:S(2)}) collective-permute-start(bf16[256,1024]{1,0:T(8,128)(2,1)S(1)} %reshape.25.own), channel_id=1, source_target_pairs={{128,0},{144,16},{160,32},{176,48},{192,64},{208,80},{224,96},{240... | collective-permute-start | bytes 1572872 | tf_op jit(solution)/shard_map/ppermute | solution.py:51
  73.3 15.5 %collective-permute-start.2 = (bf16[256,1024]{1,0:T(8,128)(2,1)S(1)}, bf16[256,1024]{1,0:T(8,128)(2,1)S(1)}, u32[]{:S(2)}, u32[]{:S(2)}) collective-permute-start(bf16[256,1024]{1,0:T(8,128)(2,1)S(1)} %collective-permute-done.1.x1), channel_id=1, source_target_pairs={{32,0},{48,16},{64,32},{80,48},{96,64},{112,80},{0,96},{16,112},{1... | collective-permute-start | bytes 1572872 | tf_op jit(solution)/shard_map/ppermute | solution.py:51
  80.0 9.2 %collective-permute-start.3 = (bf16[256,1024]{1,0:T(8,128)(2,1)S(1)}, bf16[256,1024]{1,0:T(8,128)(2,1)S(1)}, u32[]{:S(2)}, u32[]{:S(2)}) collective-permute-start(bf16[256,1024]{1,0:T(8,128)(2,1)S(1)} %reshape.25.own), channel_id=1, source_target_pairs={{16,0},{0,16},{48,32},{32,48},{80,64},{64,80},{112,96},{96,112},{1... | collective-permute-start | bytes 1572872 | tf_op jit(solution)/shard_map/ppermute | solution.py:51
  81.9 7.3 %collective-permute-start.4 = (bf16[256,1024]{1,0:T(8,128)(2,1)S(1)}, bf16[256,1024]{1,0:T(8,128)(2,1)S(1)}, u32[]{:S(2)}, u32[]{:S(2)}) collective-permute-start(bf16[256,1024]{1,0:T(8,128)(2,1)S(1)} %collective-permute-done.y), channel_id=1, source_target_pairs={{16,0},{0,16},{48,32},{32,48},{80,64},{64,80},{112,96},{96,112},{1... | collective-permute-start | bytes 1572872 | tf_op jit(solution)/shard_map/ppermute | solution.py:51
  103.4 14.2 %collective-permute-start.5 = (f32[2,256]{1,0:T(2,128)S(1)}, f32[2,256]{1,0:T(2,128)S(1)}, u32[]{:S(2)}, u32[]{:S(2)}) collective-permute-start(f32[2,256]{1,0:T(2,128)S(1)} %shard_map.45), channel_id=1, source_target_pairs={{0,8},{16,7},{32,9},{48,6},{96,10},{112,5},{128,11},{144,4},{64,12... | collective-permute-start | bytes 6152 | tf_op jit(solution)/shard_map/ppermute | solution.py:274

commit v11 on v8

--- a/solution.py
+++ b/solution.py
@@ -27,7 +27,7 @@
 
 
 def number(place):
-    return (place[0] * HOME[1] + place[1]) * HOME[2] + place[2]
+    return (place[1] * HOME[0] + place[0]) * HOME[2] + place[2]
 
 
 PLACES = list(itertools.product(*[range(d) for d in HOME]))
@@ -35,7 +35,7 @@
 
 def from_place(value, d):
     pairs = [(number(plus(u, d)), number(u)) for u in PLACES]
-    return lax.ppermute(value, ("yl", "x", "core"), pairs)
+    return lax.ppermute(value, ("yl", "xl", "core"), pairs)
 
 
 def dots(a, b):
@@ -62,7 +62,10 @@
     along = jnp.broadcast_to(assignment[...].astype(jnp.float32), (rows, rows))
     earlier = iota((rows, rows), 0) < iota((rows, rows), 1)
     rank = jnp.sum(jnp.where((along == along.T) & earlier, 1.0, 0.0), axis=0, keepdims=True)
-    slot = along[0:1] * (slots // 64) + rank
+    k = assignment[...]
+    low = (k // 8 % 4 * 2 + k // 2 % 2) * 2 + k % 2
+    home = (k // 32 * 2 + k // 4 % 2) * 16 + low
+    slot = home.astype(jnp.float32) * (slots // 64) + rank
     table = (slot == iota((slots, rows), 0).astype(jnp.float32)).astype(jnp.float32)
     placed = jnp.dot(table.astype(jnp.bfloat16), normed, preferred_element_type=jnp.float32)
     empty = jnp.sum(table, axis=1, keepdims=True) < 0.5
@@ -116,6 +119,14 @@
 
 def place_of(slot):
     return slot // 4 % 16
+
+
+def owner_cell(slot):
+    return (slot // 128 * 2 + slot // 16 % 2) * 4 + slot % 4
+
+
+def owner_place(slot):
+    return (slot // 32 % 4 * 2 + slot // 8 % 2) * 2 + slot // 4 % 2
 
 
 def last_kernel(seen, own, y, c, yc, x1, x2, out):
@@ -157,14 +168,14 @@
     keep = iota(shape, 2) // CELLS == iota(shape, 1)
     rows = jnp.where(keep, arrived[...][:, None, :], 0.0).reshape(places * ROWS, GROUP * CELLS)
     shape = (GROUP * CELLS, slots)
-    spread = (cell_of(iota(shape, 1)) == iota(shape, 0) % CELLS).astype(jnp.float32)
+    spread = (owner_cell(iota(shape, 1)) == iota(shape, 0) % CELLS).astype(jnp.float32)
     wide = exact_dot(rows, spread).reshape(places, ROWS, slots)
     u, v, to = (iota(wide.shape, axis) for axis in range(3))
     target = v % COUNT
     core = (u ^ jnp.where((target == 1) | (target == 3), 1, 0)) & 1
-    low = (u ^ jnp.where((target == 2) | (target == 3), 8, 0)) & 8
-    across = (u + jnp.where(target == 4, 2, 0)) & 6
-    here = (core + low + across == place_of(to)) | (v >= 2 * COUNT)
+    low = (u ^ jnp.where((target == 2) | (target == 3), 2, 0)) & 2
+    across = (u + jnp.where(target == 4, 4, 0)) & 12
+    here = (core + low + across == owner_place(to)) | (v >= 2 * COUNT)
     result = jnp.sum(jnp.where(here, wide, 0.0), axis=0)
     alive = result[0:1] > NEVER - 1.0
     best = jnp.max(result[0:COUNT], axis=0, keepdims=True)
@@ -192,8 +203,8 @@
 
 
 def local(embeddings, assignment):
-    home = ("yl", "x", "core")
-    far_y = lax.axis_size("yh")
+    home = ("yl", "xl", "core")
+    far_y = lax.axis_size("yh") * lax.axis_size("xh")
     n = lax.axis_size("z")
     places = len(PLACES)
     owners = far_y * places
@@ -210,7 +221,7 @@
     )
     own = lax.all_to_all(
         send.reshape(owners, per_owner, width),
-        ("yh", "z"),
+        ("yh", "xh", "z"),
         split_axis=0,
         concat_axis=0,
         tiled=True,
@@ -251,9 +262,9 @@
 
 
 def solution(mesh):
-    names = ("yh", "yl", "x", "core", "z")
+    names = ("yh", "yl", "xh", "xl", "core", "z")
     n = mesh.shape["split"]
-    parts = Mesh(mesh.devices.reshape(-1, *HOME, n), names)
+    parts = Mesh(mesh.devices.reshape(-1, 4, 2, 2, 2, n), names)
     in_specs = (P(names, None), P(names))
-    out_specs = (P(names[:4], "z", None), P(names[:4], "z", None))
+    out_specs = (P(names[:5], "z", None), P(names[:5], "z", None))
     return jax.shard_map(local, mesh=parts, in_specs=in_specs, out_specs=out_specs, check_vma=False)

time: 119 us -> 122 us (1.025)
  the two profiles are of different devices: /device:TPU:105 before, /device:TPU:117 now
where the time goes in v11:
time: 122 us
  blocking collectives  70.9 us (58%)
  waiting for transfers between devices  24.2 us (20%)
  starting transfers between devices  18.1 us (15%)
  Pallas kernels  5.19 us (4%)
  local copies, waits for them, and re-layouts  2.48 us (2%)
    all_to_all x1, blocking collectives, local(): lax.all_to_all(send.reshape(owners, per_owner, width), ('yh', 'xh', 'z'),...  56.9 us
    ppermute x5, starting transfers between devices, from_place(): return lax.ppermute(value, ('yl', 'xl', 'core'), pairs)  14.9 us
    all_to_all x1, blocking collectives, local(): lax.all_to_all(message, home, split_axis=0, concat_axis=0, tiled=True)  14 us
    ppermute x5, waiting for transfers between devices, from_place(): return lax.ppermute(value, ('yl', 'xl', 'core'), pairs)  12.6 us
    ppermute x1, waiting for transfers between devices, local(): found = lax.ppermute(found, home + ('z',), pairs)  11.6 us
    pallas_call x5, Pallas kernels, on_chip(): pl.pallas_call(kernel, out_shape=out_shape, in_specs=[vmem] * len(operand...  5.19 us
    ppermute x1, starting transfers between devices, local(): found = lax.ppermute(found, home + ('z',), pairs)  3.23 us
  transfers between devices with their start and end apart: 6, of which 3 were waited for; matrix products, arithmetic and copies ran while one was open for 0% of the time, Pallas kernels for 1%

profile of v11, /device:TPU:117, one launch (start us, length us, event | category | flops | bytes accessed | tf_op | source)
XLA Modules:
  0.0 121.6 jit_solution(479178584160707364)
XLA Ops:
  0.6 0.0 copy-start.1
  0.6 0.6 copy-done.1
  1.3 0.0 copy-start
  1.3 0.9 copy-done
  2.2 0.5 shard_map.41
  2.7 0.2 reshape.20
  2.9 56.9 %all_to_all.10 = bf16[64,4,1024]{2,1,0:T(4,128)(2,1)S(1)} all-to-all(bf16[64,4,1024]{2,1,0:T(4,128)(2,1)S(1)} %reshape.20), channel_id=1, replica_groups=mesh['yh'=2,'yl'=4,'xh'=2,'xl'=2,'core'=2,'z'=16] {'yh','xh','z'}, dimensions={0} | all-to-all | bytes 1048576 | tf_op jit(solution)/shard_map/all_to_all | solution.py:222
  59.8 0.1 reshape.21.own
  59.9 3.0 %collective-permute-start.1 = (bf16[256,1024]{1,0:T(8,128)(2,1)S(1)}, bf16[256,1024]{1,0:T(8,128)(2,1)S(1)}, u32[]{:S(2)}, u32[]{:S(2)}) collective-permute-start(bf16[256,1024]{1,0:T(8,128)(2,1)S(1)} %reshape.21.own), channel_id=1, source_target_pairs={{128,0},{144,16},{256,128},{272,144},{384,256},{400,272},{0,384},{... | collective-permute-start | bytes 1572872 | tf_op jit(solution)/shard_map/ppermute | solution.py:38
  62.9 2.8 %collective-permute-start = (bf16[256,1024]{1,0:T(8,128)(2,1)S(1)}, bf16[256,1024]{1,0:T(8,128)(2,1)S(1)}, u32[]{:S(2)}, u32[]{:S(2)}) collective-permute-start(bf16[256,1024]{1,0:T(8,128)(2,1)S(1)} %reshape.21.own), channel_id=1, source_target_pairs={{32,0},{48,16},{160,128},{176,144},{288,256},{304,272},{416,384},{... | collective-permute-start | bytes 1572872 | tf_op jit(solution)/shard_map/ppermute | solution.py:38
  65.8 8.4 %collective-permute-done.1.x1 = bf16[256,1024]{1,0:T(8,128)(2,1)S(1)} collective-permute-done((bf16[256,1024]{1,0:T(8,128)(2,1)S(1)}, bf16[256,1024]{1,0:T(8,128)(2,1)S(1)}, u32[]{:S(2)}, u32[]{:S(2)}) %collective-permute-start.1) | collective-permute-done | bytes 524320 | tf_op jit(solution)/shard_map/ppermute | solution.py:38
  74.2 3.0 %collective-permute-start.2 = (bf16[256,1024]{1,0:T(8,128)(2,1)S(1)}, bf16[256,1024]{1,0:T(8,128)(2,1)S(1)}, u32[]{:S(2)}, u32[]{:S(2)}) collective-permute-start(bf16[256,1024]{1,0:T(8,128)(2,1)S(1)} %collective-permute-done.1.x1), channel_id=1, source_target_pairs={{128,0},{144,16},{256,128},{272,144},{384,256},{400,272},{0,384},{... | collective-permute-start | bytes 1572872 | tf_op jit(solution)/shard_map/ppermute | solution.py:38
  77.2 0.0 collective-permute-done.y
  77.2 1.1 shard_map.42.near
  78.3 4.2 %collective-permute-start.3 = (bf16[256,1024]{1,0:T(8,128)(2,1)S(1)}, bf16[256,1024]{1,0:T(8,128)(2,1)S(1)}, u32[]{:S(2)}, u32[]{:S(2)}) collective-permute-start(bf16[256,1024]{1,0:T(8,128)(2,1)S(1)} %reshape.21.own), channel_id=1, source_target_pairs={{16,0},{0,16},{144,128},{128,144},{272,256},{256,272},{400,384},{3... | collective-permute-start | bytes 1572872 | tf_op jit(solution)/shard_map/ppermute | solution.py:38
  82.5 1.9 %collective-permute-start.4 = (bf16[256,1024]{1,0:T(8,128)(2,1)S(1)}, bf16[256,1024]{1,0:T(8,128)(2,1)S(1)}, u32[]{:S(2)}, u32[]{:S(2)}) collective-permute-start(bf16[256,1024]{1,0:T(8,128)(2,1)S(1)} %collective-permute-done.y), channel_id=1, source_target_pairs={{16,0},{0,16},{144,128},{128,144},{272,256},{256,272},{400,384},{3... | collective-permute-start | bytes 1572872 | tf_op jit(solution)/shard_map/ppermute | solution.py:38
  84.4 4.2 %collective-permute-done.2.x2 = bf16[256,1024]{1,0:T(8,128)(2,1)S(1)} collective-permute-done((bf16[256,1024]{1,0:T(8,128)(2,1)S(1)}, bf16[256,1024]{1,0:T(8,128)(2,1)S(1)}, u32[]{:S(2)}, u32[]{:S(2)}) %collective-permute-start.2) | collective-permute-done | bytes 524320 | tf_op jit(solution)/shard_map/ppermute | solution.py:38
  88.5 0.5 shard_map.43.seen
  89.0 0.0 collective-permute-done.3.c
  89.0 0.0 collective-permute-done.4.yc
  89.1 2.8 %shard_map.44 = f32[32,128]{1,0:T(8,128)S(1)} custom-call(f32[8,256]{1,0:T(8,128)S(1)} %shard_map.43.seen, bf16[256,1024]{1,0:T(8,128)(2,1)S(1)} %reshape.21.own, bf16[256,1024]{1,0:T(8,128)(2,1)S(1)} %collective-permute-done.y, bf16[256,1024]{1,0:T(8,128)(2,1)S(1)} %collective-permute-done.3.c, bf16[256,1024]{1,0:T(8,128)(2,1)S(1)} %collective-permute-done.4.yc, ...), custom_call_target="tpu_custom_call" | custom-call | flops 1073741824 | bytes 3149824 | tf_op jit(solution)/shard_map/pallas_call | solution.py:193
  91.8 14.0 %all_to_all.11 = f32[16,2,128]{2,1,0:T(2,128)S(1)} all-to-all(f32[16,2,128]{2,1,0:T(2,128)S(1)} %bitcast.8), channel_id=1, replica_groups=mesh['yh'=2,'yl'=4,'xh'=2,'xl'=2,'core'=2,'z'=16] {'yl','xl','core'}, dimensions={0} | all-to-all | bytes 32768 | tf_op jit(solution)/shard_map/all_to_all | solution.py:252
  105.8 0.4 shard_map.45
  106.2 3.2 %collective-permute-start.5 = (f32[2,256]{1,0:T(2,128)S(1)}, f32[2,256]{1,0:T(2,128)S(1)}, u32[]{:S(2)}, u32[]{:S(2)}) collective-permute-start(f32[2,256]{1,0:T(2,128)S(1)} %shard_map.45), channel_id=1, source_target_pairs={{0,0},{1,16},{2,32},{3,48},{4,128},{5,144},{6,160},{7,176},{8,256}... | collective-permute-start | bytes 6152 | tf_op jit(solution)/shard_map/ppermute | solution.py:260
  109.4 11.6 %collective-permute-done.5 = f32[2,256]{1,0:T(2,128)S(1)} collective-permute-done((f32[2,256]{1,0:T(2,128)S(1)}, f32[2,256]{1,0:T(2,128)S(1)}, u32[]{:S(2)}, u32[]{:S(2)}) %collective-permute-start.5) | collective-permute-done | bytes 2080 | tf_op jit(solution)/shard_map/ppermute | solution.py:260
  121.0 0.6 slice_bitcast_fusion
Async XLA Ops:
  0.6 0.7 copy-start.1
  1.3 0.9 copy-start
  59.9 14.2 %collective-permute-start.1 = (bf16[256,1024]{1,0:T(8,128)(2,1)S(1)}, bf16[256,1024]{1,0:T(8,128)(2,1)S(1)}, u32[]{:S(2)}, u32[]{:S(2)}) collective-permute-start(bf16[256,1024]{1,0:T(8,128)(2,1)S(1)} %reshape.21.own), channel_id=1, source_target_pairs={{128,0},{144,16},{256,128},{272,144},{384,256},{400,272},{0,384},{... | collective-permute-start | bytes 1572872 | tf_op jit(solution)/shard_map/ppermute | solution.py:38
  62.9 14.2 %collective-permute-start = (bf16[256,1024]{1,0:T(8,128)(2,1)S(1)}, bf16[256,1024]{1,0:T(8,128)(2,1)S(1)}, u32[]{:S(2)}, u32[]{:S(2)}) collective-permute-start(bf16[256,1024]{1,0:T(8,128)(2,1)S(1)} %reshape.21.own), channel_id=1, source_target_pairs={{32,0},{48,16},{160,128},{176,144},{288,256},{304,272},{416,384},{... | collective-permute-start | bytes 1572872 | tf_op jit(solution)/shard_map/ppermute | solution.py:38
  74.2 14.4 %collective-permute-start.2 = (bf16[256,1024]{1,0:T(8,128)(2,1)S(1)}, bf16[256,1024]{1,0:T(8,128)(2,1)S(1)}, u32[]{:S(2)}, u32[]{:S(2)}) collective-permute-start(bf16[256,1024]{1,0:T(8,128)(2,1)S(1)} %collective-permute-done.1.x1), channel_id=1, source_target_pairs={{128,0},{144,16},{256,128},{272,144},{384,256},{400,272},{0,384},{... | collective-permute-start | bytes 1572872 | tf_op jit(solution)/shard_map/ppermute | solution.py:38
  78.3 10.7 %collective-permute-start.3 = (bf16[256,1024]{1,0:T(8,128)(2,1)S(1)}, bf16[256,1024]{1,0:T(8,128)(2,1)S(1)}, u32[]{:S(2)}, u32[]{:S(2)}) collective-permute-start(bf16[256,1024]{1,0:T(8,128)(2,1)S(1)} %reshape.21.own), channel_id=1, source_target_pairs={{16,0},{0,16},{144,128},{128,144},{272,256},{256,272},{400,384},{3... | collective-permute-start | bytes 1572872 | tf_op jit(solution)/shard_map/ppermute | solution.py:38
  82.5 6.6 %collective-permute-start.4 = (bf16[256,1024]{1,0:T(8,128)(2,1)S(1)}, bf16[256,1024]{1,0:T(8,128)(2,1)S(1)}, u32[]{:S(2)}, u32[]{:S(2)}) collective-permute-start(bf16[256,1024]{1,0:T(8,128)(2,1)S(1)} %collective-permute-done.y), channel_id=1, source_target_pairs={{16,0},{0,16},{144,128},{128,144},{272,256},{256,272},{400,384},{3... | collective-permute-start | bytes 1572872 | tf_op jit(solution)/shard_map/ppermute | solution.py:38
  106.2 14.8 %collective-permute-start.5 = (f32[2,256]{1,0:T(2,128)S(1)}, f32[2,256]{1,0:T(2,128)S(1)}, u32[]{:S(2)}, u32[]{:S(2)}) collective-permute-start(f32[2,256]{1,0:T(2,128)S(1)} %shard_map.45), channel_id=1, source_target_pairs={{0,0},{1,16},{2,32},{3,48},{4,128},{5,144},{6,160},{7,176},{8,256}... | collective-permute-start | bytes 6152 | tf_op jit(solution)/shard_map/ppermute | solution.py:260

commit v12 on v8

--- a/solution.py
+++ b/solution.py
@@ -169,9 +169,9 @@
     alive = result[0:1] > NEVER - 1.0
     best = jnp.max(result[0:COUNT], axis=0, keepdims=True)
     nearest = jnp.where(alive, best, 0.0)
-    cosine = jnp.sum(result[COUNT : 2 * COUNT], axis=0, keepdims=True) * lax.rsqrt(
-        result[2 * COUNT : 2 * COUNT + 1] + EPSILON
-    )
+    square = jnp.maximum(result[2 * COUNT : 2 * COUNT + 1], 0.0)
+    total = jnp.sum(result[COUNT : 2 * COUNT], axis=0, keepdims=True)
+    cosine = total * lax.rsqrt(square + EPSILON)
     distance = jnp.where(alive, 1.0 - cosine, 0.0)
     out[...] = jnp.concatenate([nearest, distance])
 

time: 119 us -> 119 us (level)
  no operation moved by 1% of the time
where the time goes in v12:
time: 119 us; the launch traced here: 118 us
  blocking collectives  67.9 us (57%)
  starting transfers between devices  22.8 us (19%)
  waiting for transfers between devices  19.1 us (16%)
  Pallas kernels  5.18 us (4%)
  local copies, waits for them, and re-layouts  2.48 us (2%)
    all_to_all x1, blocking collectives, local(): lax.all_to_all(send.reshape(owners, per_owner, width), ('yh', 'z'), split...  54.4 us
    ppermute x5, starting transfers between devices, from_place(): return lax.ppermute(value, ('yl', 'x', 'core'), pairs)  18.7 us
    all_to_all x1, blocking collectives, local(): lax.all_to_all(message, home, split_axis=0, concat_axis=0, tiled=True)  13.5 us
    ppermute x1, waiting for transfers between devices, local(): found = lax.ppermute(found, home + ('z',), pairs)  9.91 us
    ppermute x5, waiting for transfers between devices, from_place(): return lax.ppermute(value, ('yl', 'x', 'core'), pairs)  9.18 us
    pallas_call x5, Pallas kernels, on_chip(): pl.pallas_call(kernel, out_shape=out_shape, in_specs=[vmem] * len(operand...  5.18 us
    ppermute x1, starting transfers between devices, local(): found = lax.ppermute(found, home + ('z',), pairs)  4.02 us
  transfers between devices with their start and end apart: 6, of which 3 were waited for; matrix products, arithmetic and copies ran while one was open for 0% of the time, Pallas kernels for 1%

profile of v12, /device:TPU:105, one launch (start us, length us, event | category | flops | bytes accessed | tf_op | source)
XLA Modules:
  0.0 118.1 jit_solution(830667890153152503)
XLA Ops:
  0.6 0.0 copy-start.1
  0.6 0.6 copy-done.1
  1.3 0.0 copy-start
  1.3 0.9 copy-done
  2.2 0.5 shard_map.41
  2.7 0.2 reshape.20
  2.9 54.4 %all_to_all.10 = bf16[64,4,1024]{2,1,0:T(4,128)(2,1)S(1)} all-to-all(bf16[64,4,1024]{2,1,0:T(4,128)(2,1)S(1)} %reshape.20), channel_id=1, replica_groups=mesh['yh'=4,'yl'=2,'x'=4,'core'=2,'z'=16] {'yh','z'}, dimensions={0} | all-to-all | bytes 1048576 | tf_op jit(solution)/shard_map/all_to_all | solution.py:211
  57.3 0.1 reshape.21.own
  57.4 4.4 %collective-permute-start.1 = (bf16[256,1024]{1,0:T(8,128)(2,1)S(1)}, bf16[256,1024]{1,0:T(8,128)(2,1)S(1)}, u32[]{:S(2)}, u32[]{:S(2)}) collective-permute-start(bf16[256,1024]{1,0:T(8,128)(2,1)S(1)} %reshape.21.own), channel_id=1, source_target_pairs={{32,0},{48,16},{64,32},{80,48},{96,64},{112,80},{0,96},{16,112},{1... | collective-permute-start | bytes 1572872 | tf_op jit(solution)/shard_map/ppermute | solution.py:38
  61.8 3.0 %collective-permute-start = (bf16[256,1024]{1,0:T(8,128)(2,1)S(1)}, bf16[256,1024]{1,0:T(8,128)(2,1)S(1)}, u32[]{:S(2)}, u32[]{:S(2)}) collective-permute-start(bf16[256,1024]{1,0:T(8,128)(2,1)S(1)} %reshape.21.own), channel_id=1, source_target_pairs={{128,0},{144,16},{160,32},{176,48},{192,64},{208,80},{224,96},{240... | collective-permute-start | bytes 1572872 | tf_op jit(solution)/shard_map/ppermute | solution.py:38
  64.8 7.2 %collective-permute-done.1.x1 = bf16[256,1024]{1,0:T(8,128)(2,1)S(1)} collective-permute-done((bf16[256,1024]{1,0:T(8,128)(2,1)S(1)}, bf16[256,1024]{1,0:T(8,128)(2,1)S(1)}, u32[]{:S(2)}, u32[]{:S(2)}) %collective-permute-start.1) | collective-permute-done | bytes 524320 | tf_op jit(solution)/shard_map/ppermute | solution.py:38
  72.0 5.3 %collective-permute-start.2 = (bf16[256,1024]{1,0:T(8,128)(2,1)S(1)}, bf16[256,1024]{1,0:T(8,128)(2,1)S(1)}, u32[]{:S(2)}, u32[]{:S(2)}) collective-permute-start(bf16[256,1024]{1,0:T(8,128)(2,1)S(1)} %collective-permute-done.1.x1), channel_id=1, source_target_pairs={{32,0},{48,16},{64,32},{80,48},{96,64},{112,80},{0,96},{16,112},{1... | collective-permute-start | bytes 1572872 | tf_op jit(solution)/shard_map/ppermute | solution.py:38
  77.3 0.0 collective-permute-done.y
  77.3 1.1 shard_map.42.near
  78.4 4.2 %collective-permute-start.3 = (bf16[256,1024]{1,0:T(8,128)(2,1)S(1)}, bf16[256,1024]{1,0:T(8,128)(2,1)S(1)}, u32[]{:S(2)}, u32[]{:S(2)}) collective-permute-start(bf16[256,1024]{1,0:T(8,128)(2,1)S(1)} %reshape.21.own), channel_id=1, source_target_pairs={{16,0},{0,16},{48,32},{32,48},{80,64},{64,80},{112,96},{96,112},{1... | collective-permute-start | bytes 1572872 | tf_op jit(solution)/shard_map/ppermute | solution.py:38
  82.6 1.9 %collective-permute-start.4 = (bf16[256,1024]{1,0:T(8,128)(2,1)S(1)}, bf16[256,1024]{1,0:T(8,128)(2,1)S(1)}, u32[]{:S(2)}, u32[]{:S(2)}) collective-permute-start(bf16[256,1024]{1,0:T(8,128)(2,1)S(1)} %collective-permute-done.y), channel_id=1, source_target_pairs={{16,0},{0,16},{48,32},{32,48},{80,64},{64,80},{112,96},{96,112},{1... | collective-permute-start | bytes 1572872 | tf_op jit(solution)/shard_map/ppermute | solution.py:38
  84.5 2.0 %collective-permute-done.2.x2 = bf16[256,1024]{1,0:T(8,128)(2,1)S(1)} collective-permute-done((bf16[256,1024]{1,0:T(8,128)(2,1)S(1)}, bf16[256,1024]{1,0:T(8,128)(2,1)S(1)}, u32[]{:S(2)}, u32[]{:S(2)}) %collective-permute-start.2) | collective-permute-done | bytes 524320 | tf_op jit(solution)/shard_map/ppermute | solution.py:38
  86.5 0.5 shard_map.43.seen
  87.0 0.0 collective-permute-done.3.c
  87.0 0.0 collective-permute-done.4.yc
  87.0 2.8 %shard_map.44 = f32[32,128]{1,0:T(8,128)S(1)} custom-call(f32[8,256]{1,0:T(8,128)S(1)} %shard_map.43.seen, bf16[256,1024]{1,0:T(8,128)(2,1)S(1)} %reshape.21.own, bf16[256,1024]{1,0:T(8,128)(2,1)S(1)} %collective-permute-done.y, bf16[256,1024]{1,0:T(8,128)(2,1)S(1)} %collective-permute-done.3.c, bf16[256,1024]{1,0:T(8,128)(2,1)S(1)} %collective-permute-done.4.yc, ...), custom_call_target="tpu_custom_call" | custom-call | flops 1073741824 | bytes 3149824 | tf_op jit(solution)/shard_map/pallas_call | solution.py:182
  89.8 13.5 %all_to_all.11 = f32[16,2,128]{2,1,0:T(2,128)S(1)} all-to-all(f32[16,2,128]{2,1,0:T(2,128)S(1)} %bitcast.8), channel_id=1, replica_groups=mesh['yh'=4,'yl'=2,'x'=4,'core'=2,'z'=16] {'yl','x','core'}, dimensions={0} | all-to-all | bytes 32768 | tf_op jit(solution)/shard_map/all_to_all | solution.py:241
  103.2 0.4 shard_map.45
  103.6 4.0 %collective-permute-start.5 = (f32[2,256]{1,0:T(2,128)S(1)}, f32[2,256]{1,0:T(2,128)S(1)}, u32[]{:S(2)}, u32[]{:S(2)}) collective-permute-start(f32[2,256]{1,0:T(2,128)S(1)} %shard_map.45), channel_id=1, source_target_pairs={{0,0},{1,16},{2,32},{3,48},{4,64},{5,80},{6,96},{7,112},{8,128},{9... | collective-permute-start | bytes 6152 | tf_op jit(solution)/shard_map/ppermute | solution.py:249
  107.7 9.9 %collective-permute-done.5 = f32[2,256]{1,0:T(2,128)S(1)} collective-permute-done((f32[2,256]{1,0:T(2,128)S(1)}, f32[2,256]{1,0:T(2,128)S(1)}, u32[]{:S(2)}, u32[]{:S(2)}) %collective-permute-start.5) | collective-permute-done | bytes 2080 | tf_op jit(solution)/shard_map/ppermute | solution.py:249
  117.6 0.6 slice_bitcast_fusion
Async XLA Ops:
  0.6 0.7 copy-start.1
  1.3 0.9 copy-start
  57.4 14.5 %collective-permute-start.1 = (bf16[256,1024]{1,0:T(8,128)(2,1)S(1)}, bf16[256,1024]{1,0:T(8,128)(2,1)S(1)}, u32[]{:S(2)}, u32[]{:S(2)}) collective-permute-start(bf16[256,1024]{1,0:T(8,128)(2,1)S(1)} %reshape.21.own), channel_id=1, source_target_pairs={{32,0},{48,16},{64,32},{80,48},{96,64},{112,80},{0,96},{16,112},{1... | collective-permute-start | bytes 1572872 | tf_op jit(solution)/shard_map/ppermute | solution.py:38
  61.8 15.5 %collective-permute-start = (bf16[256,1024]{1,0:T(8,128)(2,1)S(1)}, bf16[256,1024]{1,0:T(8,128)(2,1)S(1)}, u32[]{:S(2)}, u32[]{:S(2)}) collective-permute-start(bf16[256,1024]{1,0:T(8,128)(2,1)S(1)} %reshape.21.own), channel_id=1, source_target_pairs={{128,0},{144,16},{160,32},{176,48},{192,64},{208,80},{224,96},{240... | collective-permute-start | bytes 1572872 | tf_op jit(solution)/shard_map/ppermute | solution.py:38
  72.0 14.5 %collective-permute-start.2 = (bf16[256,1024]{1,0:T(8,128)(2,1)S(1)}, bf16[256,1024]{1,0:T(8,128)(2,1)S(1)}, u32[]{:S(2)}, u32[]{:S(2)}) collective-permute-start(bf16[256,1024]{1,0:T(8,128)(2,1)S(1)} %collective-permute-done.1.x1), channel_id=1, source_target_pairs={{32,0},{48,16},{64,32},{80,48},{96,64},{112,80},{0,96},{16,112},{1... | collective-permute-start | bytes 1572872 | tf_op jit(solution)/shard_map/ppermute | solution.py:38
  78.4 8.6 %collective-permute-start.3 = (bf16[256,1024]{1,0:T(8,128)(2,1)S(1)}, bf16[256,1024]{1,0:T(8,128)(2,1)S(1)}, u32[]{:S(2)}, u32[]{:S(2)}) collective-permute-start(bf16[256,1024]{1,0:T(8,128)(2,1)S(1)} %reshape.21.own), channel_id=1, source_target_pairs={{16,0},{0,16},{48,32},{32,48},{80,64},{64,80},{112,96},{96,112},{1... | collective-permute-start | bytes 1572872 | tf_op jit(solution)/shard_map/ppermute | solution.py:38
  82.6 4.4 %collective-permute-start.4 = (bf16[256,1024]{1,0:T(8,128)(2,1)S(1)}, bf16[256,1024]{1,0:T(8,128)(2,1)S(1)}, u32[]{:S(2)}, u32[]{:S(2)}) collective-permute-start(bf16[256,1024]{1,0:T(8,128)(2,1)S(1)} %collective-permute-done.y), channel_id=1, source_target_pairs={{16,0},{0,16},{48,32},{32,48},{80,64},{64,80},{112,96},{96,112},{1... | collective-permute-start | bytes 1572872 | tf_op jit(solution)/shard_map/ppermute | solution.py:38
  103.6 13.9 %collective-permute-start.5 = (f32[2,256]{1,0:T(2,128)S(1)}, f32[2,256]{1,0:T(2,128)S(1)}, u32[]{:S(2)}, u32[]{:S(2)}) collective-permute-start(f32[2,256]{1,0:T(2,128)S(1)} %shard_map.45), channel_id=1, source_target_pairs={{0,0},{1,16},{2,32},{3,48},{4,64},{5,80},{6,96},{7,112},{8,128},{9... | collective-permute-start | bytes 6152 | tf_op jit(solution)/shard_map/ppermute | solution.py:249

commit v13 on v12

--- a/solution.py
+++ b/solution.py
@@ -81,7 +81,11 @@
         best_and_sum(d, b),
         merge(best_and_sum(a, d), best_and_sum(b, d)),
     ]
-    out[...] = jnp.concatenate([b for b, _ in stats] + [t for _, t in stats] + [stats[0][0]] * 2)
+    first = (iota((8, own.shape[1]), 1) == 0).astype(jnp.bfloat16)
+    marks = [dots(first, x)[0:1] for x in (a, b, d)]
+    out[...] = jnp.concatenate(
+        [b for b, _ in stats] + [t for _, t in stats] + marks + marks[0:1] * (ROWS - 9)
+    )
 
 
 def far_kernel(near, own, y, x2, out):
@@ -89,7 +93,7 @@
     a, b = best_and_sum(far, own[...]), best_and_sum(far, y[...])
     best = jnp.maximum(near[0:2, :], jnp.concatenate([a[0], b[0]]))
     total = near[3:5, :] + jnp.concatenate([a[1], b[1]])
-    out[...] = jnp.concatenate([best, near[2:3, :], total, near[5:8, :]])
+    out[...] = jnp.concatenate([best, near[2:3, :], total, near[5:ROWS, :]])
 
 
 def iota(shape, axis):
@@ -134,7 +138,10 @@
     total = jnp.concatenate([t for _, t in stats])
     slots = best.shape[1]
     first = (iota((8, own.shape[1]), 1) == 0).astype(jnp.bfloat16)
-    alive = jnp.concatenate([dots(first, x)[0:1] for x in held]) < 1.5
+    marks = [dots(first, x)[0:1] for x in (held[1], held[3])]
+    alive = (
+        jnp.concatenate([seen[6:7, :], marks[0], seen[7:8, :], marks[1], seen[8:9, :]]) < 1.5
+    )
     square = jnp.sum(jnp.where(alive, total, 0.0))
     best = jnp.concatenate([jnp.where(alive[0:1], best[0:1], DEAD_BEST), best[1:]], axis=0)
     values = jnp.concatenate(
@@ -219,7 +226,7 @@
     x1 = from_place(own, X1)
     y = from_place(own, Y)
     x2 = from_place(x1, X1)
-    stats = jax.ShapeDtypeStruct((8, slots), jnp.float32)
+    stats = jax.ShapeDtypeStruct((ROWS, slots), jnp.float32)
     near = on_chip(near_kernel, stats, 6 * tile, own, y, x1)
     first, later, near = lax.optimization_barrier((own, y, near))
     c = from_place(first, C)

time: 119 us -> 118 us (level)
  transfers between devices with their start and end apart: 6 -> 6, of which waited for: 3 -> 3; matrix products, arithmetic and copies ran while one was open for 0% -> 0% of each run, Pallas kernels for 1% -> 2%
where the time goes in v13:
time: 118 us
  blocking collectives  67.9 us (58%)
  starting transfers between devices  22.8 us (19%)
  waiting for transfers between devices  18.8 us (16%)
  Pallas kernels  5.05 us (4%)
  local copies, waits for them, and re-layouts  2.48 us (2%)
    all_to_all x1, blocking collectives, local(): lax.all_to_all(send.reshape(owners, per_owner, width), ('yh', 'z'), split...  54.4 us
    ppermute x5, starting transfers between devices, from_place(): return lax.ppermute(value, ('yl', 'x', 'core'), pairs)  18.8 us
    all_to_all x1, blocking collectives, local(): lax.all_to_all(message, home, split_axis=0, concat_axis=0, tiled=True)  13.5 us
    ppermute x1, waiting for transfers between devices, local(): found = lax.ppermute(found, home + ('z',), pairs)  9.91 us
    ppermute x5, waiting for transfers between devices, from_place(): return lax.ppermute(value, ('yl', 'x', 'core'), pairs)  8.87 us
    pallas_call x5, Pallas kernels, on_chip(): pl.pallas_call(kernel, out_shape=out_shape, in_specs=[vmem] * len(operand...  5.05 us
    ppermute x1, starting transfers between devices, local(): found = lax.ppermute(found, home + ('z',), pairs)  4.02 us
  transfers between devices with their start and end apart: 6, of which 3 were waited for; matrix products, arithmetic and copies ran while one was open for 0% of the time, Pallas kernels for 2%

profile of v13, /device:TPU:105, one launch (start us, length us, event | category | flops | bytes accessed | tf_op | source)
XLA Modules:
  0.0 117.7 jit_solution(2011718975682304715)
XLA Ops:
  0.6 0.0 copy-start.1
  0.6 0.6 copy-done.1
  1.3 0.0 copy-start
  1.3 0.9 copy-done
  2.2 0.5 shard_map.41
  2.7 0.2 reshape.20
  2.9 54.4 %all_to_all.10 = bf16[64,4,1024]{2,1,0:T(4,128)(2,1)S(1)} all-to-all(bf16[64,4,1024]{2,1,0:T(4,128)(2,1)S(1)} %reshape.20), channel_id=1, replica_groups=mesh['yh'=4,'yl'=2,'x'=4,'core'=2,'z'=16] {'yh','z'}, dimensions={0} | all-to-all | bytes 1048576 | tf_op jit(solution)/shard_map/all_to_all | solution.py:218
  57.3 0.1 reshape.21.own
  57.4 4.4 %collective-permute-start.1 = (bf16[256,1024]{1,0:T(8,128)(2,1)S(1)}, bf16[256,1024]{1,0:T(8,128)(2,1)S(1)}, u32[]{:S(2)}, u32[]{:S(2)}) collective-permute-start(bf16[256,1024]{1,0:T(8,128)(2,1)S(1)} %reshape.21.own), channel_id=1, source_target_pairs={{32,0},{48,16},{64,32},{80,48},{96,64},{112,80},{0,96},{16,112},{1... | collective-permute-start | bytes 1572872 | tf_op jit(solution)/shard_map/ppermute | solution.py:38
  61.8 3.0 %collective-permute-start = (bf16[256,1024]{1,0:T(8,128)(2,1)S(1)}, bf16[256,1024]{1,0:T(8,128)(2,1)S(1)}, u32[]{:S(2)}, u32[]{:S(2)}) collective-permute-start(bf16[256,1024]{1,0:T(8,128)(2,1)S(1)} %reshape.21.own), channel_id=1, source_target_pairs={{128,0},{144,16},{160,32},{176,48},{192,64},{208,80},{224,96},{240... | collective-permute-start | bytes 1572872 | tf_op jit(solution)/shard_map/ppermute | solution.py:38
  64.8 7.2 %collective-permute-done.1.x1 = bf16[256,1024]{1,0:T(8,128)(2,1)S(1)} collective-permute-done((bf16[256,1024]{1,0:T(8,128)(2,1)S(1)}, bf16[256,1024]{1,0:T(8,128)(2,1)S(1)}, u32[]{:S(2)}, u32[]{:S(2)}) %collective-permute-start.1) | collective-permute-done | bytes 524320 | tf_op jit(solution)/shard_map/ppermute | solution.py:38
  72.0 5.3 %collective-permute-start.2 = (bf16[256,1024]{1,0:T(8,128)(2,1)S(1)}, bf16[256,1024]{1,0:T(8,128)(2,1)S(1)}, u32[]{:S(2)}, u32[]{:S(2)}) collective-permute-start(bf16[256,1024]{1,0:T(8,128)(2,1)S(1)} %collective-permute-done.1.x1), channel_id=1, source_target_pairs={{32,0},{48,16},{64,32},{80,48},{96,64},{112,80},{0,96},{16,112},{1... | collective-permute-start | bytes 1572872 | tf_op jit(solution)/shard_map/ppermute | solution.py:38
  77.3 0.0 collective-permute-done.y
  77.3 1.4 %shard_map.42.near = f32[16,256]{1,0:T(8,128)S(1)} custom-call(bf16[256,1024]{1,0:T(8,128)(2,1)S(1)} %reshape.21.own, bf16[256,1024]{1,0:T(8,128)(2,1)S(1)} %collective-permute-done.y, bf16[256,1024]{1,0:T(8,128)(2,1)S(1)} %collective-permute-done.1.x1), custom_call_target="tpu_custom_call" | custom-call | flops 805306368 | bytes 1572864 | tf_op jit(solution)/shard_map/pallas_call | solution.py:189
  78.7 4.2 %collective-permute-start.3 = (bf16[256,1024]{1,0:T(8,128)(2,1)S(1)}, bf16[256,1024]{1,0:T(8,128)(2,1)S(1)}, u32[]{:S(2)}, u32[]{:S(2)}) collective-permute-start(bf16[256,1024]{1,0:T(8,128)(2,1)S(1)} %reshape.21.own), channel_id=1, source_target_pairs={{16,0},{0,16},{48,32},{32,48},{80,64},{64,80},{112,96},{96,112},{1... | collective-permute-start | bytes 1572872 | tf_op jit(solution)/shard_map/ppermute | solution.py:38
  82.9 1.9 %collective-permute-start.4 = (bf16[256,1024]{1,0:T(8,128)(2,1)S(1)}, bf16[256,1024]{1,0:T(8,128)(2,1)S(1)}, u32[]{:S(2)}, u32[]{:S(2)}) collective-permute-start(bf16[256,1024]{1,0:T(8,128)(2,1)S(1)} %collective-permute-done.y), channel_id=1, source_target_pairs={{16,0},{0,16},{48,32},{32,48},{80,64},{64,80},{112,96},{96,112},{1... | collective-permute-start | bytes 1572872 | tf_op jit(solution)/shard_map/ppermute | solution.py:38
  84.8 1.7 %collective-permute-done.2.x2 = bf16[256,1024]{1,0:T(8,128)(2,1)S(1)} collective-permute-done((bf16[256,1024]{1,0:T(8,128)(2,1)S(1)}, bf16[256,1024]{1,0:T(8,128)(2,1)S(1)}, u32[]{:S(2)}, u32[]{:S(2)}) %collective-permute-start.2) | collective-permute-done | bytes 524320 | tf_op jit(solution)/shard_map/ppermute | solution.py:38
  86.5 0.5 shard_map.43.seen
  87.0 0.0 collective-permute-done.3.c
  87.0 0.0 collective-permute-done.4.yc
  87.0 2.3 %shard_map.44 = f32[32,128]{1,0:T(8,128)S(1)} custom-call(f32[16,256]{1,0:T(8,128)S(1)} %shard_map.43.seen, bf16[256,1024]{1,0:T(8,128)(2,1)S(1)} %reshape.21.own, bf16[256,1024]{1,0:T(8,128)(2,1)S(1)} %collective-permute-done.y, bf16[256,1024]{1,0:T(8,128)(2,1)S(1)} %collective-permute-done.3.c, bf16[256,1024]{1,0:T(8,128)(2,1)S(1)} %collective-permute-done.4.yc, ...), custom_call_target="tpu_custom_call" | custom-call | flops 1073741824 | bytes 3153920 | tf_op jit(solution)/shard_map/pallas_call | solution.py:189
  89.4 13.5 %all_to_all.11 = f32[16,2,128]{2,1,0:T(2,128)S(1)} all-to-all(f32[16,2,128]{2,1,0:T(2,128)S(1)} %bitcast.8), channel_id=1, replica_groups=mesh['yh'=4,'yl'=2,'x'=4,'core'=2,'z'=16] {'yl','x','core'}, dimensions={0} | all-to-all | bytes 32768 | tf_op jit(solution)/shard_map/all_to_all | solution.py:248
  102.8 0.4 shard_map.45
  103.2 4.0 %collective-permute-start.5 = (f32[2,256]{1,0:T(2,128)S(1)}, f32[2,256]{1,0:T(2,128)S(1)}, u32[]{:S(2)}, u32[]{:S(2)}) collective-permute-start(f32[2,256]{1,0:T(2,128)S(1)} %shard_map.45), channel_id=1, source_target_pairs={{0,0},{1,16},{2,32},{3,48},{4,64},{5,80},{6,96},{7,112},{8,128},{9... | collective-permute-start | bytes 6152 | tf_op jit(solution)/shard_map/ppermute | solution.py:256
  107.2 9.9 %collective-permute-done.5 = f32[2,256]{1,0:T(2,128)S(1)} collective-permute-done((f32[2,256]{1,0:T(2,128)S(1)}, f32[2,256]{1,0:T(2,128)S(1)}, u32[]{:S(2)}, u32[]{:S(2)}) %collective-permute-start.5) | collective-permute-done | bytes 2080 | tf_op jit(solution)/shard_map/ppermute | solution.py:256
  117.2 0.6 slice_bitcast_fusion
Async XLA Ops:
  0.6 0.7 copy-start.1
  1.3 0.9 copy-start
  57.4 14.5 %collective-permute-start.1 = (bf16[256,1024]{1,0:T(8,128)(2,1)S(1)}, bf16[256,1024]{1,0:T(8,128)(2,1)S(1)}, u32[]{:S(2)}, u32[]{:S(2)}) collective-permute-start(bf16[256,1024]{1,0:T(8,128)(2,1)S(1)} %reshape.21.own), channel_id=1, source_target_pairs={{32,0},{48,16},{64,32},{80,48},{96,64},{112,80},{0,96},{16,112},{1... | collective-permute-start | bytes 1572872 | tf_op jit(solution)/shard_map/ppermute | solution.py:38
  61.8 15.5 %collective-permute-start = (bf16[256,1024]{1,0:T(8,128)(2,1)S(1)}, bf16[256,1024]{1,0:T(8,128)(2,1)S(1)}, u32[]{:S(2)}, u32[]{:S(2)}) collective-permute-start(bf16[256,1024]{1,0:T(8,128)(2,1)S(1)} %reshape.21.own), channel_id=1, source_target_pairs={{128,0},{144,16},{160,32},{176,48},{192,64},{208,80},{224,96},{240... | collective-permute-start | bytes 1572872 | tf_op jit(solution)/shard_map/ppermute | solution.py:38
  72.0 14.5 %collective-permute-start.2 = (bf16[256,1024]{1,0:T(8,128)(2,1)S(1)}, bf16[256,1024]{1,0:T(8,128)(2,1)S(1)}, u32[]{:S(2)}, u32[]{:S(2)}) collective-permute-start(bf16[256,1024]{1,0:T(8,128)(2,1)S(1)} %collective-permute-done.1.x1), channel_id=1, source_target_pairs={{32,0},{48,16},{64,32},{80,48},{96,64},{112,80},{0,96},{16,112},{1... | collective-permute-start | bytes 1572872 | tf_op jit(solution)/shard_map/ppermute | solution.py:38
  78.7 8.3 %collective-permute-start.3 = (bf16[256,1024]{1,0:T(8,128)(2,1)S(1)}, bf16[256,1024]{1,0:T(8,128)(2,1)S(1)}, u32[]{:S(2)}, u32[]{:S(2)}) collective-permute-start(bf16[256,1024]{1,0:T(8,128)(2,1)S(1)} %reshape.21.own), channel_id=1, source_target_pairs={{16,0},{0,16},{48,32},{32,48},{80,64},{64,80},{112,96},{96,112},{1... | collective-permute-start | bytes 1572872 | tf_op jit(solution)/shard_map/ppermute | solution.py:38
  82.9 4.1 %collective-permute-start.4 = (bf16[256,1024]{1,0:T(8,128)(2,1)S(1)}, bf16[256,1024]{1,0:T(8,128)(2,1)S(1)}, u32[]{:S(2)}, u32[]{:S(2)}) collective-permute-start(bf16[256,1024]{1,0:T(8,128)(2,1)S(1)} %collective-permute-done.y), channel_id=1, source_target_pairs={{16,0},{0,16},{48,32},{32,48},{80,64},{64,80},{112,96},{96,112},{1... | collective-permute-start | bytes 1572872 | tf_op jit(solution)/shard_map/ppermute | solution.py:38
  103.2 13.9 %collective-permute-start.5 = (f32[2,256]{1,0:T(2,128)S(1)}, f32[2,256]{1,0:T(2,128)S(1)}, u32[]{:S(2)}, u32[]{:S(2)}) collective-permute-start(f32[2,256]{1,0:T(2,128)S(1)} %shard_map.45), channel_id=1, source_target_pairs={{0,0},{1,16},{2,32},{3,48},{4,64},{5,80},{6,96},{7,112},{8,128},{9... | collective-permute-start | bytes 6152 | tf_op jit(solution)/shard_map/ppermute | solution.py:256

commit v14 on v13

--- a/solution.py
+++ b/solution.py
@@ -17,7 +17,7 @@
 ROWS = 16
 HOME = (2, 4, 2)
 OWN, C, Y, YC = (0, 0, 0), (0, 0, 1), (1, 0, 0), (1, 0, 1)
-X1, X2 = (0, 1, 0), (0, 2, 0)
+X1, X2 = (0, 3, 0), (0, 2, 0)
 TARGETS = (OWN, C, Y, YC, X1)
 COUNT = len(TARGETS)
 
@@ -170,7 +170,7 @@
     target = v % COUNT
     core = (u ^ jnp.where((target == 1) | (target == 3), 1, 0)) & 1
     low = (u ^ jnp.where((target == 2) | (target == 3), 8, 0)) & 8
-    across = (u + jnp.where(target == 4, 2, 0)) & 6
+    across = (u + jnp.where(target == 4, 6, 0)) & 6
     here = (core + low + across == place_of(to)) | (v >= 2 * COUNT)
     result = jnp.sum(jnp.where(here, wide, 0.0), axis=0)
     alive = result[0:1] > NEVER - 1.0

time: 118 us -> 117 us (level)
  waiting for transfers between devices: 18.8 us -> 24.4 us
  starting transfers between devices: 22.8 us -> 18.1 us
  blocking collectives: 67.9 us -> 65.4 us
    ppermute x5, waiting for transfers between devices: 8.87 us -> 14.5 us  [from_place(): return lax.ppermute(value, ('yl', 'x', 'core'), pairs)]
    ppermute x5, starting transfers between devices: 18.8 us -> 14.1 us  [from_place(): return lax.ppermute(value, ('yl', 'x', 'core'), pairs)]
    all_to_all x1, blocking collectives: 13.5 us -> 11 us  [local(): lax.all_to_all(message, home, split_axis=0, concat_axis=0, tiled=True)]
where the time goes in v14:
time: 117 us; the launch traced here: 116 us
  blocking collectives  65.4 us (56%)
  waiting for transfers between devices  24.4 us (21%)
  starting transfers between devices  18.1 us (15%)
  Pallas kernels  5.05 us (4%)
  local copies, waits for them, and re-layouts  2.48 us (2%)
    all_to_all x1, blocking collectives, local(): lax.all_to_all(send.reshape(owners, per_owner, width), ('yh', 'z'), split...  54.4 us
    ppermute x5, waiting for transfers between devices, from_place(): return lax.ppermute(value, ('yl', 'x', 'core'), pairs)  14.5 us
    ppermute x5, starting transfers between devices, from_place(): return lax.ppermute(value, ('yl', 'x', 'core'), pairs)  14.1 us
    all_to_all x1, blocking collectives, local(): lax.all_to_all(message, home, split_axis=0, concat_axis=0, tiled=True)  11 us
    ppermute x1, waiting for transfers between devices, local(): found = lax.ppermute(found, home + ('z',), pairs)  9.89 us
    pallas_call x5, Pallas kernels, on_chip(): pl.pallas_call(kernel, out_shape=out_shape, in_specs=[vmem] * len(operand...  5.05 us
    ppermute x1, starting transfers between devices, local(): found = lax.ppermute(found, home + ('z',), pairs)  4.05 us
  transfers between devices with their start and end apart: 6, of which 3 were waited for; matrix products, arithmetic and copies ran while one was open for 0% of the time, Pallas kernels for 2%

profile of v14, /device:TPU:105, one launch (start us, length us, event | category | flops | bytes accessed | tf_op | source)
XLA Modules:
  0.0 116.2 jit_solution(8310968085840140516)
XLA Ops:
  0.6 0.0 copy-start.1
  0.6 0.6 copy-done.1
  1.3 0.0 copy-start
  1.3 0.9 copy-done
  2.2 0.5 shard_map.41
  2.7 0.2 reshape.20
  2.9 54.4 %all_to_all.10 = bf16[64,4,1024]{2,1,0:T(4,128)(2,1)S(1)} all-to-all(bf16[64,4,1024]{2,1,0:T(4,128)(2,1)S(1)} %reshape.20), channel_id=1, replica_groups=mesh['yh'=4,'yl'=2,'x'=4,'core'=2,'z'=16] {'yh','z'}, dimensions={0} | all-to-all | bytes 1048576 | tf_op jit(solution)/shard_map/all_to_all | solution.py:218
  57.3 0.1 reshape.21.own
  57.4 3.1 %collective-permute-start.1 = (bf16[256,1024]{1,0:T(8,128)(2,1)S(1)}, bf16[256,1024]{1,0:T(8,128)(2,1)S(1)}, u32[]{:S(2)}, u32[]{:S(2)}) collective-permute-start(bf16[256,1024]{1,0:T(8,128)(2,1)S(1)} %reshape.21.own), channel_id=1, source_target_pairs={{96,0},{112,16},{0,32},{16,48},{32,64},{48,80},{64,96},{80,112},{2... | collective-permute-start | bytes 1572872 | tf_op jit(solution)/shard_map/ppermute | solution.py:38
  60.6 3.0 %collective-permute-start = (bf16[256,1024]{1,0:T(8,128)(2,1)S(1)}, bf16[256,1024]{1,0:T(8,128)(2,1)S(1)}, u32[]{:S(2)}, u32[]{:S(2)}) collective-permute-start(bf16[256,1024]{1,0:T(8,128)(2,1)S(1)} %reshape.21.own), channel_id=1, source_target_pairs={{128,0},{144,16},{160,32},{176,48},{192,64},{208,80},{224,96},{240... | collective-permute-start | bytes 1572872 | tf_op jit(solution)/shard_map/ppermute | solution.py:38
  63.6 9.3 %collective-permute-done.1.x1 = bf16[256,1024]{1,0:T(8,128)(2,1)S(1)} collective-permute-done((bf16[256,1024]{1,0:T(8,128)(2,1)S(1)}, bf16[256,1024]{1,0:T(8,128)(2,1)S(1)}, u32[]{:S(2)}, u32[]{:S(2)}) %collective-permute-start.1) | collective-permute-done | bytes 524320 | tf_op jit(solution)/shard_map/ppermute | solution.py:38
  72.9 1.9 %collective-permute-start.2 = (bf16[256,1024]{1,0:T(8,128)(2,1)S(1)}, bf16[256,1024]{1,0:T(8,128)(2,1)S(1)}, u32[]{:S(2)}, u32[]{:S(2)}) collective-permute-start(bf16[256,1024]{1,0:T(8,128)(2,1)S(1)} %collective-permute-done.1.x1), channel_id=1, source_target_pairs={{96,0},{112,16},{0,32},{16,48},{32,64},{48,80},{64,96},{80,112},{2... | collective-permute-start | bytes 1572872 | tf_op jit(solution)/shard_map/ppermute | solution.py:38
  74.8 0.0 collective-permute-done.y
  74.8 1.4 %shard_map.42.near = f32[16,256]{1,0:T(8,128)S(1)} custom-call(bf16[256,1024]{1,0:T(8,128)(2,1)S(1)} %reshape.21.own, bf16[256,1024]{1,0:T(8,128)(2,1)S(1)} %collective-permute-done.y, bf16[256,1024]{1,0:T(8,128)(2,1)S(1)} %collective-permute-done.1.x1), custom_call_target="tpu_custom_call" | custom-call | flops 805306368 | bytes 1572864 | tf_op jit(solution)/shard_map/pallas_call | solution.py:189
  76.2 4.2 %collective-permute-start.3 = (bf16[256,1024]{1,0:T(8,128)(2,1)S(1)}, bf16[256,1024]{1,0:T(8,128)(2,1)S(1)}, u32[]{:S(2)}, u32[]{:S(2)}) collective-permute-start(bf16[256,1024]{1,0:T(8,128)(2,1)S(1)} %reshape.21.own), channel_id=1, source_target_pairs={{16,0},{0,16},{48,32},{32,48},{80,64},{64,80},{112,96},{96,112},{1... | collective-permute-start | bytes 1572872 | tf_op jit(solution)/shard_map/ppermute | solution.py:38
  80.4 1.9 %collective-permute-start.4 = (bf16[256,1024]{1,0:T(8,128)(2,1)S(1)}, bf16[256,1024]{1,0:T(8,128)(2,1)S(1)}, u32[]{:S(2)}, u32[]{:S(2)}) collective-permute-start(bf16[256,1024]{1,0:T(8,128)(2,1)S(1)} %collective-permute-done.y), channel_id=1, source_target_pairs={{16,0},{0,16},{48,32},{32,48},{80,64},{64,80},{112,96},{96,112},{1... | collective-permute-start | bytes 1572872 | tf_op jit(solution)/shard_map/ppermute | solution.py:38
  82.3 5.1 %collective-permute-done.2.x2 = bf16[256,1024]{1,0:T(8,128)(2,1)S(1)} collective-permute-done((bf16[256,1024]{1,0:T(8,128)(2,1)S(1)}, bf16[256,1024]{1,0:T(8,128)(2,1)S(1)}, u32[]{:S(2)}, u32[]{:S(2)}) %collective-permute-start.2) | collective-permute-done | bytes 524320 | tf_op jit(solution)/shard_map/ppermute | solution.py:38
  87.4 0.5 shard_map.43.seen
  87.9 0.0 collective-permute-done.3.c
  87.9 0.0 collective-permute-done.4.yc
  87.9 2.3 %shard_map.44 = f32[32,128]{1,0:T(8,128)S(1)} custom-call(f32[16,256]{1,0:T(8,128)S(1)} %shard_map.43.seen, bf16[256,1024]{1,0:T(8,128)(2,1)S(1)} %reshape.21.own, bf16[256,1024]{1,0:T(8,128)(2,1)S(1)} %collective-permute-done.y, bf16[256,1024]{1,0:T(8,128)(2,1)S(1)} %collective-permute-done.3.c, bf16[256,1024]{1,0:T(8,128)(2,1)S(1)} %collective-permute-done.4.yc, ...), custom_call_target="tpu_custom_call" | custom-call | flops 1073741824 | bytes 3153920 | tf_op jit(solution)/shard_map/pallas_call | solution.py:189
  90.3 11.0 %all_to_all.11 = f32[16,2,128]{2,1,0:T(2,128)S(1)} all-to-all(f32[16,2,128]{2,1,0:T(2,128)S(1)} %bitcast.8), channel_id=1, replica_groups=mesh['yh'=4,'yl'=2,'x'=4,'core'=2,'z'=16] {'yl','x','core'}, dimensions={0} | all-to-all | bytes 32768 | tf_op jit(solution)/shard_map/all_to_all | solution.py:248
  101.3 0.4 shard_map.45
  101.7 4.0 %collective-permute-start.5 = (f32[2,256]{1,0:T(2,128)S(1)}, f32[2,256]{1,0:T(2,128)S(1)}, u32[]{:S(2)}, u32[]{:S(2)}) collective-permute-start(f32[2,256]{1,0:T(2,128)S(1)} %shard_map.45), channel_id=1, source_target_pairs={{0,0},{1,16},{2,32},{3,48},{4,64},{5,80},{6,96},{7,112},{8,128},{9... | collective-permute-start | bytes 6152 | tf_op jit(solution)/shard_map/ppermute | solution.py:256
  105.8 9.9 %collective-permute-done.5 = f32[2,256]{1,0:T(2,128)S(1)} collective-permute-done((f32[2,256]{1,0:T(2,128)S(1)}, f32[2,256]{1,0:T(2,128)S(1)}, u32[]{:S(2)}, u32[]{:S(2)}) %collective-permute-start.5) | collective-permute-done | bytes 2080 | tf_op jit(solution)/shard_map/ppermute | solution.py:256
  115.7 0.6 slice_bitcast_fusion
Async XLA Ops:
  0.6 0.7 copy-start.1
  1.3 0.9 copy-start
  57.4 15.5 %collective-permute-start.1 = (bf16[256,1024]{1,0:T(8,128)(2,1)S(1)}, bf16[256,1024]{1,0:T(8,128)(2,1)S(1)}, u32[]{:S(2)}, u32[]{:S(2)}) collective-permute-start(bf16[256,1024]{1,0:T(8,128)(2,1)S(1)} %reshape.21.own), channel_id=1, source_target_pairs={{96,0},{112,16},{0,32},{16,48},{32,64},{48,80},{64,96},{80,112},{2... | collective-permute-start | bytes 1572872 | tf_op jit(solution)/shard_map/ppermute | solution.py:38
  60.6 14.3 %collective-permute-start = (bf16[256,1024]{1,0:T(8,128)(2,1)S(1)}, bf16[256,1024]{1,0:T(8,128)(2,1)S(1)}, u32[]{:S(2)}, u32[]{:S(2)}) collective-permute-start(bf16[256,1024]{1,0:T(8,128)(2,1)S(1)} %reshape.21.own), channel_id=1, source_target_pairs={{128,0},{144,16},{160,32},{176,48},{192,64},{208,80},{224,96},{240... | collective-permute-start | bytes 1572872 | tf_op jit(solution)/shard_map/ppermute | solution.py:38
  72.9 14.5 %collective-permute-start.2 = (bf16[256,1024]{1,0:T(8,128)(2,1)S(1)}, bf16[256,1024]{1,0:T(8,128)(2,1)S(1)}, u32[]{:S(2)}, u32[]{:S(2)}) collective-permute-start(bf16[256,1024]{1,0:T(8,128)(2,1)S(1)} %collective-permute-done.1.x1), channel_id=1, source_target_pairs={{96,0},{112,16},{0,32},{16,48},{32,64},{48,80},{64,96},{80,112},{2... | collective-permute-start | bytes 1572872 | tf_op jit(solution)/shard_map/ppermute | solution.py:38
  76.2 11.7 %collective-permute-start.3 = (bf16[256,1024]{1,0:T(8,128)(2,1)S(1)}, bf16[256,1024]{1,0:T(8,128)(2,1)S(1)}, u32[]{:S(2)}, u32[]{:S(2)}) collective-permute-start(bf16[256,1024]{1,0:T(8,128)(2,1)S(1)} %reshape.21.own), channel_id=1, source_target_pairs={{16,0},{0,16},{48,32},{32,48},{80,64},{64,80},{112,96},{96,112},{1... | collective-permute-start | bytes 1572872 | tf_op jit(solution)/shard_map/ppermute | solution.py:38
  80.4 7.6 %collective-permute-start.4 = (bf16[256,1024]{1,0:T(8,128)(2,1)S(1)}, bf16[256,1024]{1,0:T(8,128)(2,1)S(1)}, u32[]{:S(2)}, u32[]{:S(2)}) collective-permute-start(bf16[256,1024]{1,0:T(8,128)(2,1)S(1)} %collective-permute-done.y), channel_id=1, source_target_pairs={{16,0},{0,16},{48,32},{32,48},{80,64},{64,80},{112,96},{96,112},{1... | collective-permute-start | bytes 1572872 | tf_op jit(solution)/shard_map/ppermute | solution.py:38
  101.7 13.9 %collective-permute-start.5 = (f32[2,256]{1,0:T(2,128)S(1)}, f32[2,256]{1,0:T(2,128)S(1)}, u32[]{:S(2)}, u32[]{:S(2)}) collective-permute-start(f32[2,256]{1,0:T(2,128)S(1)} %shard_map.45), channel_id=1, source_target_pairs={{0,0},{1,16},{2,32},{3,48},{4,64},{5,80},{6,96},{7,112},{8,128},{9... | collective-permute-start | bytes 6152 | tf_op jit(solution)/shard_map/ppermute | solution.py:256
